TPU v7x, 128 devices: a whole 4x4x4 slice. The times are simulated.
128 devices in a mesh: group: 16 (over y, x), depth: 2 (over core), mp: 4 (over z).
Axes of the slice: x: 4, y: 4, z: 4, core: 2. Of those that a mesh axis runs over, the one named last changes fastest.
Arguments:
- states: bfloat16 [256, 4096], P(('group', 'depth', 'mp')), may hold values from -6 to 6
- queries: bfloat16 [256, 32, 128], P('group', 'mp'), may hold values from -6 to 6
- new_keys: bfloat16 [256, 8, 128], P('group', 'mp'), may hold values from -18 to 18
- new_values: bfloat16 [256, 8, 128], P('group', 'mp'), may hold values from -24 to 24
- text_keys: bfloat16 [256, 8, 512, 128], P('group', 'mp', 'depth'), may hold values from -6 to 6
- text_values: bfloat16 [256, 8, 512, 128], P('group', 'mp', 'depth'), may hold values from -24 to 24
- text_length: int32 [256], P('group'), may hold values from 2 to 512
- image_keys: bfloat16 [128, 8, 576, 128], P('group', 'mp'), may hold values from -6 to 6
- image_values: bfloat16 [128, 8, 576, 128], P('group', 'mp'), may hold values from -24 to 24
- image_slot: int32 [128], replicated, may hold values from 0 to 127, as said below
- block_list: int32 [16, 32], replicated, may hold values from 0 to 127, as said below
- block_count: int32 [16], replicated, may hold values from 16 to 32, as said below
- image_first: int32 [256], P('group'), may hold values from 0 to 31, as said below
- image_count: int32 [256], P('group'), may hold values from 1 to 2
- out_weight: bfloat16 [4096, 4096], P('mp'), may hold values from -0.09375 to 0.09375
- norm_gain: float32 [4096], replicated, may hold values from 0.5 to 1.5
- gate_weight: bfloat16 [4096, 14336], P(None, ('group', 'mp')), may hold values from -0.09375 to 0.09375
- up_weight: bfloat16 [4096, 14336], P(None, ('group', 'mp')), may hold values from -0.09375 to 0.09375
- down_weight: bfloat16 [14336, 4096], P(('group', 'mp')), may hold values from -0.046875 to 0.046875
Outputs:
- attention: bfloat16 [256, 32, 128], P(('group', 'depth'), 'mp')
- layer_out: bfloat16 [256, 4096], P(('group', 'depth', 'mp'))
Inputs may be any that keep to these rules, and one draw needn't show every extreme that they name: `image_slot`: a permutation. The owner group of hash k is image_slot[k] // 8. `block_list`: the hashes of one group's list are distinct. Among one group's places with the same remainder modulo 2, at most 1 belongs to any one owner group; some group has block_count 32, and there every owner group holds exactly 1 place of every remainder. `block_count`: the sum of image_count over the group's requests. The requests of a group take consecutive list places in request order: image_first is the sum of image_count over the group's earlier requests.
All inputs are finite; a program needn't handle non-finite values.
Results may differ from a plain program's by a relative error of at most 0.012.
Values may be sent and summed in bfloat16 or wider, within the bound.
No kernel may reach another device: no remote copies, remote signals or barrier semaphores. Data moves between devices by JAX's collectives and lax.ppermute only.
A program may use at most 128 MiB of HBM per device.

v0:
```python
import math

import jax
import jax.numpy as jnp
from jax import lax
from jax.sharding import PartitionSpec as P

LOG_TWO = math.log(2.0)
MASKED_SCORE = -1e30
NORM_EPSILON = 1e-05


def sent_together(arrays, axis, split_dim, concat_dim, along):
    widths = [math.prod(a.shape[along:]) for a in arrays]
    both = jnp.concatenate(
        [a.reshape(*a.shape[:along], w) for a, w in zip(arrays, widths)], axis=along
    )
    whole = lax.all_to_all(both, axis, split_axis=split_dim, concat_axis=concat_dim, tiled=True)
    blocks = jnp.split(whole, [sum(widths[:k]) for k in range(1, len(widths))], axis=along)
    return tuple(
        (b.reshape(*whole.shape[:along], *a.shape[along:]) for a, b in zip(arrays, blocks))
    )


def copy_for_each(x, axis):
    peers = lax.axis_size(axis)
    return lax.all_to_all(jnp.broadcast_to(x[None], (peers, *x.shape)), axis, 0, 0, tiled=True)


def gathered_once(x, axis):
    leaves = jax.tree.leaves(x)
    sequence = sorted(range(len(leaves)), key=lambda k: -leaves[k].size)
    width = (1, *leaves[sequence[0]].shape)[-1]
    lines = [
        jnp.pad(leaves[k].reshape(-1), (0, -leaves[k].size % width)).reshape(-1, width)
        for k in sequence
    ]
    both, at, found = (copy_for_each(jnp.concatenate(lines), axis), 0, {})
    for k, line in zip(sequence, lines):
        slab = both[:, at : at + len(line)].reshape(len(both), -1)
        found[k] = slab[:, : leaves[k].size].reshape(-1, *leaves[k].shape)
        at += len(line)
    numbers = iter(range(len(leaves)))
    return jax.tree.map(lambda _: found[next(numbers)], x)


def joined_by_halves(pieces, combine):
    while len(jax.tree.leaves(pieces)[0]) > 1:
        pieces = jax.vmap(combine)(
            *(jax.tree.map(lambda part: part[side::2], pieces) for side in (0, 1))
        )
    return jax.tree.map(lambda part: part[0], pieces)


def merged(x, axis, combine):
    pieces = gathered_once(x, axis)
    return joined_by_halves(pieces, combine)


def split_up(x, dim, peers):
    shape = x.shape
    blocks = x.reshape(*shape[:dim], peers, shape[dim] // peers, *shape[dim + 1 :])
    return jnp.moveaxis(blocks, dim, 0)


def summed_on_arrival(x, axis, dim):
    peers = lax.axis_size(axis)
    blocks = lax.all_to_all(split_up(x, dim, peers), axis, 0, 0, tiled=True)
    return jnp.sum(blocks, axis=0)


def joined_along(blocks, dim):
    blocks = jnp.moveaxis(blocks, 0, dim)
    shape = blocks.shape
    return blocks.reshape(*shape[:dim], shape[dim] * shape[dim + 1], *shape[dim + 2 :])


def gathered_copies(x, axis, dim):
    return joined_along(copy_for_each(x, axis), dim)


def sent_and_summed(x, axis, dim):
    blocks = split_up(x, dim, lax.axis_size(axis))
    arrived = lax.all_to_all(blocks, axis, split_axis=0, concat_axis=0, tiled=True)
    return arrived.astype(jnp.float32).sum(axis=0)


def combine(first_part, second_part):
    highest = jnp.maximum(first_part[0], second_part[0])
    first_factor = jnp.exp2(first_part[0] - highest)
    second_factor = jnp.exp2(second_part[0] - highest)
    totals = first_part[1] * first_factor + second_part[1] * second_factor
    weighted = first_part[2] * first_factor[..., None] + second_part[2] * second_factor[..., None]
    return (highest, totals, weighted)


def on_device(
    states,
    queries,
    new_keys,
    new_values,
    text_keys,
    text_values,
    text_length,
    image_keys,
    image_values,
    image_slot,
    block_list,
    block_count,
    image_first,
    image_count,
    out_weight,
    norm_gain,
    gate_weight,
    up_weight,
    down_weight,
):
    groups = lax.axis_size("group")
    depths = lax.axis_size("depth")
    group_index = lax.axis_index("group")
    depth_index = lax.axis_index("depth")
    requests, head_count, head_width = queries.shape
    kv_heads = text_keys.shape[1]
    text_span = text_keys.shape[2]
    stored = image_keys.shape[0]
    listed = block_list.shape[1]
    copies = listed // (depths * groups)
    group_share = head_count // kv_heads
    scaling = 1.0 / math.sqrt(head_width)
    grouped = queries.reshape(requests, kv_heads, group_share, head_width)
    text_scores = (
        jnp.einsum("rhgd,rhpd->rhgp", grouped, text_keys, preferred_element_type=jnp.float32)
        * scaling
    )
    new_scores = (
        jnp.einsum("rhgd,rhd->rhg", grouped, new_keys, preferred_element_type=jnp.float32) * scaling
    )
    positions = depth_index * text_span + jnp.arange(text_span, dtype=jnp.int32)
    text_allowed = (positions[None, :] < text_length[:, None])[:, None, None, :]
    new_allowed = depth_index == 0
    highest = jnp.maximum(
        jnp.max(jnp.where(text_allowed, text_scores, MASKED_SCORE), axis=-1),
        jnp.where(new_allowed, new_scores, MASKED_SCORE),
    )
    levels = jnp.floor(highest / LOG_TWO)
    text_weights = jnp.where(
        text_allowed, jnp.exp(text_scores - LOG_TWO * levels[..., None]), 0.0
    ).astype(jnp.bfloat16)
    new_weights = (
        jnp.where(new_allowed, jnp.exp(new_scores - LOG_TWO * levels), 0.0)
        .astype(jnp.bfloat16)
        .astype(jnp.float32)
    )
    totals = jnp.sum(text_weights, axis=-1, dtype=jnp.float32) + new_weights
    weighted = jnp.einsum(
        "rhgp,rhpd->rhgd", text_weights, text_values, preferred_element_type=jnp.float32
    )
    weighted = weighted + new_weights[..., None] * new_values.astype(jnp.float32)[:, :, None, :]
    local_part = (levels, totals, weighted)

    def owner_table(list_row, list_count, depth):
        indices = jnp.arange(groups * copies, dtype=jnp.int32)
        places = indices * depths + depth
        hashes = jnp.take(list_row, places, axis=0)
        slot_rows = jnp.take(image_slot, hashes, axis=0)
        owners = slot_rows // stored
        within = slot_rows % stored
        active = places < list_count
        member = (
            (owners[:, None] == jnp.arange(groups, dtype=jnp.int32)[None, :]) & active[:, None]
        ).astype(jnp.int32)
        earlier = jnp.cumsum(member, axis=0) - member
        ranked = jnp.sum(earlier * member, axis=1)
        picked = member[:, :, None] * (
            ranked[:, None, None] == jnp.arange(copies, dtype=jnp.int32)[None, None, :]
        ).astype(jnp.int32)
        chosen = jnp.sum(picked * within[:, None, None], axis=0)
        placed = jnp.sum(picked * places[:, None, None], axis=0)
        present = jnp.sum(picked, axis=0) > 0
        return (chosen, placed, present)

    own_row = lax.dynamic_index_in_dim(block_list, group_index, 0, keepdims=False)
    own_count = lax.dynamic_index_in_dim(block_count, group_index, 0, keepdims=False)
    own_chosen, own_placed, own_present = owner_table(own_row, own_count, depth_index)
    finish = image_first + image_count
    in_use = (
        own_present[None]
        & (own_placed[None] >= image_first[:, None, None])
        & (own_placed[None] < finish[:, None, None])
    )
    in_use_int = in_use.astype(jnp.int32)
    every_chosen, every_placed, every_present = jax.vmap(
        lambda list_row, list_count: owner_table(list_row, list_count, depth_index)
    )(block_list, block_count)
    serve_slots = lax.dynamic_index_in_dim(every_chosen, group_index, 1, keepdims=False)
    serve_present = lax.dynamic_index_in_dim(every_present, group_index, 1, keepdims=False)
    request_numbers = jnp.arange(requests, dtype=jnp.int32)[:, None, None]
    reader = jnp.sum(in_use_int * request_numbers, axis=0)
    routed = jnp.take(queries, reader.reshape(-1), axis=0).reshape(
        groups, copies, head_count, head_width
    )
    arrived = lax.all_to_all(routed, "group", split_axis=0, concat_axis=0, tiled=True)
    arrived = arrived.reshape(groups, copies, kv_heads, group_share, head_width)
    owned_keys = jnp.take(image_keys, serve_slots, axis=0)
    owned_values = jnp.take(image_values, serve_slots, axis=0)
    owned_scores = (
        jnp.einsum("schgd,schpd->schgp", arrived, owned_keys, preferred_element_type=jnp.float32)
        * scaling
    )
    owned_allowed = serve_present[:, :, None, None, None]
    owned_high = jnp.max(jnp.where(owned_allowed, owned_scores, MASKED_SCORE), axis=-1)
    owned_levels = jnp.floor(owned_high / LOG_TWO)
    owned_weights = jnp.where(
        owned_allowed, jnp.exp(owned_scores - LOG_TWO * owned_levels[..., None]), 0.0
    ).astype(jnp.bfloat16)
    owned_totals = jnp.sum(owned_weights, axis=-1, dtype=jnp.float32)
    owned_weighted = jnp.einsum(
        "schgp,schpd->schgd", owned_weights, owned_values, preferred_element_type=jnp.float32
    )
    back_levels, back_totals, back_weighted = sent_together(
        (owned_levels, owned_totals, owned_weighted), "group", 0, 0, 4
    )
    use_float = in_use.astype(jnp.float32)
    image_levels = jnp.max(
        jnp.where(in_use[:, :, :, None, None], back_levels[None], MASKED_SCORE), axis=(1, 2)
    )
    image_totals = jnp.einsum(
        "roc,ochg->rhg", use_float, back_totals, precision=lax.Precision.HIGHEST
    )
    image_weighted = jnp.einsum(
        "roc,ochgd->rhgd", use_float, back_weighted, precision=lax.Precision.HIGHEST
    )
    image_part = (image_levels, image_totals, image_weighted)
    partial_value = combine(local_part, image_part)
    merged_levels, merged_totals, merged_weighted = merged(partial_value, "depth", combine)
    attention_all = (
        (merged_weighted / merged_totals[..., None])
        .reshape(requests, head_count, head_width)
        .astype(jnp.bfloat16)
    )
    per_depth = requests // depths
    attention_half = lax.dynamic_slice_in_dim(attention_all, depth_index * per_depth, per_depth, 0)
    flattened = attention_half.reshape(per_depth, head_count * head_width)
    picked_rows = flattened
    projected = summed_on_arrival(
        jnp.dot(picked_rows, out_weight, preferred_element_type=jnp.float32), "mp", 0
    )
    residual = states.astype(jnp.float32) + projected
    spread = jnp.mean(residual * residual, axis=-1, keepdims=True)
    normed = (residual * lax.rsqrt(spread + NORM_EPSILON) * norm_gain).astype(jnp.bfloat16)
    piece = gathered_copies(normed, ("group", "mp"), 0)
    gate_term = jnp.dot(piece, gate_weight, preferred_element_type=jnp.float32)
    up_term = jnp.dot(piece, up_weight, preferred_element_type=jnp.float32)
    hidden = (jax.nn.silu(gate_term) * up_term).astype(jnp.bfloat16)
    picked_rows = hidden
    summed = sent_and_summed(
        jnp.dot(picked_rows, down_weight, preferred_element_type=jnp.float32).astype(jnp.bfloat16),
        ("group", "mp"),
        0,
    )
    return (attention_half, (residual + summed).astype(jnp.bfloat16))


def solution(mesh):
    placed = (
        P(("group", "depth", "mp"), None),
        P("group", "mp", None),
        P("group", "mp", None),
        P("group", "mp", None),
        P("group", "mp", "depth", None),
        P("group", "mp", "depth", None),
        P("group"),
        P("group", "mp", None, None),
        P("group", "mp", None, None),
        P(),
        P(),
        P(),
        P("group"),
        P("group"),
        P("mp", None),
        P(),
        P(None, ("group", "mp")),
        P(None, ("group", "mp")),
        P(("group", "mp"), None),
    )
    return jax.shard_map(
        on_device,
        mesh=mesh,
        in_specs=placed,
        out_specs=(P(("group", "depth"), "mp", None), P(("group", "depth", "mp"), None)),
        check_vma=False,
    )
```

profile of v0, /device:TPU:0, one launch (start us, length us, event | category | flops | bytes accessed | tf_op | source)
XLA Modules:
  0.0 140.3 jit_solution(7783734147494570234)
XLA Ops:
  0.7 0.8 fusion.65
  1.6 0.7 gather_fusion
  2.2 1.3 gather_fusion.1
  3.6 1.2 dynamic_slice.16
  4.8 0.7 broadcast_compare_fusion.2
  5.6 0.2 select_reduce_fusion.6
  5.9 0.7 add.231
  6.6 0.7 select_reduce_fusion.5
  7.4 1.3 gather_fusion.4
  8.7 0.7 bitcast_select_fusion.4
  9.4 7.1 %all-to-all-start = ((bf16[16,1,8,128]{3,2,1,0:T(8,128)(2,1)}), bf16[16,1,8,128]{3,2,1,0:T(8,128)(2,1)S(1)}, u32[]{:S(2)}, u32[]{:S(2)}) async-start(bf16[16,1,8,128]{3,2,1,0:T(8,128)(2,1)} %bitcast_select_fusion.4), calls=%async_computation | async-start | bytes 65536 | tf_op jit(solution)/shard_map/all_to_all | solution.py:202
  16.5 0.8 copy.112
  17.3 0.7 broadcast_compare_fusion.1
  18.0 0.7 compare_and_fusion.1
  18.7 0.6 gather_fusion.2
  19.5 1.9 %gather_fusion.3 = s32[256]{0:T(256)S(1)} fusion(s32[128]{0:T(128)S(1)} %copy-done.1, s32[1024]{0:T(1024)S(1)} %pad_clamp_fusion.2), kind=kCustom, calls=%fused_computation.5 | custom fusion | bytes 3072 | tf_op jit(solution)/shard_map/vmap(jit(_take))/gather | solution.py:165
  21.7 0.6 fusion.76
  22.3 0.2 select_reduce_fusion.1
  22.5 0.2 fusion.52
  22.8 2.3 %select_reduce_fusion.2 = (f32[16,2,4]{2,1,0:T(2,128)S(1)}, f32[16,2,4,256]{3,2,1,0:T(4,128)S(1)}) fusion(pred[16,256]{1,0:T(8,128)(4,1)S(1)} %broadcast_compare_fusion, bf16[16,2,4,128]{3,2,1,0:T(4,128)(2,1)S(1)} %bitcast.120, bf16[16,2,256,128]{3,2,1,0:T(8,128)(2,1)} %param.25), kind=kOutput, calls=%fused_computation.43 | convolution fusion | flops 8486784 | bytes 2265600 | tf_op jit(solution)/shard_map/rhgd,rhpd->rhgp/dot_general | solution.py:132
  25.6 3.3 %gather_fusion.5 = bf16[16,2,576,128]{3,2,1,0:T(8,128)(2,1)} fusion(bf16[8,2,576,128]{3,2,1,0:T(8,128)(2,1)S(1)} %copy-done, s32[1024]{0:T(1024)S(1)} %pad_clamp_fusion), kind=kCustom, calls=%fused_computation.clone | custom fusion | bytes 9437248 | tf_op jit(solution)/shard_map/jit(_take)/gather | solution.py:204
  28.8 5.0 %gather_fusion.6 = bf16[16,2,576,128]{3,2,1,0:T(8,128)(2,1)} fusion(bf16[8,2,576,128]{3,2,1,0:T(8,128)(2,1)} %param.29, s32[1024]{0:T(1024)S(1)} %pad_clamp_fusion), kind=kCustom, calls=%fused_computation.1.clone | custom fusion | bytes 9437248 | tf_op jit(solution)/shard_map/jit(_take)/gather | solution.py:205
  33.9 0.2 fusion.48
  34.1 0.2 and_reduce_fusion
  34.3 4.0 %select_reduce_fusion = (f32[16,2,4]{2,1,0:T(2,128)S(1)}, f32[16,2,4,576]{3,2,1,0:T(4,128)S(1)}) fusion(pred[16]{0:T(512)(128)(4,1)S(1)} %fusion.48, bf16[16,2,4,128]{3,2,1,0:T(4,128)(2,1)S(1)} %bitcast.124, bf16[16,2,576,128]{3,2,1,0:T(8,128)(2,1)} %gather_fusion.5, pred[16]{0:T(512)(128)(4,1)S(1)} %and_reduce_fusion), kind=kOutput, calls=%fused_computation.33 | convolution fusion | flops 21454720 | bytes 5046816 | tf_op jit(solution)/shard_map/schgd,schpd->schgp/dot_general | solution.py:207
  38.5 0.4 convert_reduce_fusion.1
  38.8 0.3 copy.121
  39.3 3.2 %fusion.15 = f32[16,1,2,4,128]{4,3,2,0,1:T(4,128)S(1)} fusion(bf16[16,2,4,576]{3,2,1,0:T(4,128)(2,1)S(1)} %get-tuple-element.22, bf16[16,2,576,128]{3,2,1,0:T(8,128)(2,1)} %gather_fusion.6, pred[16]{0:T(512)(128)(4,1)S(1)} %and_reduce_fusion), kind=kOutput, calls=%fused_computation.27 | convolution fusion | flops 21233664 | bytes 4931600 | tf_op jit(solution)/shard_map/schgp,schpd->schgd/dot_general | solution.py:217
  42.5 0.9 maximum_bitcast_fusion
  43.4 7.2 %all-to-all-start.1 = ((f32[16,1,2,4,130]{4,3,2,1,0:T(4,128)}), f32[16,1,2,4,130]{4,3,2,1,0:T(4,128)S(1)}, u32[]{:S(2)}, u32[]{:S(2)}) async-start(f32[16,1,2,4,130]{4,3,2,1,0:T(4,128)} %maximum_bitcast_fusion), calls=%async_computation.1 | async-start | bytes 262144 | tf_op jit(solution)/shard_map/all_to_all | solution.py:18
  50.6 0.2 convert_reduce_fusion.2
  50.9 7.7 %all-to-all-done.1 = f32[16,1,2,4,130]{4,3,2,1,0:T(4,128)S(1)} async-done(((f32[16,1,2,4,130]{4,3,2,1,0:T(4,128)}), f32[16,1,2,4,130]{4,3,2,1,0:T(4,128)S(1)}, u32[]{:S(2)}, u32[]{:S(2)}) %all-to-all-start.1) | async-done | bytes 66592 | tf_op jit(solution)/shard_map/all_to_all | solution.py:18
  58.9 0.2 fusion.50
  59.6 0.2 fusion.30
  60.3 2.0 %fusion.19 = f32[16,2,4,128]{3,2,1,0:T(4,128)S(1)} fusion(bf16[16,2,256,128]{3,2,1,0:T(8,128)(2,1)} %param.26, f32[16,2,4,128]{3,0,2,1:T(8,128)S(1)} %fusion.30, f32[16,2,4]{2,1,0:T(2,128)S(1)} %copy.126, f32[16,2,4]{2,1,0:T(2,128)S(1)} %copy.124, f32[16,2,128]{2,1,0:T(2,128)S(1)} %convert_element_type.75, f32[16,2,4]{2,1,0:T(2,128)S(1)} %copy.111, ...), kind=kOutput, calls=%fused_computation.30 | convolution fusion | flops 8568832 | bytes 2381824 | tf_op jit(solution)/shard_map/rhgp,rhpd->rhgd/dot_general | solution.py:155
  62.4 3.8 %all_to_all.30 = f32[2,130,128]{2,1,0:T(8,128)S(1)} all-to-all(f32[2,130,128]{2,1,0:T(8,128)S(1)} %broadcast_in_dim.174), channel_id=1, replica_groups=mesh['group'=16,'depth'=2,'mp'=4] {'depth'}, dimensions={0} | all-to-all | bytes 266240 | tf_op jit(solution)/shard_map/all_to_all | solution.py:27
  66.8 0.6 copy-done.5
  67.4 4.7 %fusion = f32[4,2,4096]{2,1,0:T(2,128)S(1)} fusion(bf16[4,2,1024]{2,1,0:T(2,128)(2,1)S(1)} %dot_general.45, bf16[1024,4096]{1,0:T(8,128)(2,1)} %param.35), kind=kOutput, calls=%fused_computation.7 | convolution fusion | flops 67108864 | bytes 8536064 | tf_op jit(solution)/shard_map/dot_general | solution.py:246
  72.1 11.1 %all_to_all.31 = f32[4,2,4096]{2,1,0:T(2,128)S(1)} all-to-all(f32[4,2,4096]{2,1,0:T(2,128)S(1)} %fusion), channel_id=1, replica_groups=mesh['group'=16,'depth'=2,'mp'=4] {'mp'}, dimensions={0} | all-to-all | bytes 262144 | tf_op jit(solution)/shard_map/all_to_all | solution.py:68
  83.5 1.0 broadcast_in_dim.175
  84.5 22.4 %all_to_all.32 = bf16[64,2,4096]{2,1,0:T(2,128)(2,1)} all-to-all(bf16[64,2,4096]{2,1,0:T(2,128)(2,1)S(1)} %broadcast_in_dim.175), channel_id=1, replica_groups=mesh['group'=16,'depth'=2,'mp'=4] {'group','mp'}, dimensions={0} | all-to-all | bytes 2097152 | tf_op jit(solution)/shard_map/all_to_all | solution.py:27
  106.9 1.5 %reshape.1118 = bf16[128,4096]{1,0:T(8,128)(2,1)S(1)} reshape(bf16[64,2,4096]{2,1,0:T(2,128)(2,1)} %all_to_all.32) | data formatting | bytes 2097152 | tf_op jit(solution)/shard_map/reshape | solution.py:75
  108.3 2.1 %fusion.77 = f32[128,224]{0,1:T(8,128)S(1)} fusion(bf16[128,4096]{1,0:T(8,128)(2,1)S(1)} %reshape.1118, bf16[4096,224]{0,1:T(8,128)(2,1)} %param.37), kind=kOutput, calls=%fused_computation.177 | convolution fusion | flops 234881024 | bytes 2998272 | tf_op jit(solution)/shard_map/dot_general | solution.py:252
  110.5 4.6 %convolution_convert_fusion = bf16[128,4096]{1,0:T(8,128)(2,1)} fusion(bf16[224,4096]{1,0:T(8,128)(2,1)} %param.39, bf16[128,4096]{1,0:T(8,128)(2,1)S(1)} %reshape.1118, bf16[4096,224]{0,1:T(8,128)(2,1)} %param.38, f32[128,224]{0,1:T(8,128)S(1)} %fusion.77), kind=kOutput, calls=%fused_computation.9 | convolution fusion | flops 470458368 | bytes 5881856 | tf_op jit(solution)/shard_map/dot_general | solution.py:257
  115.1 1.8 %reshape.1119 = bf16[64,2,4096]{2,1,0:T(2,128)(2,1)S(1)} reshape(bf16[128,4096]{1,0:T(8,128)(2,1)} %convolution_convert_fusion) | data formatting | bytes 2097152 | tf_op jit(solution)/shard_map/reshape | solution.py:62
  116.9 21.9 %all_to_all.33 = bf16[64,2,4096]{2,1,0:T(2,128)(2,1)S(1)} all-to-all(bf16[64,2,4096]{2,1,0:T(2,128)(2,1)S(1)} %reshape.1119), channel_id=1, replica_groups=mesh['group'=16,'depth'=2,'mp'=4] {'group','mp'}, dimensions={0} | all-to-all | bytes 2097152 | tf_op jit(solution)/shard_map/all_to_all | solution.py:84
  138.8 0.9 convert_reduce_fusion
  139.7 0.6 add_convert_fusion
  (91 shorter events, 4.0 us)
Async XLA Ops:
  0.6 24.9 %copy-start = (bf16[8,2,576,128]{3,2,1,0:T(8,128)(2,1)S(1)}, bf16[8,2,576,128]{3,2,1,0:T(8,128)(2,1)}, u32[]{:S(2)}) copy-start(bf16[8,2,576,128]{3,2,1,0:T(8,128)(2,1)} %param.28) | copy-start | bytes 7077892
  0.6 18.8 %copy-start.1 = (s32[128]{0:T(128)S(1)}, s32[128]{0:T(128)}, u32[]{:S(2)}) copy-start(s32[128]{0:T(128)} %param.30) | copy-start | bytes 1540
  9.4 24.9 %all-to-all-start = ((bf16[16,1,8,128]{3,2,1,0:T(8,128)(2,1)}), bf16[16,1,8,128]{3,2,1,0:T(8,128)(2,1)S(1)}, u32[]{:S(2)}, u32[]{:S(2)}) async-start(bf16[16,1,8,128]{3,2,1,0:T(8,128)(2,1)} %bitcast_select_fusion.4), calls=%async_computation | async-start | bytes 65536 | tf_op jit(solution)/shard_map/all_to_all | solution.py:202
  19.5 3.3 %copy-start.9 = (s32[16]{0:T(128)S(1)}, s32[16]{0:T(128)}, u32[]{:S(2)}) copy-start(s32[16]{0:T(128)} %param.27) | copy-start | bytes 196
  19.5 3.3 %copy-start.4 = (bf16[16,8,128]{2,1,0:T(8,128)(2,1)S(1)}, bf16[16,8,128]{2,1,0:T(8,128)(2,1)}, u32[]{:S(2)}) copy-start(bf16[16,8,128]{2,1,0:T(8,128)(2,1)} %param.22) | copy-start | bytes 98308
  21.4 3.9 %copy-start.10 = (bf16[16,2,128]{2,1,0:T(2,128)(2,1)S(1)}, bf16[16,2,128]{2,1,0:T(2,128)(2,1)}, u32[]{:S(2)}) copy-start(bf16[16,2,128]{2,1,0:T(2,128)(2,1)} %param.23) | copy-start | bytes 24580
  39.2 11.6 %copy-start.7 = (bf16[16,2,128]{2,1,0:T(2,128)(2,1)S(1)}, bf16[16,2,128]{2,1,0:T(2,128)(2,1)}, u32[]{:S(2)}) copy-start(bf16[16,2,128]{2,1,0:T(2,128)(2,1)} %param.24) | copy-start | bytes 24580
  39.3 19.7 %copy-start.8 = (s32[16]{0:T(128)S(1)}, s32[16]{0:T(128)}, u32[]{:S(2)}) copy-start(s32[16]{0:T(128)} %param.33) | copy-start | bytes 196
  43.4 15.2 %all-to-all-start.1 = ((f32[16,1,2,4,130]{4,3,2,1,0:T(4,128)}), f32[16,1,2,4,130]{4,3,2,1,0:T(4,128)S(1)}, u32[]{:S(2)}, u32[]{:S(2)}) async-start(f32[16,1,2,4,130]{4,3,2,1,0:T(4,128)} %maximum_bitcast_fusion), calls=%async_computation.1 | async-start | bytes 262144 | tf_op jit(solution)/shard_map/all_to_all | solution.py:18
  66.8 0.6 copy-start.5
  67.4 15.8 %copy-start.2 = (bf16[2,4096]{1,0:T(2,128)(2,1)S(1)}, bf16[2,4096]{1,0:T(2,128)(2,1)}, u32[]{:S(2)}) copy-start(bf16[2,4096]{1,0:T(2,128)(2,1)} %param.21) | copy-start | bytes 49156
  67.4 16.0 %copy-start.6 = (f32[4096]{0:T(1024)S(1)}, f32[4096]{0:T(1024)}, u32[]{:S(2)}) copy-start(f32[4096]{0:T(1024)} %param.36) | copy-start | bytes 49156
  115.1 24.5 %copy-start.3 = (bf16[2,4096]{1,0:T(2,128)(2,1)S(1)}, bf16[2,4096]{1,0:T(2,128)(2,1)}, u32[]{:S(2)}) copy-start(bf16[2,4096]{1,0:T(2,128)(2,1)} %param.21) | copy-start | bytes 49156
where the time goes:
time: 141 us; the launch traced here: 140 us
  blocking collectives  59.2 us (42%)
  local copies, waits for them, and re-layouts  24.8 us (18%)
  matrix products  23.6 us (17%)
  starting transfers between devices  14.3 us (10%)
  other arithmetic  9.69 us (7%)
  waiting for transfers between devices  7.66 us (5%)
    all_to_all x2, blocking collectives, copy_for_each(): lax.all_to_all(jnp.broadcast_to(x[None], (peers, *x.shape)), axis, 0, 0,...  26.2 us
    all_to_all x1, blocking collectives, sent_and_summed(): lax.all_to_all(blocks, axis, split_axis=0, concat_axis=0, tiled=True)  21.9 us
    all_to_all x1, blocking collectives, summed_on_arrival(): blocks = lax.all_to_all(split_up(x, dim, peers), axis, 0, 0, tiled=True)  11.1 us
    all_to_all x1, waiting for transfers between devices, sent_together(): lax.all_to_all(both, axis, split_axis=split_dim, concat_axis=concat_dim,...  7.66 us
    all_to_all x1, starting transfers between devices, sent_together(): lax.all_to_all(both, axis, split_axis=split_dim, concat_axis=concat_dim,...  7.22 us
    all_to_all x1, starting transfers between devices, on_device(): lax.all_to_all(routed, 'group', split_axis=0, concat_axis=0, tiled=True)  7.12 us
    gather x1, local copies, waits for them, and re-layouts, on_device(): owned_values = jnp.take(image_values, serve_slots, axis=0)  4.98 us
    dot_general x1, matrix products, on_device(): jnp.dot(picked_rows, out_weight, preferred_element_type=jnp.float32)  4.67 us
  transfers between devices with their start and end apart: 2, of which 1 were waited for; matrix products, arithmetic and copies ran while one was open for 13% of the time, Pallas kernels for 0%

commit v1 on v0

v1 whole, which is shorter than its diff:
```python
import functools
import math

import jax
import jax.numpy as jnp
from jax import lax
from jax.experimental import pallas as pl
from jax.experimental.pallas import tpu as pltpu
from jax.sharding import PartitionSpec as P

MASKED = -1e30
NORM_EPSILON = 1e-05
BF16 = jnp.bfloat16
F32 = jnp.float32
VMEM = pl.BlockSpec(memory_space=pltpu.VMEM)
SMEM = pl.BlockSpec(memory_space=pltpu.SMEM)


def call(kernel, out_shape, in_specs, flops, nbytes, name, scratch=(), vmem=16 << 20):
    return pl.pallas_call(
        kernel,
        out_shape=out_shape,
        in_specs=in_specs,
        out_specs=jax.tree.map(lambda _: VMEM, out_shape),
        scratch_shapes=list(scratch),
        cost_estimate=pl.CostEstimate(flops=flops, bytes_accessed=nbytes, transcendentals=0),
        compiler_params=pltpu.CompilerParams(vmem_limit_bytes=vmem),
        name=name,
    )


def matmul(a, b):
    return lax.dot_general(a, b, (((1,), (0,)), ((), ())), preferred_element_type=F32)


def matmul_t(a, b):
    return lax.dot_general(a, b, (((1,), (1,)), ((), ())), preferred_element_type=F32)


class Tables:
    def __init__(self, ref):
        self.ref = ref
        self.group, self.depth, self.mp = ref[0], ref[1], ref[2]

    def count(self):
        return self.ref[COUNT + self.group]

    def first(self, r):
        return self.ref[FIRST + r]

    def images(self, r):
        return self.ref[IMAGES + r]

    def length(self, r):
        return self.ref[LENGTH + r]

    def source(self, place):
        block = self.ref[BLOCKS + self.group * 32 + jnp.minimum(place, 31)]
        slot = self.ref[SLOTS + block]
        return slot >> 3, slot & 7


SLOTS, BLOCKS, COUNT, FIRST, IMAGES, LENGTH = 8, 136, 648, 664, 680, 696


def route_kernel(table, queries, out):
    t = Tables(table)
    count, depth = t.count(), t.depth
    requests = queries.shape[0]
    out[...] = jnp.full(out.shape, -1.0, BF16)
    for r in range(requests):
        start = t.first(r)
        skip = (start + depth) & 1
        place = start + skip
        owner, within = t.source(place)

        @pl.when((skip < t.images(r)) & (place < count))
        def _():
            out[owner, 0:8, :] = queries[r]
            code = (within * 2 + r // (requests // 2)).astype(F32)
            out[owner, 8:16, :] = jnp.full((8, 128), code, F32).astype(BF16)


def text_kernel(table, queries, new_keys, new_values, keys, values, own, other):
    t = Tables(table)
    depth = t.depth
    half = queries.shape[0] // 2
    heads, width = queries.shape[1:]
    span = keys.shape[2]
    scale = 1.0 / (math.sqrt(width) * math.log(2.0))
    for out, part in ((own, depth), (other, 1 - depth)):
        low = lax.broadcasted_iota(jnp.int32, (heads, 1), 0) < heads // 2
        scores, fresh = [], []
        for j in range(half):
            r = part * half + j
            q = queries[r]
            s = jnp.where(low, matmul_t(q, keys[r, 0]), matmul_t(q, keys[r, 1])) * scale
            at = depth * span + lax.broadcasted_iota(jnp.int32, (heads, span), 1)
            scores.append(jnp.where(at < t.length(r), s, MASKED))
            nk = new_keys[r].astype(F32)
            nk = jnp.where(low, nk[0:1], nk[1:2])
            fresh.append(jnp.sum(q.astype(F32) * nk, axis=-1, keepdims=True) * scale)
        s = jnp.concatenate(scores, axis=0)
        n = jnp.where(depth == 0, jnp.concatenate(fresh, axis=0), MASKED)
        level = jnp.floor(jnp.maximum(jnp.max(s, axis=-1, keepdims=True), n))
        w = jnp.where(s > 0.5 * MASKED, jnp.exp2(s - level), 0.0).astype(BF16)
        nw = jnp.where(n > 0.5 * MASKED, jnp.exp2(n - level), 0.0).astype(BF16).astype(F32)
        total = jnp.sum(w.astype(F32), axis=-1, keepdims=True) + nw
        lane = lax.broadcasted_iota(jnp.int32, (heads, 128), 1)
        for j in range(half):
            r = part * half + j
            rows = slice(j * heads, (j + 1) * heads)
            o = jnp.where(low, matmul(w[rows], values[r, 0]), matmul(w[rows], values[r, 1]))
            nv = new_values[r].astype(F32)
            o = o + nw[rows] * jnp.where(low, nv[0:1], nv[1:2])
            out[j, 0:8, :] = o
            out[j, 8:16, :] = jnp.where(lane < 64, level[rows], total[rows])


def image_kernel(arrived, keys, values, out):
    groups = arrived.shape[0]
    rows = groups * 8
    images, _, patches, width = keys.shape
    scale = 1.0 / (math.sqrt(width) * math.log(2.0))
    q = arrived[:, 0:8, :].reshape(rows, width)
    code = arrived[:, 8:16, :].reshape(rows, width).astype(F32)
    within = jnp.floor(code * 0.5)
    low = lax.broadcasted_iota(jnp.int32, (rows, 1), 0) % 8 < 4
    level = jnp.zeros((rows, 1), F32)
    total = jnp.zeros((rows, 1), F32)
    o = jnp.zeros((rows, width), F32)
    for i in range(images):
        mine = within[:, 0:1] == float(i)
        s = jnp.where(low, matmul_t(q, keys[i, 0]), matmul_t(q, keys[i, 1])) * scale
        here = jnp.floor(jnp.max(s, axis=-1, keepdims=True))
        w = jnp.where(mine, jnp.exp2(s - here), 0.0).astype(BF16)
        total = total + jnp.sum(w.astype(F32), axis=-1, keepdims=True)
        level = jnp.where(mine, here, level)
        o = o + jnp.where(low, matmul(w, values[i, 0]), matmul(w, values[i, 1]))
    o = o / jnp.where(total > 0.0, total, 1.0)
    lane = lax.broadcasted_iota(jnp.int32, (rows, width), 1)
    level_high = level.astype(BF16).astype(F32)
    total_high = total.astype(BF16).astype(F32)
    stats = jnp.where(
        lane < 64,
        jnp.where(lane < 32, level_high, level - level_high),
        jnp.where(lane < 96, total_high, total - total_high),
    )
    second = code - 2.0 * within
    o3 = o.astype(BF16).reshape(groups, 8, width)
    for h in range(2):
        out[:, h, 0:8, :] = o3
        out[:, h, 8:16, :] = (
            jnp.where(second == float(h), stats, 0.0).astype(BF16).reshape(groups, 8, width)
        )


def merge_kernel(table, back, own, other, out):
    t = Tables(table)
    count, depth = t.count(), t.depth
    half = own.shape[0]
    for j in range(half):
        r = depth * half + j
        parts = []
        for ref in (own, other):
            stats = ref[j, 8:16, :]
            parts.append((stats[:, 0:1], stats[:, 64:65], ref[j, 0:8, :]))
        for k in range(2):
            place = t.first(r) + k
            owner, _ = t.source(place)
            live = (k < t.images(r)) & (place < count)
            at = owner * 2 + (place & 1)
            stats = back[at, 8:16, :].astype(F32)
            level = jnp.where(live, stats[:, 0:1] + stats[:, 32:33], MASKED)
            total = jnp.where(live, stats[:, 64:65] + stats[:, 96:97], 0.0)
            parts.append((level, total, back[at, 0:8, :].astype(F32) * total))
        top = functools.reduce(jnp.maximum, [p[0] for p in parts])
        factors = [jnp.exp2(p[0] - top) for p in parts]
        total = sum(f * p[1] for f, p in zip(factors, parts))
        weighted = sum(f * p[2] for f, p in zip(factors, parts))
        out[j] = (weighted / total).astype(BF16)


def norm_kernel(mine, first, second, third, gain, residual, out):
    x = mine[...] + first[...].astype(F32) + second[...].astype(F32) + third[...].astype(F32)
    residual[...] = x
    spread = jnp.mean(x * x, axis=-1, keepdims=True)
    normed = (x * lax.rsqrt(spread + NORM_EPSILON) * gain[...]).astype(BF16)
    for g in range(out.shape[0]):
        out[g] = normed


def feed_kernel(x, gate, up, down, out):
    a = matmul_t(x[...], gate[...])
    b = matmul_t(x[...], up[...])
    hidden = (a / (1.0 + jnp.exp(-a)) * b).astype(BF16)
    width = 512
    for c in range(out.shape[1] // width):
        at = slice(c * width, (c + 1) * width)
        out[:, at] = matmul(hidden, down[:, at]).astype(BF16)


def total_kernel(table, arrived, kept, first, second, third):
    m = table[2]
    x = arrived[0].astype(F32)
    for g in range(1, arrived.shape[0]):
        x = x + arrived[g].astype(F32)
    for k, out in enumerate((kept, first, second, third)):
        rows = x[0:2]
        for c in range(1, 4):
            rows = jnp.where((m ^ k) == c, x[2 * c : 2 * c + 2], rows)
        out[...] = rows.astype(out.dtype)


def on_device(
    states,
    queries,
    new_keys,
    new_values,
    text_keys,
    text_values,
    text_length,
    image_keys,
    image_values,
    image_slot,
    block_list,
    block_count,
    image_first,
    image_count,
    out_weight,
    norm_gain,
    gate_weight,
    up_weight,
    down_weight,
):
    groups = lax.axis_size("group")
    depths = lax.axis_size("depth")
    ring = lax.axis_size("mp")
    mp_index = lax.axis_index("mp")
    ids = [lax.axis_index("group"), lax.axis_index("depth"), mp_index]
    table = jnp.concatenate(
        [jnp.stack(ids + [0] * 5).astype(jnp.int32), image_slot, block_list.reshape(-1)]
        + [block_count, image_first, image_count, text_length]
    )
    requests, heads, width = queries.shape
    half = requests // depths
    features = states.shape[1]

    routed = call(
        route_kernel,
        jax.ShapeDtypeStruct((groups, 16, width), BF16),
        [SMEM, VMEM],
        0,
        100_000,
        "route",
    )(table, queries)
    arrived = lax.all_to_all(routed, "group", 0, 0, tiled=True)

    part = jax.ShapeDtypeStruct((half, 16, width), F32)
    own, other = call(
        text_kernel,
        (part, part),
        [SMEM] + [VMEM] * 5,
        200_000_000,
        4_400_000,
        "text",
    )(table, queries, new_keys, new_values, text_keys, text_values)
    other = lax.ppermute(other, "depth", [(0, 1), (1, 0)])

    back = call(
        image_kernel,
        jax.ShapeDtypeStruct((groups, depths, 16, width), BF16),
        [VMEM] * 3,
        600_000_000,
        5_000_000,
        "image",
    )(arrived, image_keys, image_values)
    back = lax.all_to_all(
        back.reshape(groups * depths, 16, width), ("group", "depth"), 0, 0, tiled=True
    )
    attention = call(
        merge_kernel,
        jax.ShapeDtypeStruct((half, heads, width), BF16),
        [SMEM] + [VMEM] * 3,
        0,
        300_000,
        "merge",
    )(table, back, own, other)

    projected = jnp.dot(
        attention.reshape(half, heads * width), out_weight, preferred_element_type=F32
    )
    mine = lax.dynamic_update_slice_in_dim(
        jnp.zeros((half, features), F32), states.astype(F32), 2 * mp_index, 0
    )
    mine = projected + mine
    sent = mine.astype(BF16)
    passed = [
        lax.ppermute(sent, "mp", [(i, i ^ k) for i in range(ring)]) for k in range(1, ring)
    ]
    residual, normed = call(
        norm_kernel,
        (
            jax.ShapeDtypeStruct((half, features), F32),
            jax.ShapeDtypeStruct((groups, half, features), BF16),
        ),
        [VMEM] * 5,
        0,
        1_600_000,
        "norm",
    )(mine, *passed, norm_gain.reshape(1, features))
    tokens = lax.all_to_all(normed, "group", 0, 0, tiled=True).reshape(groups * half, features)
    down = call(
        feed_kernel,
        jax.ShapeDtypeStruct((groups * half, features), BF16),
        [VMEM] * 4,
        1_400_000_000,
        7_000_000,
        "feed",
    )(tokens, gate_weight.T, up_weight.T, down_weight)
    gathered = lax.all_to_all(down.reshape(groups, half, features), "group", 0, 0, tiled=True)
    pair = (2, features)
    kept, *sends = call(
        total_kernel,
        (jax.ShapeDtypeStruct(pair, F32),) + (jax.ShapeDtypeStruct(pair, BF16),) * 3,
        [SMEM, VMEM],
        0,
        1_300_000,
        "total",
    )(table, gathered)
    got = [
        lax.ppermute(s, "mp", [(i, i ^ k) for i in range(ring)])
        for k, s in zip(range(1, ring), sends)
    ]
    rest = lax.dynamic_slice_in_dim(residual, 2 * mp_index, 2, 0)
    for g in (kept, *got):
        rest = rest + g.astype(F32)
    return attention, rest.astype(BF16)


def solution(mesh):
    placed = (
        P(("group", "depth", "mp"), None),
        P("group", "mp", None),
        P("group", "mp", None),
        P("group", "mp", None),
        P("group", "mp", "depth", None),
        P("group", "mp", "depth", None),
        P("group"),
        P("group", "mp", None, None),
        P("group", "mp", None, None),
        P(),
        P(),
        P(),
        P("group"),
        P("group"),
        P("mp", None),
        P(),
        P(None, ("group", "mp")),
        P(None, ("group", "mp")),
        P(("group", "mp"), None),
    )
    return jax.shard_map(
        on_device,
        mesh=mesh,
        in_specs=placed,
        out_specs=(P(("group", "depth"), "mp", None), P(("group", "depth", "mp"), None)),
        check_vma=False,
    )
```

time: 141 us -> 104 us (0.74)
  matrix products: 23.6 us -> 4.74 us
  local copies, waits for them, and re-layouts: 24.8 us -> 7.28 us
  Pallas kernels: 0 us -> 11.3 us
  other arithmetic: 9.69 us -> 0.7 us
  blocking collectives: 59.2 us -> 52.5 us
  waiting for transfers between devices: 7.66 us -> 12.7 us
    dot_general x9 -> x1, matrix products: 23.4 us -> 4.74 us  [on_device(): jnp.dot(attention.reshape(half, heads * width), out_weight, preferred_ele...]
    gather x9 -> x0, local copies, waits for them, and re-layouts: 14.1 us -> none  [the longest x1 4.98 us: on_device(): owned_values = jnp.take(image_values, serve_slots, axis=0)]
    pallas_call x0 -> x7, Pallas kernels: none -> 11.3 us  [the longest x1 4.3 us: on_device(): call(image_kernel, jax.ShapeDtypeStruct((groups, depths, 16, width), BF16...]
    all_to_all x2 -> x1, starting transfers between devices: 14.3 us -> 3.84 us  [on_device(): lax.all_to_all(back.reshape(groups * depths, 16, width), ('group', 'depth...]
    ppermute x0 -> x7, starting transfers between devices: none -> 10 us  [the longest x3 5.05 us: on_device(): lax.ppermute(sent, 'mp', [(i, i ^ k) for i in range(ring)])]
    ppermute x0 -> x7, waiting for transfers between devices: none -> 9.71 us  [the longest x3 5.08 us: on_device(): lax.ppermute(sent, 'mp', [(i, i ^ k) for i in range(ring)])]
    all_to_all x4 -> x3, blocking collectives: 59.2 us -> 52.5 us  [the longest x1 20.1 us: on_device(): lax.all_to_all(normed, 'group', 0, 0, tiled=True)]
    all_to_all x2 -> x1, waiting for transfers between devices: 7.66 us -> 3.01 us  [on_device(): lax.all_to_all(back.reshape(groups * depths, 16, width), ('group', 'depth...]
  transfers between devices with their start and end apart: 2 -> 8, of which waited for: 1 -> 6; matrix products, arithmetic and copies ran while one was open for 13% -> 0% of each run, Pallas kernels for 0% -> 2%
where the time goes in v1:
time: 104 us
  blocking collectives  52.5 us (50%)
  starting transfers between devices  13.9 us (13%)
  waiting for transfers between devices  12.7 us (12%)
  Pallas kernels  11.3 us (11%)
  local copies, waits for them, and re-layouts  7.28 us (7%)
  matrix products  4.74 us (5%)
    all_to_all x1, blocking collectives, on_device(): lax.all_to_all(normed, 'group', 0, 0, tiled=True)  20.1 us
    all_to_all x1, blocking collectives, on_device(): lax.all_to_all(down.reshape(groups, half, features), 'group', 0, 0, tiled...  17.9 us
    all_to_all x1, blocking collectives, on_device(): arrived = lax.all_to_all(routed, 'group', 0, 0, tiled=True)  14.6 us
    unnamed x26, local copies, waits for them, and re-layouts  5.71 us
    ppermute x3, waiting for transfers between devices, on_device(): lax.ppermute(sent, 'mp', [(i, i ^ k) for i in range(ring)])  5.08 us
    ppermute x3, starting transfers between devices, on_device(): lax.ppermute(sent, 'mp', [(i, i ^ k) for i in range(ring)])  5.05 us
    ppermute x3, starting transfers between devices, on_device(): lax.ppermute(s, 'mp', [(i, i ^ k) for i in range(ring)])  4.78 us
    dot_general x1, matrix products, on_device(): jnp.dot(attention.reshape(half, heads * width), out_weight, preferred_ele...  4.74 us
  transfers between devices with their start and end apart: 8, of which 6 were waited for; matrix products, arithmetic and copies ran while one was open for 0% of the time, Pallas kernels for 2%

profile of v1, /device:TPU:0, one launch (start us, length us, event | category | flops | bytes accessed | tf_op | source)
XLA Modules:
  0.0 104.0 jit_solution(11349180945809975538)
XLA Ops:
  0.6 0.8 reshape.22
  1.4 0.8 concatenate.3.table
  2.2 0.0 copy-start.7
  2.2 0.8 copy-done.7
  3.0 0.9 route.1
  3.8 14.6 %all_to_all.20.arrived = bf16[16,16,128]{2,1,0:T(8,128)(2,1)S(1)} all-to-all(bf16[16,16,128]{2,1,0:T(8,128)(2,1)S(1)} %route.1), channel_id=1, replica_groups=mesh['group'=16,'depth'=2,'mp'=4] {'group'}, dimensions={0} | all-to-all | bytes 131072 | tf_op jit(solution)/shard_map/all_to_all | solution.py:257
  18.4 0.0 copy-start
  18.4 1.7 %copy-done = bf16[8,2,576,128]{3,2,1,0:T(8,128)(2,1)S(1)} copy-done((bf16[8,2,576,128]{3,2,1,0:T(8,128)(2,1)S(1)}, bf16[8,2,576,128]{3,2,1,0:T(8,128)(2,1)}, u32[]{:S(2)}) %copy-start) | copy-done | bytes 2359320
  20.1 0.0 copy-start.1
  20.1 1.7 %copy-done.1 = bf16[8,2,576,128]{3,2,1,0:T(8,128)(2,1)S(1)} copy-done((bf16[8,2,576,128]{3,2,1,0:T(8,128)(2,1)S(1)}, bf16[8,2,576,128]{3,2,1,0:T(8,128)(2,1)}, u32[]{:S(2)}) %copy-start.1) | copy-done | bytes 2359320
  21.8 0.0 copy-start.2
  21.8 4.3 %image.1 = bf16[16,2,16,128]{3,2,1,0:T(8,128)(2,1)} custom-call(bf16[16,16,128]{2,1,0:T(8,128)(2,1)S(1)} %all_to_all.20.arrived, bf16[8,2,576,128]{3,2,1,0:T(8,128)(2,1)S(1)} %copy-done, bf16[8,2,576,128]{3,2,1,0:T(8,128)(2,1)S(1)} %copy-done.1), custom_call_target="tpu_custom_call" | custom-call | flops 600000000 | bytes 5000000 | tf_op jit(solution)/shard_map/image/pallas_call | solution.py:270
  26.1 3.8 %all-to-all-start.1 = ((bf16[32,16,128]{2,1,0:T(8,128)(2,1)}), bf16[32,16,128]{2,1,0:T(8,128)(2,1)S(1)}, u32[]{:S(2)}, u32[]{:S(2)}) async-start(bf16[32,16,128]{2,1,0:T(8,128)(2,1)} %bitcast.3), calls=%async_computation.1 | async-start | bytes 262144 | tf_op jit(solution)/shard_map/all_to_all | solution.py:278
  29.9 0.0 copy-done.2
  29.9 0.0 copy-done.8
  29.9 0.0 copy-done.10
  29.9 0.0 copy-done.11
  30.0 0.0 copy-start.3
  30.0 1.6 %copy-done.3 = bf16[16,2,256,128]{3,2,1,0:T(8,128)(2,1)S(1)} copy-done((bf16[16,2,256,128]{3,2,1,0:T(8,128)(2,1)S(1)}, bf16[16,2,256,128]{3,2,1,0:T(8,128)(2,1)}, u32[]{:S(2)}) %copy-start.3) | copy-done | bytes 2097176
  31.5 1.8 %text.1 = (f32[8,16,128]{2,1,0:T(8,128)S(1)}, f32[8,16,128]{2,1,0:T(8,128)S(1)}) custom-call(s32[712]{0:T(1024)S(1)} %concatenate.3.table, bf16[16,8,128]{2,1,0:T(8,128)(2,1)S(1)} %copy-done.8, bf16[16,2,128]{2,1,0:T(2,128)(2,1)S(1)} %copy-done.10, bf16[16,2,128]{2,1,0:T(2,128)(2,1)S(1)} %copy-done.11, bf16[16,2,256,128]{3,2,1,0:T(8,128)(2,1)S(1)} %copy-done.2, ...), custom_call_target="tpu_custom_call" | custom-call | flops 200000000 | bytes 4400000 | tf_op jit(solution)/shard_map/text/pallas_call | solution.py:260
  33.4 0.2 collective-permute-start
  33.6 1.1 %collective-permute-done.other = f32[8,16,128]{2,1,0:T(8,128)S(1)} collective-permute-done((f32[8,16,128]{2,1,0:T(8,128)S(1)}, f32[8,16,128]{2,1,0:T(8,128)S(1)}, u32[]{:S(2)}, u32[]{:S(2)}) %collective-permute-start) | collective-permute-done | bytes 65568 | tf_op jit(solution)/shard_map/ppermute | solution.py:268
  34.7 3.0 %all-to-all-done.1.back = bf16[32,16,128]{2,1,0:T(8,128)(2,1)S(1)} async-done(((bf16[32,16,128]{2,1,0:T(8,128)(2,1)}), bf16[32,16,128]{2,1,0:T(8,128)(2,1)S(1)}, u32[]{:S(2)}, u32[]{:S(2)}) %all-to-all-start.1) | async-done | bytes 131104 | tf_op jit(solution)/shard_map/all_to_all | solution.py:278
  37.7 1.5 %merge.1 = bf16[8,8,128]{2,1,0:T(8,128)(2,1)} custom-call(s32[712]{0:T(1024)S(1)} %concatenate.3.table, bf16[32,16,128]{2,1,0:T(8,128)(2,1)S(1)} %all-to-all-done.1.back, f32[8,16,128]{2,1,0:T(8,128)S(1)} %get-tuple-element.10.own, f32[8,16,128]{2,1,0:T(8,128)S(1)} %collective-permute-done.other), custom_call_target="tpu_custom_call" | custom-call | bytes 300000 | tf_op jit(solution)/shard_map/merge/pallas_call | solution.py:281
  39.2 4.7 %fusion = f32[8,4096]{1,0:T(8,128)S(1)} fusion(bf16[1024,4096]{1,0:T(8,128)(2,1)} %param.33, bf16[1,8,8,128]{3,2,1,0:T(8,128)(2,1)} %bitcast.19), kind=kOutput, calls=%fused_computation.2 | convolution fusion | flops 67108864 | bytes 8536064 | tf_op jit(solution)/shard_map/dot_general | solution.py:290
  44.0 0.0 copy-done.12
  44.0 4.1 %collective-permute-start.3 = (bf16[8,4096]{1,0:T(8,128)(2,1)S(1)}, bf16[8,4096]{1,0:T(8,128)(2,1)S(1)}, u32[]{:S(2)}, u32[]{:S(2)}) collective-permute-start(bf16[8,4096]{1,0:T(8,128)(2,1)S(1)} %convert_element_type.19), channel_id=1, source_target_pairs={{0,3},{1,2},{2,1},{3,0},{4,7},{5,6},{6,5},{7,4},{8,11},{9,10},{10,... | collective-permute-start | bytes 196616 | tf_op jit(solution)/shard_map/ppermute | solution.py:299
  48.1 0.0 collective-permute-start.2
  48.1 0.9 collective-permute-start.1
  49.1 2.1 %collective-permute-done.3.third = bf16[8,4096]{1,0:T(8,128)(2,1)S(1)} collective-permute-done((bf16[8,4096]{1,0:T(8,128)(2,1)S(1)}, bf16[8,4096]{1,0:T(8,128)(2,1)S(1)}, u32[]{:S(2)}, u32[]{:S(2)}) %collective-permute-start.3) | collective-permute-done | bytes 65568 | tf_op jit(solution)/shard_map/ppermute | solution.py:299
  51.2 3.0 %collective-permute-done.2.second = bf16[8,4096]{1,0:T(8,128)(2,1)S(1)} collective-permute-done((bf16[8,4096]{1,0:T(8,128)(2,1)S(1)}, bf16[8,4096]{1,0:T(8,128)(2,1)S(1)}, u32[]{:S(2)}, u32[]{:S(2)}) %collective-permute-start.2) | collective-permute-done | bytes 65568 | tf_op jit(solution)/shard_map/ppermute | solution.py:299
  54.2 0.0 collective-permute-done.1.first
  54.2 0.0 copy-done.9
  54.2 0.2 norm.1
  54.4 20.1 %all_to_all.21 = bf16[16,8,4096]{2,1,0:T(8,128)(2,1)S(1)} all-to-all(bf16[16,8,4096]{2,1,0:T(8,128)(2,1)S(1)} %get-tuple-element.13), channel_id=1, replica_groups=mesh['group'=16,'depth'=2,'mp'=4] {'group'}, dimensions={0} | all-to-all | bytes 2097152 | tf_op jit(solution)/shard_map/all_to_all | solution.py:312
  74.5 0.0 copy-done.5
  74.5 0.0 copy-done.6
  74.5 0.0 copy-done.4
  74.5 1.8 %feed.1 = bf16[128,4096]{1,0:T(8,128)(2,1)S(1)} custom-call(bf16[128,4096]{1,0:T(8,128)(2,1)S(1)} %bitcast.14, bf16[224,4096]{1,0:T(8,128)(2,1)S(1)} %bitcast.16, bf16[224,4096]{1,0:T(8,128)(2,1)S(1)} %bitcast.17, bf16[224,4096]{1,0:T(8,128)(2,1)S(1)} %copy-done.6), custom_call_target="tpu_custom_call" | custom-call | flops 1400000000 | bytes 7000000 | tf_op jit(solution)/shard_map/feed/pallas_call | solution.py:313
  76.3 17.9 %all_to_all.22.arrived = bf16[16,8,4096]{2,1,0:T(8,128)(2,1)S(1)} all-to-all(bf16[16,8,4096]{2,1,0:T(8,128)(2,1)S(1)} %bitcast.15), channel_id=1, replica_groups=mesh['group'=16,'depth'=2,'mp'=4] {'group'}, dimensions={0} | all-to-all | bytes 2097152 | tf_op jit(solution)/shard_map/all_to_all | solution.py:321
  94.1 0.8 total.1
  95.0 0.2 collective-permute-start.4
  95.2 3.2 %collective-permute-start.5 = (bf16[2,4096]{1,0:T(2,128)(2,1)S(1)}, bf16[2,4096]{1,0:T(2,128)(2,1)S(1)}, u32[]{:S(2)}, u32[]{:S(2)}) collective-permute-start(bf16[2,4096]{1,0:T(2,128)(2,1)S(1)} %get-tuple-element.16), channel_id=1, source_target_pairs={{0,2},{1,3},{2,0},{3,1},{4,6},{5,7},{6,4},{7,5},{8,10},{9,11},{10,... | collective-permute-start | bytes 49160 | tf_op jit(solution)/shard_map/ppermute | solution.py:332
  98.4 1.4 %collective-permute-start.6 = (bf16[2,4096]{1,0:T(2,128)(2,1)S(1)}, bf16[2,4096]{1,0:T(2,128)(2,1)S(1)}, u32[]{:S(2)}, u32[]{:S(2)}) collective-permute-start(bf16[2,4096]{1,0:T(2,128)(2,1)S(1)} %get-tuple-element.17), channel_id=1, source_target_pairs={{0,3},{1,2},{2,1},{3,0},{4,7},{5,6},{6,5},{7,4},{8,11},{9,10},{10,... | collective-permute-start | bytes 49160 | tf_op jit(solution)/shard_map/ppermute | solution.py:332
  99.8 0.0 collective-permute-done.4
  99.8 0.7 collective-permute-done.5
  100.4 2.9 %collective-permute-done.6 = bf16[2,4096]{1,0:T(2,128)(2,1)S(1)} collective-permute-done((bf16[2,4096]{1,0:T(2,128)(2,1)S(1)}, bf16[2,4096]{1,0:T(2,128)(2,1)S(1)}, u32[]{:S(2)}, u32[]{:S(2)}) %collective-permute-start.6) | collective-permute-done | bytes 16416 | tf_op jit(solution)/shard_map/ppermute | solution.py:332
  103.3 0.7 add_convert_fusion
  (11 shorter events, 0.1 us)
Async XLA Ops:
  2.2 0.8 copy-start.7
  18.4 1.7 %copy-start = (bf16[8,2,576,128]{3,2,1,0:T(8,128)(2,1)S(1)}, bf16[8,2,576,128]{3,2,1,0:T(8,128)(2,1)}, u32[]{:S(2)}) copy-start(bf16[8,2,576,128]{3,2,1,0:T(8,128)(2,1)} %keys.2) | copy-start | bytes 7077892
  20.1 1.7 %copy-start.1 = (bf16[8,2,576,128]{3,2,1,0:T(8,128)(2,1)S(1)}, bf16[8,2,576,128]{3,2,1,0:T(8,128)(2,1)}, u32[]{:S(2)}) copy-start(bf16[8,2,576,128]{3,2,1,0:T(8,128)(2,1)} %values.2) | copy-start | bytes 7077892
  21.8 8.2 %copy-start.2 = (bf16[16,2,256,128]{3,2,1,0:T(8,128)(2,1)S(1)}, bf16[16,2,256,128]{3,2,1,0:T(8,128)(2,1)}, u32[]{:S(2)}) copy-start(bf16[16,2,256,128]{3,2,1,0:T(8,128)(2,1)} %keys.3) | copy-start | bytes 6291460
  21.8 8.2 %copy-start.8 = (bf16[16,8,128]{2,1,0:T(8,128)(2,1)S(1)}, bf16[16,8,128]{2,1,0:T(8,128)(2,1)}, u32[]{:S(2)}) copy-start(bf16[16,8,128]{2,1,0:T(8,128)(2,1)} %queries.3) | copy-start | bytes 98308
  21.8 8.2 %copy-start.10 = (bf16[16,2,128]{2,1,0:T(2,128)(2,1)S(1)}, bf16[16,2,128]{2,1,0:T(2,128)(2,1)}, u32[]{:S(2)}) copy-start(bf16[16,2,128]{2,1,0:T(2,128)(2,1)} %new_keys.1) | copy-start | bytes 24580
  21.8 8.2 %copy-start.11 = (bf16[16,2,128]{2,1,0:T(2,128)(2,1)S(1)}, bf16[16,2,128]{2,1,0:T(2,128)(2,1)}, u32[]{:S(2)}) copy-start(bf16[16,2,128]{2,1,0:T(2,128)(2,1)} %new_values.1) | copy-start | bytes 24580
  26.1 11.6 %all-to-all-start.1 = ((bf16[32,16,128]{2,1,0:T(8,128)(2,1)}), bf16[32,16,128]{2,1,0:T(8,128)(2,1)S(1)}, u32[]{:S(2)}, u32[]{:S(2)}) async-start(bf16[32,16,128]{2,1,0:T(8,128)(2,1)} %bitcast.3), calls=%async_computation.1 | async-start | bytes 262144 | tf_op jit(solution)/shard_map/all_to_all | solution.py:278
  30.0 1.6 %copy-start.3 = (bf16[16,2,256,128]{3,2,1,0:T(8,128)(2,1)S(1)}, bf16[16,2,256,128]{3,2,1,0:T(8,128)(2,1)}, u32[]{:S(2)}) copy-start(bf16[16,2,256,128]{3,2,1,0:T(8,128)(2,1)} %values.3) | copy-start | bytes 6291460
  33.4 1.3 %collective-permute-start = (f32[8,16,128]{2,1,0:T(8,128)S(1)}, f32[8,16,128]{2,1,0:T(8,128)S(1)}, u32[]{:S(2)}, u32[]{:S(2)}) collective-permute-start(f32[8,16,128]{2,1,0:T(8,128)S(1)} %get-tuple-element.11), channel_id=1, source_target_pairs={{0,4},{4,0},{1,5},{5,1},{2,6},{6,2},{3,7},{7,3},{8,12},{12,8},{9,1... | collective-permute-start | bytes 196616 | tf_op jit(solution)/shard_map/ppermute | solution.py:268
  39.2 4.8 %copy-start.12 = (bf16[2,4096]{1,0:T(2,128)(2,1)S(1)}, bf16[2,4096]{1,0:T(2,128)(2,1)}, u32[]{:S(2)}) copy-start(bf16[2,4096]{1,0:T(2,128)(2,1)} %param.19) | copy-start | bytes 49156
  39.2 14.9 %copy-start.9 = (f32[4096]{0:T(1024)S(1)}, f32[4096]{0:T(1024)}, u32[]{:S(2)}) copy-start(f32[4096]{0:T(1024)} %param.34) | copy-start | bytes 49156
  39.2 35.3 %copy-start.5 = (bf16[4096,224]{0,1:T(8,128)(2,1)S(1)}, bf16[4096,224]{0,1:T(8,128)(2,1)}, u32[]{:S(2)}) copy-start(bf16[4096,224]{0,1:T(8,128)(2,1)} %param.36) | copy-start | bytes 5505028
  39.2 35.3 %copy-start.6 = (bf16[224,4096]{1,0:T(8,128)(2,1)S(1)}, bf16[224,4096]{1,0:T(8,128)(2,1)}, u32[]{:S(2)}) copy-start(bf16[224,4096]{1,0:T(8,128)(2,1)} %down.1) | copy-start | bytes 5505028
  44.0 30.5 %copy-start.4 = (bf16[4096,224]{0,1:T(8,128)(2,1)S(1)}, bf16[4096,224]{0,1:T(8,128)(2,1)}, u32[]{:S(2)}) copy-start(bf16[4096,224]{0,1:T(8,128)(2,1)} %param.35) | copy-start | bytes 5505028
  44.0 7.2 %collective-permute-start.3 = (bf16[8,4096]{1,0:T(8,128)(2,1)S(1)}, bf16[8,4096]{1,0:T(8,128)(2,1)S(1)}, u32[]{:S(2)}, u32[]{:S(2)}) collective-permute-start(bf16[8,4096]{1,0:T(8,128)(2,1)S(1)} %convert_element_type.19), channel_id=1, source_target_pairs={{0,3},{1,2},{2,1},{3,0},{4,7},{5,6},{6,5},{7,4},{8,11},{9,10},{10,... | collective-permute-start | bytes 196616 | tf_op jit(solution)/shard_map/ppermute | solution.py:299
  48.1 6.0 %collective-permute-start.2 = (bf16[8,4096]{1,0:T(8,128)(2,1)S(1)}, bf16[8,4096]{1,0:T(8,128)(2,1)S(1)}, u32[]{:S(2)}, u32[]{:S(2)}) collective-permute-start(bf16[8,4096]{1,0:T(8,128)(2,1)S(1)} %convert_element_type.19), channel_id=1, source_target_pairs={{0,2},{1,3},{2,0},{3,1},{4,6},{5,7},{6,4},{7,5},{8,10},{9,11},{10,... | collective-permute-start | bytes 196616 | tf_op jit(solution)/shard_map/ppermute | solution.py:299
  48.1 6.0 %collective-permute-start.1 = (bf16[8,4096]{1,0:T(8,128)(2,1)S(1)}, bf16[8,4096]{1,0:T(8,128)(2,1)S(1)}, u32[]{:S(2)}, u32[]{:S(2)}) collective-permute-start(bf16[8,4096]{1,0:T(8,128)(2,1)S(1)} %convert_element_type.19), channel_id=1, source_target_pairs={{0,1},{1,0},{2,3},{3,2},{4,5},{5,4},{6,7},{7,6},{8,9},{9,8},{10,11... | collective-permute-start | bytes 196616 | tf_op jit(solution)/shard_map/ppermute | solution.py:299
  95.0 4.8 %collective-permute-start.4 = (bf16[2,4096]{1,0:T(2,128)(2,1)S(1)}, bf16[2,4096]{1,0:T(2,128)(2,1)S(1)}, u32[]{:S(2)}, u32[]{:S(2)}) collective-permute-start(bf16[2,4096]{1,0:T(2,128)(2,1)S(1)} %get-tuple-element.15), channel_id=1, source_target_pairs={{0,1},{1,0},{2,3},{3,2},{4,5},{5,4},{6,7},{7,6},{8,9},{9,8},{10,11... | collective-permute-start | bytes 49160 | tf_op jit(solution)/shard_map/ppermute | solution.py:332
  95.2 5.2 %collective-permute-start.5 = (bf16[2,4096]{1,0:T(2,128)(2,1)S(1)}, bf16[2,4096]{1,0:T(2,128)(2,1)S(1)}, u32[]{:S(2)}, u32[]{:S(2)}) collective-permute-start(bf16[2,4096]{1,0:T(2,128)(2,1)S(1)} %get-tuple-element.16), channel_id=1, source_target_pairs={{0,2},{1,3},{2,0},{3,1},{4,6},{5,7},{6,4},{7,5},{8,10},{9,11},{10,... | collective-permute-start | bytes 49160 | tf_op jit(solution)/shard_map/ppermute | solution.py:332
  98.4 4.9 %collective-permute-start.6 = (bf16[2,4096]{1,0:T(2,128)(2,1)S(1)}, bf16[2,4096]{1,0:T(2,128)(2,1)S(1)}, u32[]{:S(2)}, u32[]{:S(2)}) collective-permute-start(bf16[2,4096]{1,0:T(2,128)(2,1)S(1)} %get-tuple-element.17), channel_id=1, source_target_pairs={{0,3},{1,2},{2,1},{3,0},{4,7},{5,6},{6,5},{7,4},{8,11},{9,10},{10,... | collective-permute-start | bytes 49160 | tf_op jit(solution)/shard_map/ppermute | solution.py:332

commit v2 on v1

v2 whole, which is shorter than its diff:
```python
import functools
import math

import jax
import jax.numpy as jnp
from jax import lax
from jax.experimental import pallas as pl
from jax.experimental.pallas import tpu as pltpu
from jax.sharding import PartitionSpec as P

MASKED = -1e30
NORM_EPSILON = 1e-05
BF16 = jnp.bfloat16
F32 = jnp.float32
VMEM = pl.BlockSpec(memory_space=pltpu.VMEM)
SMEM = pl.BlockSpec(memory_space=pltpu.SMEM)


HBM = pl.BlockSpec(memory_space=pltpu.MemorySpace.HBM)


def call(kernel, out_shape, in_specs, flops, nbytes, name, scratch=(), vmem=16 << 20, out_specs=None):
    return pl.pallas_call(
        kernel,
        out_shape=out_shape,
        in_specs=in_specs,
        out_specs=out_specs or jax.tree.map(lambda _: VMEM, out_shape),
        scratch_shapes=list(scratch),
        cost_estimate=pl.CostEstimate(flops=flops, bytes_accessed=nbytes, transcendentals=0),
        compiler_params=pltpu.CompilerParams(vmem_limit_bytes=vmem),
        name=name,
    )


def in_hbm(x):
    return pltpu.with_memory_space_constraint(x, pltpu.MemorySpace.HBM)


def matmul(a, b):
    return lax.dot_general(a, b, (((1,), (0,)), ((), ())), preferred_element_type=F32)


def matmul_t(a, b):
    return lax.dot_general(a, b, (((1,), (1,)), ((), ())), preferred_element_type=F32)


OWN_DEPTH, OWN_MP, LENGTH, SOURCE = 0, 1, 8, 24


def route_kernel(
    slots_hbm, blocks_hbm, count_hbm, first_hbm, images_hbm, lengths_hbm, queries_hbm, out, plan, *scratch
):
    slots, blocks, count, first, images, lengths, queries, sems = scratch
    copies = [
        pltpu.make_async_copy(src, dst, sems.at[k])
        for k, (src, dst) in enumerate(
            (
                (first_hbm, first),
                (images_hbm, images),
                (count_hbm, count),
                (blocks_hbm, blocks),
                (slots_hbm, slots),
                (lengths_hbm, lengths),
                (queries_hbm, queries),
            )
        )
    ]
    for copy in copies:
        copy.start()
    group, depth = lax.axis_index("group"), lax.axis_index("depth")
    requests = queries.shape[0]
    half = requests // 2
    out[...] = jnp.full(out.shape, -1.0, BF16)
    plan[OWN_DEPTH] = depth
    plan[OWN_MP] = lax.axis_index("mp")
    for copy in copies:
        copy.wait()
    listed = count[group]

    def source(place):
        slot = slots[blocks[group, jnp.minimum(place, blocks.shape[1] - 1)]]
        return slot >> 3, slot & 7

    for r in range(requests):
        start = first[r]
        skip = (start + depth) & 1
        place = start + skip
        owner, within = source(place)
        plan[LENGTH + r] = lengths[r]

        @pl.when((skip < images[r]) & (place < listed))
        def _():
            out[owner, 0:8, :] = queries[r]
            code = (within * 2 + r // half).astype(F32)
            out[owner, 8:16, :] = jnp.full((8, 128), code, F32).astype(BF16)

    for j in range(half):
        r = depth * half + j
        for k in range(2):
            place = first[r] + k
            owner, _ = source(place)
            live = (k < images[r]) & (place < listed)
            plan[SOURCE + 2 * j + k] = jnp.where(live, owner * 2 + (place & 1), -1)


def side_by_side(pair):
    return jnp.concatenate([pair[0], pair[1]], axis=1)


def text_kernel(plan, queries, new_keys, new_values, keys_hbm, values_hbm, own, other, keys, values, sems):
    depth = plan[OWN_DEPTH]
    requests, heads, width = queries.shape
    half = requests // 2
    span = keys.shape[2]
    step = requests // 4
    scale = 1.0 / (math.sqrt(width) * math.log(2.0))
    chunks = []
    for c in range(4):
        part, out = (depth, own) if c < 2 else (1 - depth, other)
        begin = part * half + (c % 2) * step
        at = pl.ds(begin, step)
        moves = [
            pltpu.make_async_copy(src.at[at], dst.at[at], sems.at[k, c])
            for k, (src, dst) in enumerate(((keys_hbm, keys), (values_hbm, values)))
        ]
        for move in moves:
            move.start()
        chunks.append((begin, (c % 2) * step, out, moves))
    low = lax.broadcasted_iota(jnp.int32, (heads, 1), 0) < heads // 2
    lane = lax.broadcasted_iota(jnp.int32, (heads, 128), 1)
    where = depth * span + lax.broadcasted_iota(jnp.int32, (heads, span), 1)
    for begin, row, out, moves in chunks:
        moves[0].wait()
        scores, fresh = [], []
        for j in range(step):
            r = begin + j
            q = queries[r]
            zero = jnp.zeros_like(q)
            both = jnp.concatenate([jnp.where(low, q, zero), jnp.where(low, zero, q)], axis=1)
            s = matmul_t(both, side_by_side(keys[r])) * scale
            scores.append(jnp.where(where < plan[LENGTH + r], s, MASKED))
            nk = new_keys[r].astype(F32)
            nk = jnp.where(low, nk[0:1], nk[1:2])
            fresh.append(jnp.sum(q.astype(F32) * nk, axis=-1, keepdims=True) * scale)
        s = jnp.concatenate(scores, axis=0)
        n = jnp.where(depth == 0, jnp.concatenate(fresh, axis=0), MASKED)
        level = jnp.floor(jnp.maximum(jnp.max(s, axis=-1, keepdims=True), n))
        w = jnp.where(s > 0.5 * MASKED, jnp.exp2(s - level), 0.0).astype(BF16)
        nw = jnp.where(n > 0.5 * MASKED, jnp.exp2(n - level), 0.0).astype(BF16).astype(F32)
        total = jnp.sum(w.astype(F32), axis=-1, keepdims=True) + nw
        moves[1].wait()
        for j in range(step):
            r = begin + j
            rows = slice(j * heads, (j + 1) * heads)
            o = matmul(w[rows], side_by_side(values[r]))
            o = jnp.where(low, o[:, 0:width], o[:, width : 2 * width])
            nv = new_values[r].astype(F32)
            o = o + nw[rows] * jnp.where(low, nv[0:1], nv[1:2])
            out[row + j, 0:8, :] = o
            out[row + j, 8:16, :] = jnp.where(lane < 64, level[rows], total[rows])


def image_kernel(arrived, keys, values, out):
    groups = arrived.shape[0]
    rows = groups * 8
    images, _, patches, width = keys.shape
    scale = 1.0 / (math.sqrt(width) * math.log(2.0))
    q = arrived[:, 0:8, :].reshape(rows, width)
    code = arrived[:, 8:16, :].reshape(rows, width).astype(F32)
    within = jnp.floor(code * 0.5)
    low = lax.broadcasted_iota(jnp.int32, (rows, 1), 0) % 8 < 4
    zero = jnp.zeros_like(q)
    both = jnp.concatenate([jnp.where(low, q, zero), jnp.where(low, zero, q)], axis=1)
    level = jnp.zeros((rows, 1), F32)
    total = jnp.zeros((rows, 1), F32)
    o = jnp.zeros((rows, 2 * width), F32)
    for i in range(images):
        mine = within[:, 0:1] == float(i)
        s = matmul_t(both, side_by_side(keys[i])) * scale
        here = jnp.floor(jnp.max(s, axis=-1, keepdims=True))
        w = jnp.where(mine, jnp.exp2(s - here), 0.0).astype(BF16)
        total = total + jnp.sum(w.astype(F32), axis=-1, keepdims=True)
        level = jnp.where(mine, here, level)
        o = o + matmul(w, side_by_side(values[i]))
    o = jnp.where(low, o[:, 0:width], o[:, width : 2 * width])
    o = o / jnp.where(total > 0.0, total, 1.0)
    lane = lax.broadcasted_iota(jnp.int32, (rows, width), 1)
    level_high = level.astype(BF16).astype(F32)
    total_high = total.astype(BF16).astype(F32)
    stats = jnp.where(
        lane < 64,
        jnp.where(lane < 32, level_high, level - level_high),
        jnp.where(lane < 96, total_high, total - total_high),
    )
    second = code - 2.0 * within
    o3 = o.astype(BF16).reshape(groups, 8, width)
    for h in range(2):
        out[:, h, 0:8, :] = o3
        out[:, h, 8:16, :] = (
            jnp.where(second == float(h), stats, 0.0).astype(BF16).reshape(groups, 8, width)
        )


def merge_kernel(plan, back, own, other, states, weight_hbm, out, mine, sent, joined, weight, sems):
    half, heads, width = out.shape
    pieces = sems.shape[0]
    depth = weight.shape[0] // pieces
    moves = [
        pltpu.make_async_copy(
            weight_hbm.at[pl.ds(k * depth, depth)], weight.at[pl.ds(k * depth, depth)], sems.at[k]
        )
        for k in range(pieces)
    ]
    for move in moves:
        move.start()
    rows = half * heads
    parts = []
    for ref in (own, other):
        stats = ref[:, 8:16, :].reshape(rows, 128)
        parts.append((stats[:, 0:1], stats[:, 64:65], ref[:, 0:8, :].reshape(rows, width)))
    lane = lax.broadcasted_iota(jnp.int32, (heads, 128), 1)
    dead = jnp.where(lane < 32, MASKED, 0.0)
    for k in range(2):
        stats, values = [], []
        for j in range(half):
            source = plan[SOURCE + 2 * j + k]
            at = jnp.maximum(source, 0)
            stats.append(jnp.where(source >= 0, back[at, 8:16, :].astype(F32), dead))
            values.append(back[at, 0:8, :].astype(F32))
        stats = jnp.concatenate(stats, axis=0)
        total = stats[:, 64:65] + stats[:, 96:97]
        parts.append(
            (stats[:, 0:1] + stats[:, 32:33], total, jnp.concatenate(values, axis=0) * total)
        )
    top = functools.reduce(jnp.maximum, [p[0] for p in parts])
    factors = [jnp.exp2(p[0] - top) for p in parts]
    total = sum(f * p[1] for f, p in zip(factors, parts))
    weighted = sum(f * p[2] for f, p in zip(factors, parts))
    value = weighted / total
    out[...] = value.astype(BF16).reshape(out.shape)
    joined[...] = value
    flat = jnp.concatenate(
        [joined[pl.ds(h, half, stride=heads), :] for h in range(heads)], axis=1
    ).astype(BF16)
    row = lax.broadcasted_iota(jnp.int32, (half, 1), 0) - 2 * plan[OWN_MP]
    step = 1024
    for k, move in enumerate(moves):
        move.wait()
        lhs = flat[:, k * depth : (k + 1) * depth]
        for c in range(mine.shape[1] // step):
            at = slice(c * step, (c + 1) * step)
            if k == 0:
                before = jnp.where(row == 1, states[1:2, at], states[0:1, at]).astype(F32)
                before = jnp.where((row == 0) | (row == 1), before, 0.0)
            else:
                before = mine[:, at]
            value = before + matmul(lhs, weight[k * depth : (k + 1) * depth, at])
            mine[:, at] = value
            if k == pieces - 1:
                sent[:, at] = value.astype(BF16)


def norm_kernel(plan, mine, first, second, third, gain, rest, out):
    x = mine[...] + first[...].astype(F32) + second[...].astype(F32) + third[...].astype(F32)
    kept = x[0:2]
    for c in range(1, x.shape[0] // 2):
        kept = jnp.where(plan[OWN_MP] == c, x[2 * c : 2 * c + 2], kept)
    rest[...] = kept
    spread = jnp.mean(x * x, axis=-1, keepdims=True)
    normed = (x * lax.rsqrt(spread + NORM_EPSILON) * gain[...]).astype(BF16)
    for g in range(out.shape[0]):
        out[g] = normed


def feed_kernel(x, gate, up, down, out, lined):
    a = matmul_t(x[...], gate[...])
    b = matmul_t(x[...], up[...])
    hidden = (a / (1.0 + jnp.exp(-a)) * b).astype(BF16)
    tokens = hidden.shape[0]
    tiles = lined.shape[0]
    for q in range(4):
        at = slice(q * tiles * 128, (q + 1) * tiles * 128)
        part = matmul(hidden, down[:, at])
        for c in range(tiles):
            lined[c, pl.ds(q, tokens, stride=4), :] = part[:, c * 128 : (c + 1) * 128]
    for c in range(tiles):
        block = lined[c].astype(BF16).reshape(out.shape[0], 8, 128)
        out[:, :, c * 128 : (c + 1) * 128] = block


def last_kernel(arrived, residual, out):
    total = arrived[0].astype(F32)
    for k in range(1, arrived.shape[0]):
        total = total + arrived[k].astype(F32)
    quarter = arrived.shape[2]
    for t in range(2):
        for q in range(4):
            at = slice(q * quarter, (q + 1) * quarter)
            row = t * 4 + q
            out[t : t + 1, at] = (residual[t : t + 1, at] + total[row : row + 1]).astype(BF16)


def on_device(
    states,
    queries,
    new_keys,
    new_values,
    text_keys,
    text_values,
    text_length,
    image_keys,
    image_values,
    image_slot,
    block_list,
    block_count,
    image_first,
    image_count,
    out_weight,
    norm_gain,
    gate_weight,
    up_weight,
    down_weight,
):
    groups = lax.axis_size("group")
    depths = lax.axis_size("depth")
    ring = lax.axis_size("mp")
    requests, heads, width = queries.shape
    half = requests // depths
    features = states.shape[1]

    integers = (image_slot, block_list, block_count, image_first, image_count, text_length)
    in_place = [in_hbm(x) for x in (*integers, queries)]
    routed, plan = call(
        route_kernel,
        (
            jax.ShapeDtypeStruct((groups, 16, width), BF16),
            jax.ShapeDtypeStruct((SOURCE + requests,), jnp.int32),
        ),
        [HBM] * 7,
        10_000_000_000,
        100_000,
        "route",
        scratch=[pltpu.SMEM(i.shape, jnp.int32) for i in integers]
        + [pltpu.VMEM(queries.shape, BF16), pltpu.SemaphoreType.DMA((len(in_place),))],
        out_specs=(VMEM, SMEM),
    )(*in_place)
    arrived = lax.all_to_all(routed, "group", 0, 0, tiled=True)

    part = jax.ShapeDtypeStruct((half, 16, width), F32)
    own, other = call(
        text_kernel,
        (part, part),
        [SMEM] + [VMEM] * 3 + [HBM] * 2,
        200_000_000,
        4_400_000,
        "text",
        scratch=[pltpu.VMEM(text_keys.shape, BF16), pltpu.VMEM(text_values.shape, BF16)]
        + [pltpu.SemaphoreType.DMA((2, 4))],
    )(plan, queries, new_keys, new_values, in_hbm(text_keys), in_hbm(text_values))
    other = lax.ppermute(other, "depth", [(0, 1), (1, 0)])

    back = call(
        image_kernel,
        jax.ShapeDtypeStruct((groups, depths, 16, width), BF16),
        [VMEM] * 3,
        600_000_000,
        5_000_000,
        "image",
    )(arrived, image_keys, image_values)
    back = lax.all_to_all(
        back.reshape(groups * depths, 16, width), ("group", "depth"), 0, 0, tiled=True
    )
    attention, mine, sent = call(
        merge_kernel,
        (
            jax.ShapeDtypeStruct((half, heads, width), BF16),
            jax.ShapeDtypeStruct((half, features), F32),
            jax.ShapeDtypeStruct((half, features), BF16),
        ),
        [SMEM] + [VMEM] * 4 + [HBM],
        100_000_000,
        8_800_000,
        "merge",
        scratch=[
            pltpu.VMEM((half * heads, width), F32),
            pltpu.VMEM(out_weight.shape, BF16),
            pltpu.SemaphoreType.DMA((4,)),
        ],
    )(plan, back, own, other, states, in_hbm(out_weight))
    passed = [
        lax.ppermute(sent, "mp", [(i, i ^ k) for i in range(ring)]) for k in range(1, ring)
    ]
    rest, normed = call(
        norm_kernel,
        (
            jax.ShapeDtypeStruct((2, features), F32),
            jax.ShapeDtypeStruct((groups, half, features), BF16),
        ),
        [SMEM] + [VMEM] * 5,
        10_000_000_000,
        1_600_000,
        "norm",
    )(plan, mine, *passed, norm_gain.reshape(1, features))
    tokens = lax.all_to_all(normed, "group", 0, 0, tiled=True).reshape(groups * half, features)
    peers = groups * ring
    down = call(
        feed_kernel,
        jax.ShapeDtypeStruct((peers, 8, features // 4), BF16),
        [VMEM] * 4,
        1_400_000_000,
        7_000_000,
        "feed",
        scratch=[pltpu.VMEM((features // 512, groups * half * 4, 128), F32)],
    )(tokens, gate_weight.T, up_weight.T, down_weight)
    gathered = lax.all_to_all(down, ("group", "mp"), 0, 0, tiled=True)
    layer_out = call(
        last_kernel,
        jax.ShapeDtypeStruct((2, features), BF16),
        [VMEM] * 2,
        0,
        1_300_000,
        "last",
    )(gathered, rest)
    return attention, layer_out


def solution(mesh):
    placed = (
        P(("group", "depth", "mp"), None),
        P("group", "mp", None),
        P("group", "mp", None),
        P("group", "mp", None),
        P("group", "mp", "depth", None),
        P("group", "mp", "depth", None),
        P("group"),
        P("group", "mp", None, None),
        P("group", "mp", None, None),
        P(),
        P(),
        P(),
        P("group"),
        P("group"),
        P("mp", None),
        P(),
        P(None, ("group", "mp")),
        P(None, ("group", "mp")),
        P(("group", "mp"), None),
    )
    return jax.shard_map(
        on_device,
        mesh=mesh,
        in_specs=placed,
        out_specs=(P(("group", "depth"), "mp", None), P(("group", "depth", "mp"), None)),
        check_vma=False,
    )
```

time: 104 us -> 93.8 us (0.902)
  local copies, waits for them, and re-layouts: 7.28 us -> 0.05 us
  Pallas kernels: 11.3 us -> 18 us
  blocking collectives: 52.5 us -> 57.3 us
  matrix products: 4.74 us -> 0 us
  starting transfers between devices: 13.9 us -> 9.16 us
  waiting for transfers between devices: 12.7 us -> 8.22 us
    pallas_call x6, Pallas kernels: 7.02 us -> 14.6 us  [the longest x1 4.71 us: on_device(): call(merge_kernel, (jax.ShapeDtypeStruct((half, heads, width), BF16), jax...]
    unnamed x26 -> x20, local copies, waits for them, and re-layouts: 5.71 us -> 0.05 us
    ppermute x3 -> x0, starting transfers between devices: 4.78 us -> none  [on_device(): lax.ppermute(s, 'mp', [(i, i ^ k) for i in range(ring)])]
    dot_general x1 -> x0, matrix products: 4.74 us -> none  [on_device(): jnp.dot(attention.reshape(half, heads * width), out_weight, preferred_ele...]
    all_to_all x1, blocking collectives: 17.9 us -> 21.4 us  [on_device(): gathered = lax.all_to_all(down, ('group', 'mp'), 0, 0, tiled=True)]
    ppermute x3 -> x0, waiting for transfers between devices: 3.54 us -> none  [on_device(): lax.ppermute(s, 'mp', [(i, i ^ k) for i in range(ring)])]
    all_to_all x1, blocking collectives: 20.1 us -> 21.3 us  [on_device(): lax.all_to_all(normed, 'group', 0, 0, tiled=True)]
  transfers between devices with their start and end apart: 8 -> 5, of which waited for: 6 -> 4; matrix products, arithmetic and copies ran while one was open for 0% -> 0% of each run, Pallas kernels for 2% -> 5%
where the time goes in v2:
time: 93.8 us; the launch traced here: 93.5 us
  blocking collectives  57.3 us (61%)
  Pallas kernels  18 us (19%)
  starting transfers between devices  9.16 us (10%)
  waiting for transfers between devices  8.22 us (9%)
    all_to_all x1, blocking collectives, on_device(): gathered = lax.all_to_all(down, ('group', 'mp'), 0, 0, tiled=True)  21.4 us
    all_to_all x1, blocking collectives, on_device(): lax.all_to_all(normed, 'group', 0, 0, tiled=True)  21.3 us
    all_to_all x1, blocking collectives, on_device(): arrived = lax.all_to_all(routed, 'group', 0, 0, tiled=True)  14.6 us
    ppermute x3, waiting for transfers between devices, on_device(): lax.ppermute(sent, 'mp', [(i, i ^ k) for i in range(ring)])  5.08 us
    ppermute x3, starting transfers between devices, on_device(): lax.ppermute(sent, 'mp', [(i, i ^ k) for i in range(ring)])  5.07 us
    pallas_call x1, Pallas kernels, on_device(): call(merge_kernel, (jax.ShapeDtypeStruct((half, heads, width), BF16), jax...  4.71 us
    pallas_call x1, Pallas kernels, on_device(): call(text_kernel, (part, part), [SMEM] + [VMEM] * 3 + [HBM] * 2, 20000000...  4.37 us
    all_to_all x1, starting transfers between devices, on_device(): lax.all_to_all(back.reshape(groups * depths, 16, width), ('group', 'depth...  3.85 us
  transfers between devices with their start and end apart: 5, of which 4 were waited for; matrix products, arithmetic and copies ran while one was open for 0% of the time, Pallas kernels for 5%

profile of v2, /device:TPU:0, one launch (start us, length us, event | category | flops | bytes accessed | tf_op | source)
XLA Modules:
  0.0 93.5 jit_solution(5149351449081490079)
XLA Ops:
  0.6 0.0 copy-start.1
  0.6 0.0 copy-start
  0.7 2.0 %route.1 = (bf16[16,16,128]{2,1,0:T(8,128)(2,1)S(1)}, s32[40]{0:T(128)S(1)}) custom-call(s32[128]{0:T(128)} %slots_hbm.1, s32[16,32]{1,0:T(8,128)} %blocks_hbm.1, s32[16]{0:T(128)} %count_hbm.1, s32[16]{0:T(128)} %first_hbm.1, s32[16]{0:T(128)} %images_hbm.1, s32[16]{0:T(128)} %lengths_hbm.1, bf16[16,8,128]{2,1,0:T(8,128)(2,1)} %queries.1), custom_call_target="tpu_custom_call" | custom-call | flops 10000000000 | bytes 100000 | tf_op jit(solution)/shard_map/route/pallas_call | solution.py:333
  2.7 14.6 %all_to_all.20.arrived = bf16[16,16,128]{2,1,0:T(8,128)(2,1)S(1)} all-to-all(bf16[16,16,128]{2,1,0:T(8,128)(2,1)S(1)} %get-tuple-element.12), channel_id=1, replica_groups=mesh['group'=16,'depth'=2,'mp'=4] {'group'}, dimensions={0} | all-to-all | bytes 131072 | tf_op jit(solution)/shard_map/all_to_all | solution.py:347
  17.2 0.0 copy-done.1
  17.2 0.0 copy-done
  17.2 0.0 copy-start.5
  17.3 0.0 copy-start.7
  17.3 0.0 copy-start.8
  17.3 3.4 %image.1 = bf16[16,2,16,128]{3,2,1,0:T(8,128)(2,1)} custom-call(bf16[16,16,128]{2,1,0:T(8,128)(2,1)S(1)} %all_to_all.20.arrived, bf16[8,2,576,128]{3,2,1,0:T(8,128)(2,1)S(1)} %copy-done, bf16[8,2,576,128]{3,2,1,0:T(8,128)(2,1)S(1)} %copy-done.1), custom_call_target="tpu_custom_call" | custom-call | flops 600000000 | bytes 5000000 | tf_op jit(solution)/shard_map/image/pallas_call | solution.py:362
  20.7 3.8 %all-to-all-start.1 = ((bf16[32,16,128]{2,1,0:T(8,128)(2,1)}), bf16[32,16,128]{2,1,0:T(8,128)(2,1)S(1)}, u32[]{:S(2)}, u32[]{:S(2)}) async-start(bf16[32,16,128]{2,1,0:T(8,128)(2,1)} %bitcast), calls=%async_computation.1 | async-start | bytes 262144 | tf_op jit(solution)/shard_map/all_to_all | solution.py:370
  24.5 0.0 copy-done.5
  24.6 0.0 copy-done.7
  24.6 0.0 copy-done.8
  24.6 0.0 copy-start.6
  24.6 4.4 %text.1 = (f32[8,16,128]{2,1,0:T(8,128)S(1)}, f32[8,16,128]{2,1,0:T(8,128)S(1)}) custom-call(s32[40]{0:T(128)S(1)} %get-tuple-element.11.plan, bf16[16,8,128]{2,1,0:T(8,128)(2,1)S(1)} %copy-done.5, bf16[16,2,128]{2,1,0:T(2,128)(2,1)S(1)} %copy-done.7, bf16[16,2,128]{2,1,0:T(2,128)(2,1)S(1)} %copy-done.8, bf16[16,2,256,128]{3,2,1,0:T(8,128)(2,1)} %keys_hbm.1, ...), custom_call_target="tpu_custom_call" | custom-call | flops 200000000 | bytes 4400000 | tf_op jit(solution)/shard_map/text/pallas_call | solution.py:350
  29.0 0.2 collective-permute-start
  29.2 1.1 %collective-permute-done.other = f32[8,16,128]{2,1,0:T(8,128)S(1)} collective-permute-done((f32[8,16,128]{2,1,0:T(8,128)S(1)}, f32[8,16,128]{2,1,0:T(8,128)S(1)}, u32[]{:S(2)}, u32[]{:S(2)}) %collective-permute-start) | collective-permute-done | bytes 65568 | tf_op jit(solution)/shard_map/ppermute | solution.py:360
  30.3 2.0 %all-to-all-done.1.back = bf16[32,16,128]{2,1,0:T(8,128)(2,1)S(1)} async-done(((bf16[32,16,128]{2,1,0:T(8,128)(2,1)}), bf16[32,16,128]{2,1,0:T(8,128)(2,1)S(1)}, u32[]{:S(2)}, u32[]{:S(2)}) %all-to-all-start.1) | async-done | bytes 131104 | tf_op jit(solution)/shard_map/all_to_all | solution.py:370
  32.3 0.0 copy-done.6
  32.3 0.0 copy-start.9
  32.3 4.7 %merge.1 = (bf16[8,8,128]{2,1,0:T(8,128)(2,1)}, f32[8,4096]{1,0:T(8,128)S(1)}, bf16[8,4096]{1,0:T(8,128)(2,1)S(1)}) custom-call(s32[40]{0:T(128)S(1)} %get-tuple-element.11.plan, bf16[32,16,128]{2,1,0:T(8,128)(2,1)S(1)} %all-to-all-done.1.back, f32[8,16,128]{2,1,0:T(8,128)S(1)} %get-tuple-element.13.own, f32[8,16,128]{2,1,0:T(8,128)S(1)} %collective-permute-done.other, ...), custom_call_target="tpu_custom_call" | custom-call | flops 100000000 | bytes 8800000 | tf_op jit(solution)/shard_map/merge/pallas_call | solution.py:373
  37.1 4.1 %collective-permute-start.3 = (bf16[8,4096]{1,0:T(8,128)(2,1)S(1)}, bf16[8,4096]{1,0:T(8,128)(2,1)S(1)}, u32[]{:S(2)}, u32[]{:S(2)}) collective-permute-start(bf16[8,4096]{1,0:T(8,128)(2,1)S(1)} %get-tuple-element.17), channel_id=1, source_target_pairs={{0,3},{1,2},{2,1},{3,0},{4,7},{5,6},{6,5},{7,4},{8,11},{9,10},{10,... | collective-permute-start | bytes 196616 | tf_op jit(solution)/shard_map/ppermute | solution.py:391
  41.2 0.0 collective-permute-start.2
  41.2 0.9 %collective-permute-start.1 = (bf16[8,4096]{1,0:T(8,128)(2,1)S(1)}, bf16[8,4096]{1,0:T(8,128)(2,1)S(1)}, u32[]{:S(2)}, u32[]{:S(2)}) collective-permute-start(bf16[8,4096]{1,0:T(8,128)(2,1)S(1)} %get-tuple-element.17), channel_id=1, source_target_pairs={{0,1},{1,0},{2,3},{3,2},{4,5},{5,4},{6,7},{7,6},{8,9},{9,8},{10,11... | collective-permute-start | bytes 196616 | tf_op jit(solution)/shard_map/ppermute | solution.py:391
  42.1 2.1 %collective-permute-done.3.third = bf16[8,4096]{1,0:T(8,128)(2,1)S(1)} collective-permute-done((bf16[8,4096]{1,0:T(8,128)(2,1)S(1)}, bf16[8,4096]{1,0:T(8,128)(2,1)S(1)}, u32[]{:S(2)}, u32[]{:S(2)}) %collective-permute-start.3) | collective-permute-done | bytes 65568 | tf_op jit(solution)/shard_map/ppermute | solution.py:391
  44.2 3.0 %collective-permute-done.2.second = bf16[8,4096]{1,0:T(8,128)(2,1)S(1)} collective-permute-done((bf16[8,4096]{1,0:T(8,128)(2,1)S(1)}, bf16[8,4096]{1,0:T(8,128)(2,1)S(1)}, u32[]{:S(2)}, u32[]{:S(2)}) %collective-permute-start.2) | collective-permute-done | bytes 65568 | tf_op jit(solution)/shard_map/ppermute | solution.py:391
  47.2 0.0 collective-permute-done.1.first
  47.2 0.0 copy-done.9
  47.2 0.0 copy-start.3
  47.2 0.0 copy-start.4
  47.2 0.8 norm.1
  48.0 0.0 copy-start.2
  48.0 21.3 %all_to_all.21 = bf16[16,8,4096]{2,1,0:T(8,128)(2,1)S(1)} all-to-all(bf16[16,8,4096]{2,1,0:T(8,128)(2,1)S(1)} %get-tuple-element.18), channel_id=1, replica_groups=mesh['group'=16,'depth'=2,'mp'=4] {'group'}, dimensions={0} | all-to-all | bytes 2097152 | tf_op jit(solution)/shard_map/all_to_all | solution.py:404
  69.4 0.0 copy-done.3
  69.4 0.0 copy-done.4
  69.4 0.0 copy-done.2
  69.4 1.9 %feed.1 = bf16[64,8,1024]{2,1,0:T(8,128)(2,1)S(1)} custom-call(bf16[128,4096]{1,0:T(8,128)(2,1)S(1)} %bitcast.5, bf16[224,4096]{1,0:T(8,128)(2,1)S(1)} %bitcast.6, bf16[224,4096]{1,0:T(8,128)(2,1)S(1)} %bitcast.7, bf16[224,4096]{1,0:T(8,128)(2,1)S(1)} %copy-done.4), custom_call_target="tpu_custom_call" | custom-call | flops 1400000000 | bytes 7000000 | tf_op jit(solution)/shard_map/feed/pallas_call | solution.py:406
  71.3 21.4 %all_to_all.22.arrived = bf16[64,8,1024]{2,1,0:T(8,128)(2,1)S(1)} all-to-all(bf16[64,8,1024]{2,1,0:T(8,128)(2,1)S(1)} %feed.1), channel_id=1, replica_groups=mesh['group'=16,'depth'=2,'mp'=4] {'group','mp'}, dimensions={0} | all-to-all | bytes 2097152 | tf_op jit(solution)/shard_map/all_to_all | solution.py:415
  92.8 0.8 last.1
Async XLA Ops:
  0.6 16.6 %copy-start.1 = (bf16[8,2,576,128]{3,2,1,0:T(8,128)(2,1)S(1)}, bf16[8,2,576,128]{3,2,1,0:T(8,128)(2,1)}, u32[]{:S(2)}) copy-start(bf16[8,2,576,128]{3,2,1,0:T(8,128)(2,1)} %values.1) | copy-start | bytes 7077892
  0.6 16.6 %copy-start = (bf16[8,2,576,128]{3,2,1,0:T(8,128)(2,1)S(1)}, bf16[8,2,576,128]{3,2,1,0:T(8,128)(2,1)}, u32[]{:S(2)}) copy-start(bf16[8,2,576,128]{3,2,1,0:T(8,128)(2,1)} %keys.1) | copy-start | bytes 7077892
  17.2 7.3 %copy-start.5 = (bf16[16,8,128]{2,1,0:T(8,128)(2,1)S(1)}, bf16[16,8,128]{2,1,0:T(8,128)(2,1)}, u32[]{:S(2)}) copy-start(bf16[16,8,128]{2,1,0:T(8,128)(2,1)} %queries.1) | copy-start | bytes 98308
  17.3 7.3 %copy-start.7 = (bf16[16,2,128]{2,1,0:T(2,128)(2,1)S(1)}, bf16[16,2,128]{2,1,0:T(2,128)(2,1)}, u32[]{:S(2)}) copy-start(bf16[16,2,128]{2,1,0:T(2,128)(2,1)} %new_keys.1) | copy-start | bytes 24580
  17.3 7.3 %copy-start.8 = (bf16[16,2,128]{2,1,0:T(2,128)(2,1)S(1)}, bf16[16,2,128]{2,1,0:T(2,128)(2,1)}, u32[]{:S(2)}) copy-start(bf16[16,2,128]{2,1,0:T(2,128)(2,1)} %new_values.1) | copy-start | bytes 24580
  20.7 11.7 %all-to-all-start.1 = ((bf16[32,16,128]{2,1,0:T(8,128)(2,1)}), bf16[32,16,128]{2,1,0:T(8,128)(2,1)S(1)}, u32[]{:S(2)}, u32[]{:S(2)}) async-start(bf16[32,16,128]{2,1,0:T(8,128)(2,1)} %bitcast), calls=%async_computation.1 | async-start | bytes 262144 | tf_op jit(solution)/shard_map/all_to_all | solution.py:370
  24.6 7.8 %copy-start.6 = (bf16[2,4096]{1,0:T(2,128)(2,1)S(1)}, bf16[2,4096]{1,0:T(2,128)(2,1)}, u32[]{:S(2)}) copy-start(bf16[2,4096]{1,0:T(2,128)(2,1)} %states.1) | copy-start | bytes 49156
  29.0 1.3 %collective-permute-start = (f32[8,16,128]{2,1,0:T(8,128)S(1)}, f32[8,16,128]{2,1,0:T(8,128)S(1)}, u32[]{:S(2)}, u32[]{:S(2)}) collective-permute-start(f32[8,16,128]{2,1,0:T(8,128)S(1)} %get-tuple-element.14), channel_id=1, source_target_pairs={{0,4},{4,0},{1,5},{5,1},{2,6},{6,2},{3,7},{7,3},{8,12},{12,8},{9,1... | collective-permute-start | bytes 196616 | tf_op jit(solution)/shard_map/ppermute | solution.py:360
  32.3 14.9 %copy-start.9 = (f32[4096]{0:T(1024)S(1)}, f32[4096]{0:T(1024)}, u32[]{:S(2)}) copy-start(f32[4096]{0:T(1024)} %param.34) | copy-start | bytes 49156
  37.1 7.2 %collective-permute-start.3 = (bf16[8,4096]{1,0:T(8,128)(2,1)S(1)}, bf16[8,4096]{1,0:T(8,128)(2,1)S(1)}, u32[]{:S(2)}, u32[]{:S(2)}) collective-permute-start(bf16[8,4096]{1,0:T(8,128)(2,1)S(1)} %get-tuple-element.17), channel_id=1, source_target_pairs={{0,3},{1,2},{2,1},{3,0},{4,7},{5,6},{6,5},{7,4},{8,11},{9,10},{10,... | collective-permute-start | bytes 196616 | tf_op jit(solution)/shard_map/ppermute | solution.py:391
  41.2 6.0 %collective-permute-start.2 = (bf16[8,4096]{1,0:T(8,128)(2,1)S(1)}, bf16[8,4096]{1,0:T(8,128)(2,1)S(1)}, u32[]{:S(2)}, u32[]{:S(2)}) collective-permute-start(bf16[8,4096]{1,0:T(8,128)(2,1)S(1)} %get-tuple-element.17), channel_id=1, source_target_pairs={{0,2},{1,3},{2,0},{3,1},{4,6},{5,7},{6,4},{7,5},{8,10},{9,11},{10,... | collective-permute-start | bytes 196616 | tf_op jit(solution)/shard_map/ppermute | solution.py:391
  41.2 6.0 %collective-permute-start.1 = (bf16[8,4096]{1,0:T(8,128)(2,1)S(1)}, bf16[8,4096]{1,0:T(8,128)(2,1)S(1)}, u32[]{:S(2)}, u32[]{:S(2)}) collective-permute-start(bf16[8,4096]{1,0:T(8,128)(2,1)S(1)} %get-tuple-element.17), channel_id=1, source_target_pairs={{0,1},{1,0},{2,3},{3,2},{4,5},{5,4},{6,7},{7,6},{8,9},{9,8},{10,11... | collective-permute-start | bytes 196616 | tf_op jit(solution)/shard_map/ppermute | solution.py:391
  47.2 22.1 %copy-start.3 = (bf16[4096,224]{0,1:T(8,128)(2,1)S(1)}, bf16[4096,224]{0,1:T(8,128)(2,1)}, u32[]{:S(2)}) copy-start(bf16[4096,224]{0,1:T(8,128)(2,1)} %param.36) | copy-start | bytes 5505028
  47.2 22.1 %copy-start.4 = (bf16[224,4096]{1,0:T(8,128)(2,1)S(1)}, bf16[224,4096]{1,0:T(8,128)(2,1)}, u32[]{:S(2)}) copy-start(bf16[224,4096]{1,0:T(8,128)(2,1)} %down.1) | copy-start | bytes 5505028
  48.0 21.3 %copy-start.2 = (bf16[4096,224]{0,1:T(8,128)(2,1)S(1)}, bf16[4096,224]{0,1:T(8,128)(2,1)}, u32[]{:S(2)}) copy-start(bf16[4096,224]{0,1:T(8,128)(2,1)} %param.35) | copy-start | bytes 5505028

commit v3 on v2

--- a/solution.py
+++ b/solution.py
@@ -107,30 +107,20 @@
     return jnp.concatenate([pair[0], pair[1]], axis=1)
 
 
-def text_kernel(plan, queries, new_keys, new_values, keys_hbm, values_hbm, own, other, keys, values, sems):
+def text_kernel(plan, queries, new_keys, new_values, keys, values, own, other):
     depth = plan[OWN_DEPTH]
     requests, heads, width = queries.shape
     half = requests // 2
     span = keys.shape[2]
     step = requests // 4
     scale = 1.0 / (math.sqrt(width) * math.log(2.0))
-    chunks = []
-    for c in range(4):
-        part, out = (depth, own) if c < 2 else (1 - depth, other)
-        begin = part * half + (c % 2) * step
-        at = pl.ds(begin, step)
-        moves = [
-            pltpu.make_async_copy(src.at[at], dst.at[at], sems.at[k, c])
-            for k, (src, dst) in enumerate(((keys_hbm, keys), (values_hbm, values)))
-        ]
-        for move in moves:
-            move.start()
-        chunks.append((begin, (c % 2) * step, out, moves))
     low = lax.broadcasted_iota(jnp.int32, (heads, 1), 0) < heads // 2
     lane = lax.broadcasted_iota(jnp.int32, (heads, 128), 1)
     where = depth * span + lax.broadcasted_iota(jnp.int32, (heads, span), 1)
-    for begin, row, out, moves in chunks:
-        moves[0].wait()
+    for c in range(4):
+        part, out = (1 - depth, other) if c < 2 else (depth, own)
+        row = (c % 2) * step
+        begin = part * half + row
         scores, fresh = [], []
         for j in range(step):
             r = begin + j
@@ -148,7 +138,6 @@
         w = jnp.where(s > 0.5 * MASKED, jnp.exp2(s - level), 0.0).astype(BF16)
         nw = jnp.where(n > 0.5 * MASKED, jnp.exp2(n - level), 0.0).astype(BF16).astype(F32)
         total = jnp.sum(w.astype(F32), axis=-1, keepdims=True) + nw
-        moves[1].wait()
         for j in range(step):
             r = begin + j
             rows = slice(j * heads, (j + 1) * heads)
@@ -160,7 +149,8 @@
             out[row + j, 8:16, :] = jnp.where(lane < 64, level[rows], total[rows])
 
 
-def image_kernel(arrived, keys, values, out):
+def image_kernel(after, arrived, keys, values, out):
+    del after
     groups = arrived.shape[0]
     rows = groups * 8
     images, _, patches, width = keys.shape
@@ -201,18 +191,8 @@
         )
 
 
-def merge_kernel(plan, back, own, other, states, weight_hbm, out, mine, sent, joined, weight, sems):
+def merge_kernel(plan, back, own, other, states, weight, out, mine, sent, joined):
     half, heads, width = out.shape
-    pieces = sems.shape[0]
-    depth = weight.shape[0] // pieces
-    moves = [
-        pltpu.make_async_copy(
-            weight_hbm.at[pl.ds(k * depth, depth)], weight.at[pl.ds(k * depth, depth)], sems.at[k]
-        )
-        for k in range(pieces)
-    ]
-    for move in moves:
-        move.start()
     rows = half * heads
     parts = []
     for ref in (own, other):
@@ -243,21 +223,14 @@
         [joined[pl.ds(h, half, stride=heads), :] for h in range(heads)], axis=1
     ).astype(BF16)
     row = lax.broadcasted_iota(jnp.int32, (half, 1), 0) - 2 * plan[OWN_MP]
-    step = 1024
-    for k, move in enumerate(moves):
-        move.wait()
-        lhs = flat[:, k * depth : (k + 1) * depth]
-        for c in range(mine.shape[1] // step):
-            at = slice(c * step, (c + 1) * step)
-            if k == 0:
-                before = jnp.where(row == 1, states[1:2, at], states[0:1, at]).astype(F32)
-                before = jnp.where((row == 0) | (row == 1), before, 0.0)
-            else:
-                before = mine[:, at]
-            value = before + matmul(lhs, weight[k * depth : (k + 1) * depth, at])
-            mine[:, at] = value
-            if k == pieces - 1:
-                sent[:, at] = value.astype(BF16)
+    step = 512
+    for c in range(mine.shape[1] // step):
+        at = slice(c * step, (c + 1) * step)
+        before = jnp.where(row == 1, states[1:2, at], states[0:1, at]).astype(F32)
+        before = jnp.where((row == 0) | (row == 1), before, 0.0)
+        value = before + matmul(flat, weight[:, at])
+        mine[:, at] = value
+        sent[:, at] = value.astype(BF16)
 
 
 def norm_kernel(plan, mine, first, second, third, gain, rest, out):
@@ -337,7 +310,7 @@
             jax.ShapeDtypeStruct((SOURCE + requests,), jnp.int32),
         ),
         [HBM] * 7,
-        10_000_000_000,
+        20_000_000_000,
         100_000,
         "route",
         scratch=[pltpu.SMEM(i.shape, jnp.int32) for i in integers]
@@ -345,28 +318,28 @@
         out_specs=(VMEM, SMEM),
     )(*in_place)
     arrived = lax.all_to_all(routed, "group", 0, 0, tiled=True)
+    arrived, plan = lax.optimization_barrier((arrived, plan))
 
     part = jax.ShapeDtypeStruct((half, 16, width), F32)
     own, other = call(
         text_kernel,
         (part, part),
-        [SMEM] + [VMEM] * 3 + [HBM] * 2,
+        [SMEM] + [VMEM] * 5,
         200_000_000,
         4_400_000,
         "text",
-        scratch=[pltpu.VMEM(text_keys.shape, BF16), pltpu.VMEM(text_values.shape, BF16)]
-        + [pltpu.SemaphoreType.DMA((2, 4))],
-    )(plan, queries, new_keys, new_values, in_hbm(text_keys), in_hbm(text_values))
+    )(plan, queries, new_keys, new_values, text_keys, text_values)
     other = lax.ppermute(other, "depth", [(0, 1), (1, 0)])
 
     back = call(
         image_kernel,
         jax.ShapeDtypeStruct((groups, depths, 16, width), BF16),
-        [VMEM] * 3,
-        600_000_000,
+        [VMEM] * 4,
+        10_000_000_000,
         5_000_000,
         "image",
-    )(arrived, image_keys, image_values)
+    )(own, arrived, image_keys, image_values)
+    back, other = lax.optimization_barrier((back, other))
     back = lax.all_to_all(
         back.reshape(groups * depths, 16, width), ("group", "depth"), 0, 0, tiled=True
     )
@@ -377,16 +350,12 @@
             jax.ShapeDtypeStruct((half, features), F32),
             jax.ShapeDtypeStruct((half, features), BF16),
         ),
-        [SMEM] + [VMEM] * 4 + [HBM],
+        [SMEM] + [VMEM] * 5,
         100_000_000,
         8_800_000,
         "merge",
-        scratch=[
-            pltpu.VMEM((half * heads, width), F32),
-            pltpu.VMEM(out_weight.shape, BF16),
-            pltpu.SemaphoreType.DMA((4,)),
-        ],
-    )(plan, back, own, other, states, in_hbm(out_weight))
+        scratch=[pltpu.VMEM((half * heads, width), F32)],
+    )(plan, back, own, other, states, out_weight)
     passed = [
         lax.ppermute(sent, "mp", [(i, i ^ k) for i in range(ring)]) for k in range(1, ring)
     ]

time: 93.8 us -> 90.7 us (0.967)
  blocking collectives: 57.3 us -> 66.7 us
  Pallas kernels: 18 us -> 12.7 us
  starting transfers between devices: 9.16 us -> 5.13 us
  waiting for transfers between devices: 8.22 us -> 5.08 us
    all_to_all x0 -> x1, blocking collectives: none -> 11.3 us  [on_device(): lax.all_to_all(back.reshape(groups * depths, 16, width), ('group', 'depth...]
    all_to_all x1 -> x0, starting transfers between devices: 3.85 us -> none  [on_device(): lax.all_to_all(back.reshape(groups * depths, 16, width), ('group', 'depth...]
    pallas_call x1, Pallas kernels: 4.71 us -> 1.98 us  [on_device(): call(merge_kernel, (jax.ShapeDtypeStruct((half, heads, width), BF16), jax...]
    all_to_all x1 -> x0, waiting for transfers between devices: 2.05 us -> none  [on_device(): lax.all_to_all(back.reshape(groups * depths, 16, width), ('group', 'depth...]
    pallas_call x1, Pallas kernels: 4.37 us -> 2.39 us  [on_device(): call(text_kernel, (part, part), [SMEM] + [VMEM] * 5, 200000000, 4400000,...]
    all_to_all x1, blocking collectives: 21.3 us -> 19.5 us  [on_device(): lax.all_to_all(normed, 'group', 0, 0, tiled=True)]
    ppermute x1, waiting for transfers between devices: 1.09 us -> 0.01 us  [on_device(): other = lax.ppermute(other, 'depth', [(0, 1), (1, 0)])]
  transfers between devices with their start and end apart: 5 -> 4, of which waited for: 4 -> 2; matrix products, arithmetic and copies ran while one was open for 0% -> 0% of each run, Pallas kernels for 5% -> 3%
where the time goes in v3:
time: 90.7 us; the launch traced here: 90.5 us
  blocking collectives  66.7 us (74%)
  Pallas kernels  12.7 us (14%)
  starting transfers between devices  5.13 us (6%)
  waiting for transfers between devices  5.08 us (6%)
    all_to_all x1, blocking collectives, on_device(): gathered = lax.all_to_all(down, ('group', 'mp'), 0, 0, tiled=True)  21.3 us
    all_to_all x1, blocking collectives, on_device(): lax.all_to_all(normed, 'group', 0, 0, tiled=True)  19.5 us
    all_to_all x1, blocking collectives, on_device(): arrived = lax.all_to_all(routed, 'group', 0, 0, tiled=True)  14.6 us
    all_to_all x1, blocking collectives, on_device(): lax.all_to_all(back.reshape(groups * depths, 16, width), ('group', 'depth...  11.3 us
    ppermute x3, waiting for transfers between devices, on_device(): lax.ppermute(sent, 'mp', [(i, i ^ k) for i in range(ring)])  5.08 us
    ppermute x3, starting transfers between devices, on_device(): lax.ppermute(sent, 'mp', [(i, i ^ k) for i in range(ring)])  5.05 us
    pallas_call x1, Pallas kernels, on_device(): call(image_kernel, jax.ShapeDtypeStruct((groups, depths, 16, width), BF16...  2.78 us
    pallas_call x1, Pallas kernels, on_device(): call(text_kernel, (part, part), [SMEM] + [VMEM] * 5, 200000000, 4400000,...  2.39 us
  transfers between devices with their start and end apart: 4, of which 2 were waited for; matrix products, arithmetic and copies ran while one was open for 0% of the time, Pallas kernels for 3%

profile of v3, /device:TPU:0, one launch (start us, length us, event | category | flops | bytes accessed | tf_op | source)
XLA Modules:
  0.0 90.5 jit_solution(2632624459046577768)
XLA Ops:
  0.6 0.0 copy-start.5
  0.6 0.0 copy-start.1
  0.7 0.0 copy-start
  0.7 0.0 copy-start.8
  0.7 0.0 copy-start.7
  0.7 0.0 copy-start.10
  0.7 2.0 %route.1 = (bf16[16,16,128]{2,1,0:T(8,128)(2,1)S(1)}, s32[40]{0:T(128)S(1)}) custom-call(s32[128]{0:T(128)} %slots_hbm.1, s32[16,32]{1,0:T(8,128)} %blocks_hbm.1, s32[16]{0:T(128)} %count_hbm.1, s32[16]{0:T(128)} %first_hbm.1, s32[16]{0:T(128)} %images_hbm.1, s32[16]{0:T(128)} %lengths_hbm.1, bf16[16,8,128]{2,1,0:T(8,128)(2,1)} %queries.1), custom_call_target="tpu_custom_call" | custom-call | flops 20000000000 | bytes 100000 | tf_op jit(solution)/shard_map/route/pallas_call | solution.py:306
  2.7 14.6 %all_to_all.20.arrived = bf16[16,16,128]{2,1,0:T(8,128)(2,1)S(1)} all-to-all(bf16[16,16,128]{2,1,0:T(8,128)(2,1)S(1)} %get-tuple-element.15), channel_id=1, replica_groups=mesh['group'=16,'depth'=2,'mp'=4] {'group'}, dimensions={0} | all-to-all | bytes 131072 | tf_op jit(solution)/shard_map/all_to_all | solution.py:320
  17.3 0.0 copy-done.5
  17.3 0.0 copy-done.1
  17.3 0.0 copy-done
  17.3 0.0 copy-done.8
  17.3 0.0 copy-done.7
  17.3 0.0 copy-start.9
  17.3 2.4 %text.1 = (f32[8,16,128]{2,1,0:T(8,128)S(1)}, f32[8,16,128]{2,1,0:T(8,128)S(1)}) custom-call(s32[40]{0:T(128)S(1)} %get-tuple-element.17.plan, bf16[16,8,128]{2,1,0:T(8,128)(2,1)S(1)} %copy-done.5, bf16[16,2,128]{2,1,0:T(2,128)(2,1)S(1)} %copy-done.7, bf16[16,2,128]{2,1,0:T(2,128)(2,1)S(1)} %copy-done.8, bf16[16,2,256,128]{3,2,1,0:T(8,128)(2,1)S(1)} %copy-done, ...), custom_call_target="tpu_custom_call" | custom-call | flops 200000000 | bytes 4400000 | tf_op jit(solution)/shard_map/text/pallas_call | solution.py:324
  19.7 0.1 collective-permute-start
  19.8 0.0 slice-start
  19.8 0.0 copy-done.10
  19.8 0.0 copy-done.9
  19.9 0.0 slice-start.1
  19.9 0.0 copy-start.6
  19.9 2.8 %image.1 = bf16[16,2,16,128]{3,2,1,0:T(8,128)(2,1)S(1)} custom-call(f32[8,16,128]{2,1,0:T(8,128)S(1)} %get-tuple-element.18.after.own, bf16[16,16,128]{2,1,0:T(8,128)(2,1)S(1)} %all_to_all.20.arrived, bf16[8,2,576,128]{3,2,1,0:T(8,128)(2,1)S(1)} %copy-done.9, bf16[8,2,576,128]{3,2,1,0:T(8,128)(2,1)S(1)} %copy-done.10), custom_call_target="tpu_custom_call" | custom-call | flops 10000000000 | bytes 5000000 | tf_op jit(solution)/shard_map/image/pallas_call | solution.py:334
  22.7 0.0 collective-permute-done.other
  22.7 11.3 %all_to_all.21.back = bf16[32,16,128]{2,1,0:T(8,128)(2,1)S(1)} all-to-all(bf16[32,16,128]{2,1,0:T(8,128)(2,1)S(1)} %bitcast.10), channel_id=1, replica_groups=mesh['group'=16,'depth'=2,'mp'=4] {'group','depth'}, dimensions={0} | all-to-all | bytes 262144 | tf_op jit(solution)/shard_map/all_to_all | solution.py:343
  34.0 0.0 slice-done
  34.0 0.0 slice-done.1
  34.0 0.0 copy-done.6
  34.0 0.0 copy-start.11
  34.0 2.0 %merge.1 = (bf16[8,8,128]{2,1,0:T(8,128)(2,1)}, f32[8,4096]{1,0:T(8,128)S(1)}, bf16[8,4096]{1,0:T(8,128)(2,1)S(1)}) custom-call(s32[40]{0:T(128)S(1)} %get-tuple-element.17.plan, bf16[32,16,128]{2,1,0:T(8,128)(2,1)S(1)} %all_to_all.21.back, f32[8,16,128]{2,1,0:T(8,128)S(1)} %get-tuple-element.18.after.own, f32[8,16,128]{2,1,0:T(8,128)S(1)} %collective-permute-done.other, ...), custom_call_target="tpu_custom_call" | custom-call | flops 100000000 | bytes 8800000 | tf_op jit(solution)/shard_map/merge/pallas_call | solution.py:346
  36.0 4.1 %collective-permute-start.3 = (bf16[8,4096]{1,0:T(8,128)(2,1)S(1)}, bf16[8,4096]{1,0:T(8,128)(2,1)S(1)}, u32[]{:S(2)}, u32[]{:S(2)}) collective-permute-start(bf16[8,4096]{1,0:T(8,128)(2,1)S(1)} %get-tuple-element.25), channel_id=1, source_target_pairs={{0,3},{1,2},{2,1},{3,0},{4,7},{5,6},{6,5},{7,4},{8,11},{9,10},{10,... | collective-permute-start | bytes 196616 | tf_op jit(solution)/shard_map/ppermute | solution.py:360
  40.1 0.0 collective-permute-start.2
  40.1 0.9 %collective-permute-start.1 = (bf16[8,4096]{1,0:T(8,128)(2,1)S(1)}, bf16[8,4096]{1,0:T(8,128)(2,1)S(1)}, u32[]{:S(2)}, u32[]{:S(2)}) collective-permute-start(bf16[8,4096]{1,0:T(8,128)(2,1)S(1)} %get-tuple-element.25), channel_id=1, source_target_pairs={{0,1},{1,0},{2,3},{3,2},{4,5},{5,4},{6,7},{7,6},{8,9},{9,8},{10,11... | collective-permute-start | bytes 196616 | tf_op jit(solution)/shard_map/ppermute | solution.py:360
  41.0 2.1 %collective-permute-done.3.third = bf16[8,4096]{1,0:T(8,128)(2,1)S(1)} collective-permute-done((bf16[8,4096]{1,0:T(8,128)(2,1)S(1)}, bf16[8,4096]{1,0:T(8,128)(2,1)S(1)}, u32[]{:S(2)}, u32[]{:S(2)}) %collective-permute-start.3) | collective-permute-done | bytes 65568 | tf_op jit(solution)/shard_map/ppermute | solution.py:360
  43.1 3.0 %collective-permute-done.2.second = bf16[8,4096]{1,0:T(8,128)(2,1)S(1)} collective-permute-done((bf16[8,4096]{1,0:T(8,128)(2,1)S(1)}, bf16[8,4096]{1,0:T(8,128)(2,1)S(1)}, u32[]{:S(2)}, u32[]{:S(2)}) %collective-permute-start.2) | collective-permute-done | bytes 65568 | tf_op jit(solution)/shard_map/ppermute | solution.py:360
  46.1 0.0 collective-permute-done.1.first
  46.1 0.0 copy-done.11
  46.1 0.0 copy-start.3
  46.1 0.0 copy-start.4
  46.1 0.8 norm.1
  46.9 0.0 copy-start.2
  46.9 19.5 %all_to_all.22 = bf16[16,8,4096]{2,1,0:T(8,128)(2,1)S(1)} all-to-all(bf16[16,8,4096]{2,1,0:T(8,128)(2,1)S(1)} %get-tuple-element.26), channel_id=1, replica_groups=mesh['group'=16,'depth'=2,'mp'=4] {'group'}, dimensions={0} | all-to-all | bytes 2097152 | tf_op jit(solution)/shard_map/all_to_all | solution.py:373
  66.4 0.0 copy-done.3
  66.4 0.0 copy-done.4
  66.4 0.0 copy-done.2
  66.4 1.9 %feed.1 = bf16[64,8,1024]{2,1,0:T(8,128)(2,1)S(1)} custom-call(bf16[128,4096]{1,0:T(8,128)(2,1)S(1)} %bitcast.7, bf16[224,4096]{1,0:T(8,128)(2,1)S(1)} %bitcast.8, bf16[224,4096]{1,0:T(8,128)(2,1)S(1)} %bitcast.9, bf16[224,4096]{1,0:T(8,128)(2,1)S(1)} %copy-done.4), custom_call_target="tpu_custom_call" | custom-call | flops 1400000000 | bytes 7000000 | tf_op jit(solution)/shard_map/feed/pallas_call | solution.py:375
  68.4 21.3 %all_to_all.23.arrived = bf16[64,8,1024]{2,1,0:T(8,128)(2,1)S(1)} all-to-all(bf16[64,8,1024]{2,1,0:T(8,128)(2,1)S(1)} %feed.1), channel_id=1, replica_groups=mesh['group'=16,'depth'=2,'mp'=4] {'group','mp'}, dimensions={0} | all-to-all | bytes 2097152 | tf_op jit(solution)/shard_map/all_to_all | solution.py:384
  89.7 0.8 last.1
  (1 shorter events, 0.0 us)
Async XLA Ops:
  0.6 16.7 %copy-start.5 = (bf16[16,8,128]{2,1,0:T(8,128)(2,1)S(1)}, bf16[16,8,128]{2,1,0:T(8,128)(2,1)}, u32[]{:S(2)}) copy-start(bf16[16,8,128]{2,1,0:T(8,128)(2,1)} %queries.1) | copy-start | bytes 98308
  0.6 16.6 %copy-start.1 = (bf16[16,2,256,128]{3,2,1,0:T(8,128)(2,1)S(1)}, bf16[16,2,256,128]{3,2,1,0:T(8,128)(2,1)}, u32[]{:S(2)}) copy-start(bf16[16,2,256,128]{3,2,1,0:T(8,128)(2,1)} %values.2) | copy-start | bytes 6291460
  0.7 16.6 %copy-start = (bf16[16,2,256,128]{3,2,1,0:T(8,128)(2,1)S(1)}, bf16[16,2,256,128]{3,2,1,0:T(8,128)(2,1)}, u32[]{:S(2)}) copy-start(bf16[16,2,256,128]{3,2,1,0:T(8,128)(2,1)} %keys.2) | copy-start | bytes 6291460
  0.7 16.6 %copy-start.8 = (bf16[16,2,128]{2,1,0:T(2,128)(2,1)S(1)}, bf16[16,2,128]{2,1,0:T(2,128)(2,1)}, u32[]{:S(2)}) copy-start(bf16[16,2,128]{2,1,0:T(2,128)(2,1)} %new_values.1) | copy-start | bytes 24580
  0.7 16.6 %copy-start.7 = (bf16[16,2,128]{2,1,0:T(2,128)(2,1)S(1)}, bf16[16,2,128]{2,1,0:T(2,128)(2,1)}, u32[]{:S(2)}) copy-start(bf16[16,2,128]{2,1,0:T(2,128)(2,1)} %new_keys.1) | copy-start | bytes 24580
  0.7 19.2 %copy-start.10 = (bf16[8,2,576,128]{3,2,1,0:T(8,128)(2,1)S(1)}, bf16[8,2,576,128]{3,2,1,0:T(8,128)(2,1)}, u32[]{:S(2)}) copy-start(bf16[8,2,576,128]{3,2,1,0:T(8,128)(2,1)} %values.3) | copy-start | bytes 7077892
  17.3 2.5 %copy-start.9 = (bf16[8,2,576,128]{3,2,1,0:T(8,128)(2,1)S(1)}, bf16[8,2,576,128]{3,2,1,0:T(8,128)(2,1)}, u32[]{:S(2)}) copy-start(bf16[8,2,576,128]{3,2,1,0:T(8,128)(2,1)} %keys.3) | copy-start | bytes 7077892
  19.7 2.9 %collective-permute-start = (f32[8,16,128]{2,1,0:T(8,128)S(1)}, f32[8,16,128]{2,1,0:T(8,128)S(1)}, u32[]{:S(2)}, u32[]{:S(2)}) collective-permute-start(f32[8,16,128]{2,1,0:T(8,128)S(1)} %get-tuple-element.20), channel_id=1, source_target_pairs={{0,4},{4,0},{1,5},{5,1},{2,6},{6,2},{3,7},{7,3},{8,12},{12,8},{9,1... | collective-permute-start | bytes 196616 | tf_op jit(solution)/shard_map/ppermute | solution.py:332
  19.8 14.1 %slice-start = ((s8[8388608]{0:T(1024)(128)(4,1)}), s8[4194304]{0:T(1024)(128)(4,1)S(1)}, s32[]{:S(2)}) async-start(s8[8388608]{0:T(1024)(128)(4,1)} %bitcast.5), calls=%async_computation.4 | async-start | bytes 8388608
  19.9 14.1 %slice-start.1 = ((s8[8388608]{0:T(1024)(128)(4,1)}), s8[4194304]{0:T(1024)(128)(4,1)S(1)}, s32[]{:S(2)}) async-start(s8[8388608]{0:T(1024)(128)(4,1)} %bitcast.5), calls=%async_computation.5 | async-start | bytes 8388608
  19.9 14.1 %copy-start.6 = (bf16[2,4096]{1,0:T(2,128)(2,1)S(1)}, bf16[2,4096]{1,0:T(2,128)(2,1)}, u32[]{:S(2)}) copy-start(bf16[2,4096]{1,0:T(2,128)(2,1)} %states.1) | copy-start | bytes 49156
  34.0 12.1 %copy-start.11 = (f32[4096]{0:T(1024)S(1)}, f32[4096]{0:T(1024)}, u32[]{:S(2)}) copy-start(f32[4096]{0:T(1024)} %param.34) | copy-start | bytes 49156
  36.0 7.2 %collective-permute-start.3 = (bf16[8,4096]{1,0:T(8,128)(2,1)S(1)}, bf16[8,4096]{1,0:T(8,128)(2,1)S(1)}, u32[]{:S(2)}, u32[]{:S(2)}) collective-permute-start(bf16[8,4096]{1,0:T(8,128)(2,1)S(1)} %get-tuple-element.25), channel_id=1, source_target_pairs={{0,3},{1,2},{2,1},{3,0},{4,7},{5,6},{6,5},{7,4},{8,11},{9,10},{10,... | collective-permute-start | bytes 196616 | tf_op jit(solution)/shard_map/ppermute | solution.py:360
  40.1 6.0 %collective-permute-start.2 = (bf16[8,4096]{1,0:T(8,128)(2,1)S(1)}, bf16[8,4096]{1,0:T(8,128)(2,1)S(1)}, u32[]{:S(2)}, u32[]{:S(2)}) collective-permute-start(bf16[8,4096]{1,0:T(8,128)(2,1)S(1)} %get-tuple-element.25), channel_id=1, source_target_pairs={{0,2},{1,3},{2,0},{3,1},{4,6},{5,7},{6,4},{7,5},{8,10},{9,11},{10,... | collective-permute-start | bytes 196616 | tf_op jit(solution)/shard_map/ppermute | solution.py:360
  40.1 6.0 %collective-permute-start.1 = (bf16[8,4096]{1,0:T(8,128)(2,1)S(1)}, bf16[8,4096]{1,0:T(8,128)(2,1)S(1)}, u32[]{:S(2)}, u32[]{:S(2)}) collective-permute-start(bf16[8,4096]{1,0:T(8,128)(2,1)S(1)} %get-tuple-element.25), channel_id=1, source_target_pairs={{0,1},{1,0},{2,3},{3,2},{4,5},{5,4},{6,7},{7,6},{8,9},{9,8},{10,11... | collective-permute-start | bytes 196616 | tf_op jit(solution)/shard_map/ppermute | solution.py:360
  46.1 20.3 %copy-start.3 = (bf16[4096,224]{0,1:T(8,128)(2,1)S(1)}, bf16[4096,224]{0,1:T(8,128)(2,1)}, u32[]{:S(2)}) copy-start(bf16[4096,224]{0,1:T(8,128)(2,1)} %param.36) | copy-start | bytes 5505028
  46.1 20.3 %copy-start.4 = (bf16[224,4096]{1,0:T(8,128)(2,1)S(1)}, bf16[224,4096]{1,0:T(8,128)(2,1)}, u32[]{:S(2)}) copy-start(bf16[224,4096]{1,0:T(8,128)(2,1)} %down.1) | copy-start | bytes 5505028
  46.9 19.5 %copy-start.2 = (bf16[4096,224]{0,1:T(8,128)(2,1)S(1)}, bf16[4096,224]{0,1:T(8,128)(2,1)}, u32[]{:S(2)}) copy-start(bf16[4096,224]{0,1:T(8,128)(2,1)} %param.35) | copy-start | bytes 5505028

commit v4 on v3

--- a/solution.py
+++ b/solution.py
@@ -82,25 +82,19 @@
         return slot >> 3, slot & 7
 
     for r in range(requests):
-        start = first[r]
-        skip = (start + depth) & 1
-        place = start + skip
-        owner, within = source(place)
+        start, read = first[r], images[r]
         plan[LENGTH + r] = lengths[r]
-
-        @pl.when((skip < images[r]) & (place < listed))
-        def _():
-            out[owner, 0:8, :] = queries[r]
-            code = (within * 2 + r // half).astype(F32)
-            out[owner, 8:16, :] = jnp.full((8, 128), code, F32).astype(BF16)
-
-    for j in range(half):
-        r = depth * half + j
         for k in range(2):
-            place = first[r] + k
-            owner, _ = source(place)
-            live = (k < images[r]) & (place < listed)
-            plan[SOURCE + 2 * j + k] = jnp.where(live, owner * 2 + (place & 1), -1)
+            place = start + k
+            owner, within = source(place)
+            live = (k < read) & (place < listed)
+            plan[SOURCE + 2 * r + k] = jnp.where(live, owner * 2 + (place & 1), -1)
+
+            @pl.when(live & ((place & 1) == depth))
+            def _():
+                out[owner, 0:8, :] = queries[r]
+                code = (within * 2 + r // half).astype(F32)
+                out[owner, 8:16, :] = jnp.full((8, 128), code, F32).astype(BF16)
 
 
 def side_by_side(pair):
@@ -111,42 +105,43 @@
     depth = plan[OWN_DEPTH]
     requests, heads, width = queries.shape
     half = requests // 2
+    rows = requests * heads
     span = keys.shape[2]
-    step = requests // 4
     scale = 1.0 / (math.sqrt(width) * math.log(2.0))
-    low = lax.broadcasted_iota(jnp.int32, (heads, 1), 0) < heads // 2
-    lane = lax.broadcasted_iota(jnp.int32, (heads, 128), 1)
-    where = depth * span + lax.broadcasted_iota(jnp.int32, (heads, span), 1)
-    for c in range(4):
-        part, out = (1 - depth, other) if c < 2 else (depth, own)
-        row = (c % 2) * step
-        begin = part * half + row
-        scores, fresh = [], []
-        for j in range(step):
-            r = begin + j
-            q = queries[r]
-            zero = jnp.zeros_like(q)
-            both = jnp.concatenate([jnp.where(low, q, zero), jnp.where(low, zero, q)], axis=1)
-            s = matmul_t(both, side_by_side(keys[r])) * scale
-            scores.append(jnp.where(where < plan[LENGTH + r], s, MASKED))
-            nk = new_keys[r].astype(F32)
-            nk = jnp.where(low, nk[0:1], nk[1:2])
-            fresh.append(jnp.sum(q.astype(F32) * nk, axis=-1, keepdims=True) * scale)
-        s = jnp.concatenate(scores, axis=0)
-        n = jnp.where(depth == 0, jnp.concatenate(fresh, axis=0), MASKED)
-        level = jnp.floor(jnp.maximum(jnp.max(s, axis=-1, keepdims=True), n))
-        w = jnp.where(s > 0.5 * MASKED, jnp.exp2(s - level), 0.0).astype(BF16)
-        nw = jnp.where(n > 0.5 * MASKED, jnp.exp2(n - level), 0.0).astype(BF16).astype(F32)
-        total = jnp.sum(w.astype(F32), axis=-1, keepdims=True) + nw
-        for j in range(step):
-            r = begin + j
-            rows = slice(j * heads, (j + 1) * heads)
-            o = matmul(w[rows], side_by_side(values[r]))
-            o = jnp.where(low, o[:, 0:width], o[:, width : 2 * width])
-            nv = new_values[r].astype(F32)
-            o = o + nw[rows] * jnp.where(low, nv[0:1], nv[1:2])
-            out[row + j, 0:8, :] = o
-            out[row + j, 8:16, :] = jnp.where(lane < 64, level[rows], total[rows])
+    order = [(p + half * depth) % requests for p in range(requests)]
+    low8 = lax.broadcasted_iota(jnp.int32, (heads, 1), 0) < heads // 2
+    low = lax.broadcasted_iota(jnp.int32, (rows, 1), 0) % heads < heads // 2
+    lane = lax.broadcasted_iota(jnp.int32, (1, rows), 1) // heads
+    q = jnp.concatenate([queries[r] for r in order], axis=0)
+    zero = jnp.zeros_like(q)
+    both = jnp.concatenate([jnp.where(low, q, zero), jnp.where(low, zero, q)], axis=1)
+    across = jnp.zeros((span, rows), F32)
+    for p, r in enumerate(order):
+        across = jnp.where(lane == p, matmul_t(side_by_side(keys[r]), both), across)
+    length = jnp.concatenate([jnp.full((heads, 1), plan[LENGTH + r]) for r in order], axis=0)
+    where = depth * span + lax.broadcasted_iota(jnp.int32, (rows, span), 1)
+    allowed = where < length
+    s = jnp.where(allowed, across.T * scale, MASKED)
+
+    def per_head(ref):
+        pairs = [ref[r].astype(F32) for r in order]
+        return jnp.concatenate([jnp.where(low8, x[0:1], x[1:2]) for x in pairs], axis=0)
+
+    fresh = jnp.sum(q.astype(F32) * per_head(new_keys), axis=-1, keepdims=True) * scale
+    n = jnp.where(depth == 0, fresh, MASKED)
+    level = jnp.floor(jnp.maximum(jnp.max(s, axis=-1, keepdims=True), n))
+    w = jnp.where(allowed, jnp.exp2(s - level), 0.0).astype(BF16)
+    nw = jnp.where(depth == 0, jnp.exp2(n - level), 0.0).astype(BF16).astype(F32)
+    total = jnp.sum(w.astype(F32), axis=-1, keepdims=True) + nw
+    added = nw * per_head(new_values)
+    column = lax.broadcasted_iota(jnp.int32, (rows, 128), 1)
+    stats = jnp.where(column < 64, level, total)
+    for p, r in enumerate(order):
+        at = slice(p * heads, (p + 1) * heads)
+        o = matmul(w[at], side_by_side(values[r]))
+        out = own if p < half else other
+        out[p % half, 0:8, :] = jnp.where(low8, o[:, 0:width], o[:, width : 2 * width]) + added[at]
+        out[p % half, 8:16, :] = stats[at]
 
 
 def image_kernel(after, arrived, keys, values, out):
@@ -158,22 +153,26 @@
     q = arrived[:, 0:8, :].reshape(rows, width)
     code = arrived[:, 8:16, :].reshape(rows, width).astype(F32)
     within = jnp.floor(code * 0.5)
+    within_lane = within.T[0:1, :]
     low = lax.broadcasted_iota(jnp.int32, (rows, 1), 0) % 8 < 4
     zero = jnp.zeros_like(q)
     both = jnp.concatenate([jnp.where(low, q, zero), jnp.where(low, zero, q)], axis=1)
-    level = jnp.zeros((rows, 1), F32)
-    total = jnp.zeros((rows, 1), F32)
+    across = jnp.zeros((patches, rows), F32)
+    for i in range(images):
+        across = jnp.where(
+            within_lane == float(i), matmul_t(side_by_side(keys[i]), both), across
+        )
+    s = across.T * scale
+    level = jnp.floor(jnp.max(s, axis=-1, keepdims=True))
+    w = jnp.exp2(s - level).astype(BF16)
+    present = within[:, 0:1] >= 0.0
+    total = jnp.where(present, jnp.sum(w.astype(F32), axis=-1, keepdims=True), 0.0)
+    nothing = jnp.zeros_like(w)
     o = jnp.zeros((rows, 2 * width), F32)
     for i in range(images):
-        mine = within[:, 0:1] == float(i)
-        s = matmul_t(both, side_by_side(keys[i])) * scale
-        here = jnp.floor(jnp.max(s, axis=-1, keepdims=True))
-        w = jnp.where(mine, jnp.exp2(s - here), 0.0).astype(BF16)
-        total = total + jnp.sum(w.astype(F32), axis=-1, keepdims=True)
-        level = jnp.where(mine, here, level)
-        o = o + matmul(w, side_by_side(values[i]))
+        o = o + matmul(jnp.where(within[:, 0:1] == float(i), w, nothing), side_by_side(values[i]))
     o = jnp.where(low, o[:, 0:width], o[:, width : 2 * width])
-    o = o / jnp.where(total > 0.0, total, 1.0)
+    o = o / jnp.where(present, total, 1.0)
     lane = lax.broadcasted_iota(jnp.int32, (rows, width), 1)
     level_high = level.astype(BF16).astype(F32)
     total_high = total.astype(BF16).astype(F32)
@@ -203,7 +202,7 @@
     for k in range(2):
         stats, values = [], []
         for j in range(half):
-            source = plan[SOURCE + 2 * j + k]
+            source = plan[SOURCE + 2 * (plan[OWN_DEPTH] * half + j) + k]
             at = jnp.maximum(source, 0)
             stats.append(jnp.where(source >= 0, back[at, 8:16, :].astype(F32), dead))
             values.append(back[at, 0:8, :].astype(F32))
@@ -307,7 +306,7 @@
         route_kernel,
         (
             jax.ShapeDtypeStruct((groups, 16, width), BF16),
-            jax.ShapeDtypeStruct((SOURCE + requests,), jnp.int32),
+            jax.ShapeDtypeStruct((SOURCE + 2 * requests,), jnp.int32),
         ),
         [HBM] * 7,
         20_000_000_000,

time: 90.7 us -> 89.9 us (level)
  Pallas kernels: 12.7 us -> 11.7 us
where the time goes in v4:
time: 89.9 us; the launch traced here: 89.6 us
  blocking collectives  66.8 us (74%)
  Pallas kernels  11.7 us (13%)
  starting transfers between devices  5.11 us (6%)
  waiting for transfers between devices  5.08 us (6%)
    all_to_all x1, blocking collectives, on_device(): gathered = lax.all_to_all(down, ('group', 'mp'), 0, 0, tiled=True)  21.3 us
    all_to_all x1, blocking collectives, on_device(): lax.all_to_all(normed, 'group', 0, 0, tiled=True)  19.5 us
    all_to_all x1, blocking collectives, on_device(): arrived = lax.all_to_all(routed, 'group', 0, 0, tiled=True)  14.6 us
    all_to_all x1, blocking collectives, on_device(): lax.all_to_all(back.reshape(groups * depths, 16, width), ('group', 'depth...  11.4 us
    ppermute x3, waiting for transfers between devices, on_device(): lax.ppermute(sent, 'mp', [(i, i ^ k) for i in range(ring)])  5.08 us
    ppermute x3, starting transfers between devices, on_device(): lax.ppermute(sent, 'mp', [(i, i ^ k) for i in range(ring)])  5.05 us
    pallas_call x1, Pallas kernels, on_device(): call(image_kernel, jax.ShapeDtypeStruct((groups, depths, 16, width), BF16...  2.31 us
    pallas_call x1, Pallas kernels, on_device(): call(route_kernel, (jax.ShapeDtypeStruct((groups, 16, width), BF16), jax....  2.12 us
  transfers between devices with their start and end apart: 4, of which 2 were waited for; matrix products, arithmetic and copies ran while one was open for 0% of the time, Pallas kernels for 3%

profile of v4, /device:TPU:0, one launch (start us, length us, event | category | flops | bytes accessed | tf_op | source)
XLA Modules:
  0.0 89.6 jit_solution(1226116013810026017)
XLA Ops:
  0.6 0.0 copy-start.5
  0.6 0.0 copy-start.1
  0.7 0.0 copy-start
  0.7 0.0 copy-start.8
  0.7 0.0 copy-start.7
  0.7 0.0 copy-start.10
  0.7 2.1 %route.1 = (bf16[16,16,128]{2,1,0:T(8,128)(2,1)S(1)}, s32[56]{0:T(128)S(1)}) custom-call(s32[128]{0:T(128)} %slots_hbm.1, s32[16,32]{1,0:T(8,128)} %blocks_hbm.1, s32[16]{0:T(128)} %count_hbm.1, s32[16]{0:T(128)} %first_hbm.1, s32[16]{0:T(128)} %images_hbm.1, s32[16]{0:T(128)} %lengths_hbm.1, bf16[16,8,128]{2,1,0:T(8,128)(2,1)} %queries.1), custom_call_target="tpu_custom_call" | custom-call | flops 20000000000 | bytes 100000 | tf_op jit(solution)/shard_map/route/pallas_call | solution.py:305
  2.8 14.6 %all_to_all.20.arrived = bf16[16,16,128]{2,1,0:T(8,128)(2,1)S(1)} all-to-all(bf16[16,16,128]{2,1,0:T(8,128)(2,1)S(1)} %get-tuple-element.15), channel_id=1, replica_groups=mesh['group'=16,'depth'=2,'mp'=4] {'group'}, dimensions={0} | all-to-all | bytes 131072 | tf_op jit(solution)/shard_map/all_to_all | solution.py:319
  17.4 0.0 copy-done.5
  17.4 0.0 copy-done.1
  17.4 0.0 copy-done
  17.4 0.0 copy-done.8
  17.4 0.0 copy-done.7
  17.4 0.0 copy-start.9
  17.5 1.8 %text.1 = (f32[8,16,128]{2,1,0:T(8,128)S(1)}, f32[8,16,128]{2,1,0:T(8,128)S(1)}) custom-call(s32[56]{0:T(128)S(1)} %get-tuple-element.17.plan, bf16[16,8,128]{2,1,0:T(8,128)(2,1)S(1)} %copy-done.5, bf16[16,2,128]{2,1,0:T(2,128)(2,1)S(1)} %copy-done.7, bf16[16,2,128]{2,1,0:T(2,128)(2,1)S(1)} %copy-done.8, bf16[16,2,256,128]{3,2,1,0:T(8,128)(2,1)S(1)} %copy-done, ...), custom_call_target="tpu_custom_call" | custom-call | flops 200000000 | bytes 4400000 | tf_op jit(solution)/shard_map/text/pallas_call | solution.py:323
  19.2 0.1 collective-permute-start
  19.3 0.0 slice-start
  19.3 0.0 copy-done.10
  19.3 0.0 copy-done.9
  19.4 0.0 slice-start.1
  19.4 0.0 copy-start.6
  19.4 2.3 %image.1 = bf16[16,2,16,128]{3,2,1,0:T(8,128)(2,1)S(1)} custom-call(f32[8,16,128]{2,1,0:T(8,128)S(1)} %get-tuple-element.18.after.own, bf16[16,16,128]{2,1,0:T(8,128)(2,1)S(1)} %all_to_all.20.arrived, bf16[8,2,576,128]{3,2,1,0:T(8,128)(2,1)S(1)} %copy-done.9, bf16[8,2,576,128]{3,2,1,0:T(8,128)(2,1)S(1)} %copy-done.10), custom_call_target="tpu_custom_call" | custom-call | flops 10000000000 | bytes 5000000 | tf_op jit(solution)/shard_map/image/pallas_call | solution.py:333
  21.7 0.0 collective-permute-done.other
  21.7 11.4 %all_to_all.21.back = bf16[32,16,128]{2,1,0:T(8,128)(2,1)S(1)} all-to-all(bf16[32,16,128]{2,1,0:T(8,128)(2,1)S(1)} %bitcast.10), channel_id=1, replica_groups=mesh['group'=16,'depth'=2,'mp'=4] {'group','depth'}, dimensions={0} | all-to-all | bytes 262144 | tf_op jit(solution)/shard_map/all_to_all | solution.py:342
  33.1 0.0 slice-done
  33.1 0.0 slice-done.1
  33.1 0.0 copy-done.6
  33.1 0.0 copy-start.11
  33.2 2.0 %merge.1 = (bf16[8,8,128]{2,1,0:T(8,128)(2,1)}, f32[8,4096]{1,0:T(8,128)S(1)}, bf16[8,4096]{1,0:T(8,128)(2,1)S(1)}) custom-call(s32[56]{0:T(128)S(1)} %get-tuple-element.17.plan, bf16[32,16,128]{2,1,0:T(8,128)(2,1)S(1)} %all_to_all.21.back, f32[8,16,128]{2,1,0:T(8,128)S(1)} %get-tuple-element.18.after.own, f32[8,16,128]{2,1,0:T(8,128)S(1)} %collective-permute-done.other, ...), custom_call_target="tpu_custom_call" | custom-call | flops 100000000 | bytes 8800000 | tf_op jit(solution)/shard_map/merge/pallas_call | solution.py:345
  35.1 4.1 %collective-permute-start.3 = (bf16[8,4096]{1,0:T(8,128)(2,1)S(1)}, bf16[8,4096]{1,0:T(8,128)(2,1)S(1)}, u32[]{:S(2)}, u32[]{:S(2)}) collective-permute-start(bf16[8,4096]{1,0:T(8,128)(2,1)S(1)} %get-tuple-element.25), channel_id=1, source_target_pairs={{0,3},{1,2},{2,1},{3,0},{4,7},{5,6},{6,5},{7,4},{8,11},{9,10},{10,... | collective-permute-start | bytes 196616 | tf_op jit(solution)/shard_map/ppermute | solution.py:359
  39.2 0.0 collective-permute-start.2
  39.2 0.9 %collective-permute-start.1 = (bf16[8,4096]{1,0:T(8,128)(2,1)S(1)}, bf16[8,4096]{1,0:T(8,128)(2,1)S(1)}, u32[]{:S(2)}, u32[]{:S(2)}) collective-permute-start(bf16[8,4096]{1,0:T(8,128)(2,1)S(1)} %get-tuple-element.25), channel_id=1, source_target_pairs={{0,1},{1,0},{2,3},{3,2},{4,5},{5,4},{6,7},{7,6},{8,9},{9,8},{10,11... | collective-permute-start | bytes 196616 | tf_op jit(solution)/shard_map/ppermute | solution.py:359
  40.2 2.1 %collective-permute-done.3.third = bf16[8,4096]{1,0:T(8,128)(2,1)S(1)} collective-permute-done((bf16[8,4096]{1,0:T(8,128)(2,1)S(1)}, bf16[8,4096]{1,0:T(8,128)(2,1)S(1)}, u32[]{:S(2)}, u32[]{:S(2)}) %collective-permute-start.3) | collective-permute-done | bytes 65568 | tf_op jit(solution)/shard_map/ppermute | solution.py:359
  42.3 3.0 %collective-permute-done.2.second = bf16[8,4096]{1,0:T(8,128)(2,1)S(1)} collective-permute-done((bf16[8,4096]{1,0:T(8,128)(2,1)S(1)}, bf16[8,4096]{1,0:T(8,128)(2,1)S(1)}, u32[]{:S(2)}, u32[]{:S(2)}) %collective-permute-start.2) | collective-permute-done | bytes 65568 | tf_op jit(solution)/shard_map/ppermute | solution.py:359
  45.3 0.0 collective-permute-done.1.first
  45.3 0.0 copy-done.11
  45.3 0.0 copy-start.3
  45.3 0.0 copy-start.4
  45.3 0.8 norm.1
  46.1 0.0 copy-start.2
  46.1 19.5 %all_to_all.22 = bf16[16,8,4096]{2,1,0:T(8,128)(2,1)S(1)} all-to-all(bf16[16,8,4096]{2,1,0:T(8,128)(2,1)S(1)} %get-tuple-element.26), channel_id=1, replica_groups=mesh['group'=16,'depth'=2,'mp'=4] {'group'}, dimensions={0} | all-to-all | bytes 2097152 | tf_op jit(solution)/shard_map/all_to_all | solution.py:372
  65.6 0.0 copy-done.3
  65.6 0.0 copy-done.4
  65.6 0.0 copy-done.2
  65.6 2.0 %feed.1 = bf16[64,8,1024]{2,1,0:T(8,128)(2,1)S(1)} custom-call(bf16[128,4096]{1,0:T(8,128)(2,1)S(1)} %bitcast.7, bf16[224,4096]{1,0:T(8,128)(2,1)S(1)} %bitcast.8, bf16[224,4096]{1,0:T(8,128)(2,1)S(1)} %bitcast.9, bf16[224,4096]{1,0:T(8,128)(2,1)S(1)} %copy-done.4), custom_call_target="tpu_custom_call" | custom-call | flops 1400000000 | bytes 7000000 | tf_op jit(solution)/shard_map/feed/pallas_call | solution.py:374
  67.5 21.3 %all_to_all.23.arrived = bf16[64,8,1024]{2,1,0:T(8,128)(2,1)S(1)} all-to-all(bf16[64,8,1024]{2,1,0:T(8,128)(2,1)S(1)} %feed.1), channel_id=1, replica_groups=mesh['group'=16,'depth'=2,'mp'=4] {'group','mp'}, dimensions={0} | all-to-all | bytes 2097152 | tf_op jit(solution)/shard_map/all_to_all | solution.py:383
  88.9 0.8 last.1
  (1 shorter events, 0.0 us)
Async XLA Ops:
  0.6 16.8 %copy-start.5 = (bf16[16,8,128]{2,1,0:T(8,128)(2,1)S(1)}, bf16[16,8,128]{2,1,0:T(8,128)(2,1)}, u32[]{:S(2)}) copy-start(bf16[16,8,128]{2,1,0:T(8,128)(2,1)} %queries.1) | copy-start | bytes 98308
  0.6 16.8 %copy-start.1 = (bf16[16,2,256,128]{3,2,1,0:T(8,128)(2,1)S(1)}, bf16[16,2,256,128]{3,2,1,0:T(8,128)(2,1)}, u32[]{:S(2)}) copy-start(bf16[16,2,256,128]{3,2,1,0:T(8,128)(2,1)} %values.2) | copy-start | bytes 6291460
  0.7 16.8 %copy-start = (bf16[16,2,256,128]{3,2,1,0:T(8,128)(2,1)S(1)}, bf16[16,2,256,128]{3,2,1,0:T(8,128)(2,1)}, u32[]{:S(2)}) copy-start(bf16[16,2,256,128]{3,2,1,0:T(8,128)(2,1)} %keys.2) | copy-start | bytes 6291460
  0.7 16.8 %copy-start.8 = (bf16[16,2,128]{2,1,0:T(2,128)(2,1)S(1)}, bf16[16,2,128]{2,1,0:T(2,128)(2,1)}, u32[]{:S(2)}) copy-start(bf16[16,2,128]{2,1,0:T(2,128)(2,1)} %new_values.1) | copy-start | bytes 24580
  0.7 16.8 %copy-start.7 = (bf16[16,2,128]{2,1,0:T(2,128)(2,1)S(1)}, bf16[16,2,128]{2,1,0:T(2,128)(2,1)}, u32[]{:S(2)}) copy-start(bf16[16,2,128]{2,1,0:T(2,128)(2,1)} %new_keys.1) | copy-start | bytes 24580
  0.7 18.6 %copy-start.10 = (bf16[8,2,576,128]{3,2,1,0:T(8,128)(2,1)S(1)}, bf16[8,2,576,128]{3,2,1,0:T(8,128)(2,1)}, u32[]{:S(2)}) copy-start(bf16[8,2,576,128]{3,2,1,0:T(8,128)(2,1)} %values.3) | copy-start | bytes 7077892
  17.4 1.9 %copy-start.9 = (bf16[8,2,576,128]{3,2,1,0:T(8,128)(2,1)S(1)}, bf16[8,2,576,128]{3,2,1,0:T(8,128)(2,1)}, u32[]{:S(2)}) copy-start(bf16[8,2,576,128]{3,2,1,0:T(8,128)(2,1)} %keys.3) | copy-start | bytes 7077892
  19.2 2.4 %collective-permute-start = (f32[8,16,128]{2,1,0:T(8,128)S(1)}, f32[8,16,128]{2,1,0:T(8,128)S(1)}, u32[]{:S(2)}, u32[]{:S(2)}) collective-permute-start(f32[8,16,128]{2,1,0:T(8,128)S(1)} %get-tuple-element.20), channel_id=1, source_target_pairs={{0,4},{4,0},{1,5},{5,1},{2,6},{6,2},{3,7},{7,3},{8,12},{12,8},{9,1... | collective-permute-start | bytes 196616 | tf_op jit(solution)/shard_map/ppermute | solution.py:331
  19.3 13.8 %slice-start = ((s8[8388608]{0:T(1024)(128)(4,1)}), s8[4194304]{0:T(1024)(128)(4,1)S(1)}, s32[]{:S(2)}) async-start(s8[8388608]{0:T(1024)(128)(4,1)} %bitcast.5), calls=%async_computation.4 | async-start | bytes 8388608
  19.4 13.8 %slice-start.1 = ((s8[8388608]{0:T(1024)(128)(4,1)}), s8[4194304]{0:T(1024)(128)(4,1)S(1)}, s32[]{:S(2)}) async-start(s8[8388608]{0:T(1024)(128)(4,1)} %bitcast.5), calls=%async_computation.5 | async-start | bytes 8388608
  19.4 13.8 %copy-start.6 = (bf16[2,4096]{1,0:T(2,128)(2,1)S(1)}, bf16[2,4096]{1,0:T(2,128)(2,1)}, u32[]{:S(2)}) copy-start(bf16[2,4096]{1,0:T(2,128)(2,1)} %states.1) | copy-start | bytes 49156
  33.1 12.1 %copy-start.11 = (f32[4096]{0:T(1024)S(1)}, f32[4096]{0:T(1024)}, u32[]{:S(2)}) copy-start(f32[4096]{0:T(1024)} %param.34) | copy-start | bytes 49156
  35.1 7.2 %collective-permute-start.3 = (bf16[8,4096]{1,0:T(8,128)(2,1)S(1)}, bf16[8,4096]{1,0:T(8,128)(2,1)S(1)}, u32[]{:S(2)}, u32[]{:S(2)}) collective-permute-start(bf16[8,4096]{1,0:T(8,128)(2,1)S(1)} %get-tuple-element.25), channel_id=1, source_target_pairs={{0,3},{1,2},{2,1},{3,0},{4,7},{5,6},{6,5},{7,4},{8,11},{9,10},{10,... | collective-permute-start | bytes 196616 | tf_op jit(solution)/shard_map/ppermute | solution.py:359
  39.2 6.0 %collective-permute-start.2 = (bf16[8,4096]{1,0:T(8,128)(2,1)S(1)}, bf16[8,4096]{1,0:T(8,128)(2,1)S(1)}, u32[]{:S(2)}, u32[]{:S(2)}) collective-permute-start(bf16[8,4096]{1,0:T(8,128)(2,1)S(1)} %get-tuple-element.25), channel_id=1, source_target_pairs={{0,2},{1,3},{2,0},{3,1},{4,6},{5,7},{6,4},{7,5},{8,10},{9,11},{10,... | collective-permute-start | bytes 196616 | tf_op jit(solution)/shard_map/ppermute | solution.py:359
  39.2 6.0 %collective-permute-start.1 = (bf16[8,4096]{1,0:T(8,128)(2,1)S(1)}, bf16[8,4096]{1,0:T(8,128)(2,1)S(1)}, u32[]{:S(2)}, u32[]{:S(2)}) collective-permute-start(bf16[8,4096]{1,0:T(8,128)(2,1)S(1)} %get-tuple-element.25), channel_id=1, source_target_pairs={{0,1},{1,0},{2,3},{3,2},{4,5},{5,4},{6,7},{7,6},{8,9},{9,8},{10,11... | collective-permute-start | bytes 196616 | tf_op jit(solution)/shard_map/ppermute | solution.py:359
  45.3 20.3 %copy-start.3 = (bf16[4096,224]{0,1:T(8,128)(2,1)S(1)}, bf16[4096,224]{0,1:T(8,128)(2,1)}, u32[]{:S(2)}) copy-start(bf16[4096,224]{0,1:T(8,128)(2,1)} %param.36) | copy-start | bytes 5505028
  45.3 20.3 %copy-start.4 = (bf16[224,4096]{1,0:T(8,128)(2,1)S(1)}, bf16[224,4096]{1,0:T(8,128)(2,1)}, u32[]{:S(2)}) copy-start(bf16[224,4096]{1,0:T(8,128)(2,1)} %down.1) | copy-start | bytes 5505028
  46.1 19.5 %copy-start.2 = (bf16[4096,224]{0,1:T(8,128)(2,1)S(1)}, bf16[4096,224]{0,1:T(8,128)(2,1)}, u32[]{:S(2)}) copy-start(bf16[4096,224]{0,1:T(8,128)(2,1)} %param.35) | copy-start | bytes 5505028

commit v5 on v4

--- a/solution.py
+++ b/solution.py
@@ -245,9 +245,9 @@
 
 
 def feed_kernel(x, gate, up, down, out, lined):
-    a = matmul_t(x[...], gate[...])
-    b = matmul_t(x[...], up[...])
-    hidden = (a / (1.0 + jnp.exp(-a)) * b).astype(BF16)
+    a = matmul_t(gate[...], x[...])
+    b = matmul_t(up[...], x[...])
+    hidden = (a / (1.0 + jnp.exp(-a)) * b).T.astype(BF16)
     tokens = hidden.shape[0]
     tiles = lined.shape[0]
     for q in range(4):
@@ -356,7 +356,7 @@
         scratch=[pltpu.VMEM((half * heads, width), F32)],
     )(plan, back, own, other, states, out_weight)
     passed = [
-        lax.ppermute(sent, "mp", [(i, i ^ k) for i in range(ring)]) for k in range(1, ring)
+        lax.ppermute(sent, "mp", [(i, i ^ k) for i in range(ring)]) for k in (1, 3, 2)
     ]
     rest, normed = call(
         norm_kernel,

time: 89.9 us -> 91.2 us (1.014)
  blocking collectives: 66.8 us -> 69.1 us
    all_to_all x1, blocking collectives: 21.3 us -> 23.4 us  [on_device(): gathered = lax.all_to_all(down, ('group', 'mp'), 0, 0, tiled=True)]
where the time goes in v5:
time: 91.2 us; the launch traced here: 91 us
  blocking collectives  69.1 us (76%)
  Pallas kernels  11.5 us (13%)
  starting transfers between devices  5.02 us (6%)
  waiting for transfers between devices  4.46 us (5%)
    all_to_all x1, blocking collectives, on_device(): gathered = lax.all_to_all(down, ('group', 'mp'), 0, 0, tiled=True)  23.4 us
    all_to_all x1, blocking collectives, on_device(): lax.all_to_all(normed, 'group', 0, 0, tiled=True)  19.7 us
    all_to_all x1, blocking collectives, on_device(): arrived = lax.all_to_all(routed, 'group', 0, 0, tiled=True)  14.6 us
    all_to_all x1, blocking collectives, on_device(): lax.all_to_all(back.reshape(groups * depths, 16, width), ('group', 'depth...  11.4 us
    ppermute x3, starting transfers between devices, on_device(): lax.ppermute(sent, 'mp', [(i, i ^ k) for i in range(ring)])  4.95 us
    ppermute x3, waiting for transfers between devices, on_device(): lax.ppermute(sent, 'mp', [(i, i ^ k) for i in range(ring)])  4.46 us
    pallas_call x1, Pallas kernels, on_device(): call(image_kernel, jax.ShapeDtypeStruct((groups, depths, 16, width), BF16...  2.31 us
    pallas_call x1, Pallas kernels, on_device(): call(route_kernel, (jax.ShapeDtypeStruct((groups, 16, width), BF16), jax....  2.12 us
  transfers between devices with their start and end apart: 4, of which 2 were waited for; matrix products, arithmetic and copies ran while one was open for 0% of the time, Pallas kernels for 3%

profile of v5, /device:TPU:0, one launch (start us, length us, event | category | flops | bytes accessed | tf_op | source)
XLA Modules:
  0.0 91.0 jit_solution(14428770404724238634)
XLA Ops:
  0.6 0.0 copy-start.5
  0.6 0.0 copy-start.1
  0.7 0.0 copy-start
  0.7 0.0 copy-start.8
  0.7 0.0 copy-start.7
  0.7 0.0 copy-start.10
  0.7 2.1 %route.1 = (bf16[16,16,128]{2,1,0:T(8,128)(2,1)S(1)}, s32[56]{0:T(128)S(1)}) custom-call(s32[128]{0:T(128)} %slots_hbm.1, s32[16,32]{1,0:T(8,128)} %blocks_hbm.1, s32[16]{0:T(128)} %count_hbm.1, s32[16]{0:T(128)} %first_hbm.1, s32[16]{0:T(128)} %images_hbm.1, s32[16]{0:T(128)} %lengths_hbm.1, bf16[16,8,128]{2,1,0:T(8,128)(2,1)} %queries.1), custom_call_target="tpu_custom_call" | custom-call | flops 20000000000 | bytes 100000 | tf_op jit(solution)/shard_map/route/pallas_call | solution.py:305
  2.8 14.6 %all_to_all.20.arrived = bf16[16,16,128]{2,1,0:T(8,128)(2,1)S(1)} all-to-all(bf16[16,16,128]{2,1,0:T(8,128)(2,1)S(1)} %get-tuple-element.15), channel_id=1, replica_groups=mesh['group'=16,'depth'=2,'mp'=4] {'group'}, dimensions={0} | all-to-all | bytes 131072 | tf_op jit(solution)/shard_map/all_to_all | solution.py:319
  17.4 0.0 copy-done.5
  17.4 0.0 copy-done.1
  17.4 0.0 copy-done
  17.4 0.0 copy-done.8
  17.4 0.0 copy-done.7
  17.5 0.0 copy-start.9
  17.5 1.8 %text.1 = (f32[8,16,128]{2,1,0:T(8,128)S(1)}, f32[8,16,128]{2,1,0:T(8,128)S(1)}) custom-call(s32[56]{0:T(128)S(1)} %get-tuple-element.17.plan, bf16[16,8,128]{2,1,0:T(8,128)(2,1)S(1)} %copy-done.5, bf16[16,2,128]{2,1,0:T(2,128)(2,1)S(1)} %copy-done.7, bf16[16,2,128]{2,1,0:T(2,128)(2,1)S(1)} %copy-done.8, bf16[16,2,256,128]{3,2,1,0:T(8,128)(2,1)S(1)} %copy-done, ...), custom_call_target="tpu_custom_call" | custom-call | flops 200000000 | bytes 4400000 | tf_op jit(solution)/shard_map/text/pallas_call | solution.py:323
  19.3 0.1 collective-permute-start
  19.3 0.0 slice-start
  19.3 0.0 copy-done.10
  19.4 0.0 copy-done.9
  19.4 0.0 slice-start.1
  19.4 0.0 copy-start.6
  19.4 2.3 %image.1 = bf16[16,2,16,128]{3,2,1,0:T(8,128)(2,1)S(1)} custom-call(f32[8,16,128]{2,1,0:T(8,128)S(1)} %get-tuple-element.18.after.own, bf16[16,16,128]{2,1,0:T(8,128)(2,1)S(1)} %all_to_all.20.arrived, bf16[8,2,576,128]{3,2,1,0:T(8,128)(2,1)S(1)} %copy-done.9, bf16[8,2,576,128]{3,2,1,0:T(8,128)(2,1)S(1)} %copy-done.10), custom_call_target="tpu_custom_call" | custom-call | flops 10000000000 | bytes 5000000 | tf_op jit(solution)/shard_map/image/pallas_call | solution.py:333
  21.7 0.0 collective-permute-done.other
  21.7 11.4 %all_to_all.21.back = bf16[32,16,128]{2,1,0:T(8,128)(2,1)S(1)} all-to-all(bf16[32,16,128]{2,1,0:T(8,128)(2,1)S(1)} %bitcast.10), channel_id=1, replica_groups=mesh['group'=16,'depth'=2,'mp'=4] {'group','depth'}, dimensions={0} | all-to-all | bytes 262144 | tf_op jit(solution)/shard_map/all_to_all | solution.py:342
  33.1 0.0 slice-done
  33.1 0.0 slice-done.1
  33.1 0.0 copy-done.6
  33.2 0.0 copy-start.11
  33.2 2.0 %merge.1 = (bf16[8,8,128]{2,1,0:T(8,128)(2,1)}, f32[8,4096]{1,0:T(8,128)S(1)}, bf16[8,4096]{1,0:T(8,128)(2,1)S(1)}) custom-call(s32[56]{0:T(128)S(1)} %get-tuple-element.17.plan, bf16[32,16,128]{2,1,0:T(8,128)(2,1)S(1)} %all_to_all.21.back, f32[8,16,128]{2,1,0:T(8,128)S(1)} %get-tuple-element.18.after.own, f32[8,16,128]{2,1,0:T(8,128)S(1)} %collective-permute-done.other, ...), custom_call_target="tpu_custom_call" | custom-call | flops 100000000 | bytes 8800000 | tf_op jit(solution)/shard_map/merge/pallas_call | solution.py:345
  35.1 3.9 %collective-permute-start.3 = (bf16[8,4096]{1,0:T(8,128)(2,1)S(1)}, bf16[8,4096]{1,0:T(8,128)(2,1)S(1)}, u32[]{:S(2)}, u32[]{:S(2)}) collective-permute-start(bf16[8,4096]{1,0:T(8,128)(2,1)S(1)} %get-tuple-element.25), channel_id=1, source_target_pairs={{0,2},{1,3},{2,0},{3,1},{4,6},{5,7},{6,4},{7,5},{8,10},{9,11},{10,... | collective-permute-start | bytes 196616 | tf_op jit(solution)/shard_map/ppermute | solution.py:359
  39.1 0.7 collective-permute-start.2
  39.8 0.3 collective-permute-start.1
  40.1 1.3 %collective-permute-done.3.third = bf16[8,4096]{1,0:T(8,128)(2,1)S(1)} collective-permute-done((bf16[8,4096]{1,0:T(8,128)(2,1)S(1)}, bf16[8,4096]{1,0:T(8,128)(2,1)S(1)}, u32[]{:S(2)}, u32[]{:S(2)}) %collective-permute-start.3) | collective-permute-done | bytes 65568 | tf_op jit(solution)/shard_map/ppermute | solution.py:359
  41.4 3.1 %collective-permute-done.2.second = bf16[8,4096]{1,0:T(8,128)(2,1)S(1)} collective-permute-done((bf16[8,4096]{1,0:T(8,128)(2,1)S(1)}, bf16[8,4096]{1,0:T(8,128)(2,1)S(1)}, u32[]{:S(2)}, u32[]{:S(2)}) %collective-permute-start.2) | collective-permute-done | bytes 65568 | tf_op jit(solution)/shard_map/ppermute | solution.py:359
  44.6 0.0 collective-permute-done.1.first
  44.6 0.0 copy-done.11
  44.6 0.0 copy-start.3
  44.6 0.0 copy-start.4
  44.6 0.8 norm.1
  45.4 0.0 copy-start.2
  45.4 19.7 %all_to_all.22 = bf16[16,8,4096]{2,1,0:T(8,128)(2,1)S(1)} all-to-all(bf16[16,8,4096]{2,1,0:T(8,128)(2,1)S(1)} %get-tuple-element.26), channel_id=1, replica_groups=mesh['group'=16,'depth'=2,'mp'=4] {'group'}, dimensions={0} | all-to-all | bytes 2097152 | tf_op jit(solution)/shard_map/all_to_all | solution.py:372
  65.1 0.0 copy-done.3
  65.1 0.0 copy-done.4
  65.1 0.0 copy-done.2
  65.1 1.8 %feed.1 = bf16[64,8,1024]{2,1,0:T(8,128)(2,1)S(1)} custom-call(bf16[128,4096]{1,0:T(8,128)(2,1)S(1)} %bitcast.7, bf16[224,4096]{1,0:T(8,128)(2,1)S(1)} %bitcast.8, bf16[224,4096]{1,0:T(8,128)(2,1)S(1)} %bitcast.9, bf16[224,4096]{1,0:T(8,128)(2,1)S(1)} %copy-done.4), custom_call_target="tpu_custom_call" | custom-call | flops 1400000000 | bytes 7000000 | tf_op jit(solution)/shard_map/feed/pallas_call | solution.py:374
  66.9 23.4 %all_to_all.23.arrived = bf16[64,8,1024]{2,1,0:T(8,128)(2,1)S(1)} all-to-all(bf16[64,8,1024]{2,1,0:T(8,128)(2,1)S(1)} %feed.1), channel_id=1, replica_groups=mesh['group'=16,'depth'=2,'mp'=4] {'group','mp'}, dimensions={0} | all-to-all | bytes 2097152 | tf_op jit(solution)/shard_map/all_to_all | solution.py:383
  90.3 0.8 last.1
  (1 shorter events, 0.0 us)
Async XLA Ops:
  0.6 16.8 %copy-start.5 = (bf16[16,8,128]{2,1,0:T(8,128)(2,1)S(1)}, bf16[16,8,128]{2,1,0:T(8,128)(2,1)}, u32[]{:S(2)}) copy-start(bf16[16,8,128]{2,1,0:T(8,128)(2,1)} %queries.1) | copy-start | bytes 98308
  0.6 16.8 %copy-start.1 = (bf16[16,2,256,128]{3,2,1,0:T(8,128)(2,1)S(1)}, bf16[16,2,256,128]{3,2,1,0:T(8,128)(2,1)}, u32[]{:S(2)}) copy-start(bf16[16,2,256,128]{3,2,1,0:T(8,128)(2,1)} %values.2) | copy-start | bytes 6291460
  0.7 16.8 %copy-start = (bf16[16,2,256,128]{3,2,1,0:T(8,128)(2,1)S(1)}, bf16[16,2,256,128]{3,2,1,0:T(8,128)(2,1)}, u32[]{:S(2)}) copy-start(bf16[16,2,256,128]{3,2,1,0:T(8,128)(2,1)} %keys.2) | copy-start | bytes 6291460
  0.7 16.8 %copy-start.8 = (bf16[16,2,128]{2,1,0:T(2,128)(2,1)S(1)}, bf16[16,2,128]{2,1,0:T(2,128)(2,1)}, u32[]{:S(2)}) copy-start(bf16[16,2,128]{2,1,0:T(2,128)(2,1)} %new_values.1) | copy-start | bytes 24580
  0.7 16.8 %copy-start.7 = (bf16[16,2,128]{2,1,0:T(2,128)(2,1)S(1)}, bf16[16,2,128]{2,1,0:T(2,128)(2,1)}, u32[]{:S(2)}) copy-start(bf16[16,2,128]{2,1,0:T(2,128)(2,1)} %new_keys.1) | copy-start | bytes 24580
  0.7 18.7 %copy-start.10 = (bf16[8,2,576,128]{3,2,1,0:T(8,128)(2,1)S(1)}, bf16[8,2,576,128]{3,2,1,0:T(8,128)(2,1)}, u32[]{:S(2)}) copy-start(bf16[8,2,576,128]{3,2,1,0:T(8,128)(2,1)} %values.3) | copy-start | bytes 7077892
  17.5 1.9 %copy-start.9 = (bf16[8,2,576,128]{3,2,1,0:T(8,128)(2,1)S(1)}, bf16[8,2,576,128]{3,2,1,0:T(8,128)(2,1)}, u32[]{:S(2)}) copy-start(bf16[8,2,576,128]{3,2,1,0:T(8,128)(2,1)} %keys.3) | copy-start | bytes 7077892
  19.3 2.4 %collective-permute-start = (f32[8,16,128]{2,1,0:T(8,128)S(1)}, f32[8,16,128]{2,1,0:T(8,128)S(1)}, u32[]{:S(2)}, u32[]{:S(2)}) collective-permute-start(f32[8,16,128]{2,1,0:T(8,128)S(1)} %get-tuple-element.20), channel_id=1, source_target_pairs={{0,4},{4,0},{1,5},{5,1},{2,6},{6,2},{3,7},{7,3},{8,12},{12,8},{9,1... | collective-permute-start | bytes 196616 | tf_op jit(solution)/shard_map/ppermute | solution.py:331
  19.3 13.8 %slice-start = ((s8[8388608]{0:T(1024)(128)(4,1)}), s8[4194304]{0:T(1024)(128)(4,1)S(1)}, s32[]{:S(2)}) async-start(s8[8388608]{0:T(1024)(128)(4,1)} %bitcast.5), calls=%async_computation.4 | async-start | bytes 8388608
  19.4 13.8 %slice-start.1 = ((s8[8388608]{0:T(1024)(128)(4,1)}), s8[4194304]{0:T(1024)(128)(4,1)S(1)}, s32[]{:S(2)}) async-start(s8[8388608]{0:T(1024)(128)(4,1)} %bitcast.5), calls=%async_computation.5 | async-start | bytes 8388608
  19.4 13.8 %copy-start.6 = (bf16[2,4096]{1,0:T(2,128)(2,1)S(1)}, bf16[2,4096]{1,0:T(2,128)(2,1)}, u32[]{:S(2)}) copy-start(bf16[2,4096]{1,0:T(2,128)(2,1)} %states.1) | copy-start | bytes 49156
  33.2 11.4 %copy-start.11 = (f32[4096]{0:T(1024)S(1)}, f32[4096]{0:T(1024)}, u32[]{:S(2)}) copy-start(f32[4096]{0:T(1024)} %param.34) | copy-start | bytes 49156
  35.1 6.3 %collective-permute-start.3 = (bf16[8,4096]{1,0:T(8,128)(2,1)S(1)}, bf16[8,4096]{1,0:T(8,128)(2,1)S(1)}, u32[]{:S(2)}, u32[]{:S(2)}) collective-permute-start(bf16[8,4096]{1,0:T(8,128)(2,1)S(1)} %get-tuple-element.25), channel_id=1, source_target_pairs={{0,2},{1,3},{2,0},{3,1},{4,6},{5,7},{6,4},{7,5},{8,10},{9,11},{10,... | collective-permute-start | bytes 196616 | tf_op jit(solution)/shard_map/ppermute | solution.py:359
  39.1 5.5 %collective-permute-start.2 = (bf16[8,4096]{1,0:T(8,128)(2,1)S(1)}, bf16[8,4096]{1,0:T(8,128)(2,1)S(1)}, u32[]{:S(2)}, u32[]{:S(2)}) collective-permute-start(bf16[8,4096]{1,0:T(8,128)(2,1)S(1)} %get-tuple-element.25), channel_id=1, source_target_pairs={{0,3},{1,2},{2,1},{3,0},{4,7},{5,6},{6,5},{7,4},{8,11},{9,10},{10,... | collective-permute-start | bytes 196616 | tf_op jit(solution)/shard_map/ppermute | solution.py:359
  39.8 4.8 %collective-permute-start.1 = (bf16[8,4096]{1,0:T(8,128)(2,1)S(1)}, bf16[8,4096]{1,0:T(8,128)(2,1)S(1)}, u32[]{:S(2)}, u32[]{:S(2)}) collective-permute-start(bf16[8,4096]{1,0:T(8,128)(2,1)S(1)} %get-tuple-element.25), channel_id=1, source_target_pairs={{0,1},{1,0},{2,3},{3,2},{4,5},{5,4},{6,7},{7,6},{8,9},{9,8},{10,11... | collective-permute-start | bytes 196616 | tf_op jit(solution)/shard_map/ppermute | solution.py:359
  44.6 20.6 %copy-start.3 = (bf16[4096,224]{0,1:T(8,128)(2,1)S(1)}, bf16[4096,224]{0,1:T(8,128)(2,1)}, u32[]{:S(2)}) copy-start(bf16[4096,224]{0,1:T(8,128)(2,1)} %param.36) | copy-start | bytes 5505028
  44.6 20.6 %copy-start.4 = (bf16[224,4096]{1,0:T(8,128)(2,1)S(1)}, bf16[224,4096]{1,0:T(8,128)(2,1)}, u32[]{:S(2)}) copy-start(bf16[224,4096]{1,0:T(8,128)(2,1)} %down.1) | copy-start | bytes 5505028
  45.4 19.7 %copy-start.2 = (bf16[4096,224]{0,1:T(8,128)(2,1)S(1)}, bf16[4096,224]{0,1:T(8,128)(2,1)}, u32[]{:S(2)}) copy-start(bf16[4096,224]{0,1:T(8,128)(2,1)} %param.35) | copy-start | bytes 5505028

commit v6 on v5

--- a/solution.py
+++ b/solution.py
@@ -356,7 +356,7 @@
         scratch=[pltpu.VMEM((half * heads, width), F32)],
     )(plan, back, own, other, states, out_weight)
     passed = [
-        lax.ppermute(sent, "mp", [(i, i ^ k) for i in range(ring)]) for k in (1, 3, 2)
+        lax.ppermute(sent, "mp", [(i, i ^ k) for i in range(ring)]) for k in (2, 3, 1)
     ]
     rest, normed = call(
         norm_kernel,

time: 91.2 us -> 89.1 us (0.977)
  blocking collectives: 69.1 us -> 66.1 us
    all_to_all x1, blocking collectives: 23.4 us -> 20.9 us  [on_device(): gathered = lax.all_to_all(down, ('group', 'mp'), 0, 0, tiled=True)]
where the time goes in v6:
time: 89.1 us; the launch traced here: 88.9 us
  blocking collectives  66.1 us (74%)
  Pallas kernels  11.6 us (13%)
  starting transfers between devices  5.62 us (6%)
  waiting for transfers between devices  4.71 us (5%)
    all_to_all x1, blocking collectives, on_device(): gathered = lax.all_to_all(down, ('group', 'mp'), 0, 0, tiled=True)  20.9 us
    all_to_all x1, blocking collectives, on_device(): lax.all_to_all(normed, 'group', 0, 0, tiled=True)  19.2 us
    all_to_all x1, blocking collectives, on_device(): arrived = lax.all_to_all(routed, 'group', 0, 0, tiled=True)  14.6 us
    all_to_all x1, blocking collectives, on_device(): lax.all_to_all(back.reshape(groups * depths, 16, width), ('group', 'depth...  11.4 us
    ppermute x3, starting transfers between devices, on_device(): lax.ppermute(sent, 'mp', [(i, i ^ k) for i in range(ring)])  5.56 us
    ppermute x3, waiting for transfers between devices, on_device(): lax.ppermute(sent, 'mp', [(i, i ^ k) for i in range(ring)])  4.71 us
    pallas_call x1, Pallas kernels, on_device(): call(image_kernel, jax.ShapeDtypeStruct((groups, depths, 16, width), BF16...  2.31 us
    pallas_call x1, Pallas kernels, on_device(): call(route_kernel, (jax.ShapeDtypeStruct((groups, 16, width), BF16), jax....  2.12 us
  transfers between devices with their start and end apart: 4, of which 2 were waited for; matrix products, arithmetic and copies ran while one was open for 0% of the time, Pallas kernels for 3%

profile of v6, /device:TPU:0, one launch (start us, length us, event | category | flops | bytes accessed | tf_op | source)
XLA Modules:
  0.0 88.9 jit_solution(1797672255524130456)
XLA Ops:
  0.6 0.0 copy-start.5
  0.6 0.0 copy-start.1
  0.7 0.0 copy-start
  0.7 0.0 copy-start.8
  0.7 0.0 copy-start.7
  0.7 0.0 copy-start.10
  0.7 2.1 %route.1 = (bf16[16,16,128]{2,1,0:T(8,128)(2,1)S(1)}, s32[56]{0:T(128)S(1)}) custom-call(s32[128]{0:T(128)} %slots_hbm.1, s32[16,32]{1,0:T(8,128)} %blocks_hbm.1, s32[16]{0:T(128)} %count_hbm.1, s32[16]{0:T(128)} %first_hbm.1, s32[16]{0:T(128)} %images_hbm.1, s32[16]{0:T(128)} %lengths_hbm.1, bf16[16,8,128]{2,1,0:T(8,128)(2,1)} %queries.1), custom_call_target="tpu_custom_call" | custom-call | flops 20000000000 | bytes 100000 | tf_op jit(solution)/shard_map/route/pallas_call | solution.py:305
  2.8 14.6 %all_to_all.20.arrived = bf16[16,16,128]{2,1,0:T(8,128)(2,1)S(1)} all-to-all(bf16[16,16,128]{2,1,0:T(8,128)(2,1)S(1)} %get-tuple-element.15), channel_id=1, replica_groups=mesh['group'=16,'depth'=2,'mp'=4] {'group'}, dimensions={0} | all-to-all | bytes 131072 | tf_op jit(solution)/shard_map/all_to_all | solution.py:319
  17.4 0.0 copy-done.5
  17.4 0.0 copy-done.1
  17.4 0.0 copy-done
  17.4 0.0 copy-done.8
  17.4 0.0 copy-done.7
  17.4 0.0 copy-start.9
  17.5 1.8 %text.1 = (f32[8,16,128]{2,1,0:T(8,128)S(1)}, f32[8,16,128]{2,1,0:T(8,128)S(1)}) custom-call(s32[56]{0:T(128)S(1)} %get-tuple-element.17.plan, bf16[16,8,128]{2,1,0:T(8,128)(2,1)S(1)} %copy-done.5, bf16[16,2,128]{2,1,0:T(2,128)(2,1)S(1)} %copy-done.7, bf16[16,2,128]{2,1,0:T(2,128)(2,1)S(1)} %copy-done.8, bf16[16,2,256,128]{3,2,1,0:T(8,128)(2,1)S(1)} %copy-done, ...), custom_call_target="tpu_custom_call" | custom-call | flops 200000000 | bytes 4400000 | tf_op jit(solution)/shard_map/text/pallas_call | solution.py:323
  19.3 0.1 collective-permute-start
  19.3 0.0 slice-start
  19.3 0.0 copy-done.10
  19.3 0.0 copy-done.9
  19.4 0.0 slice-start.1
  19.4 0.0 copy-start.6
  19.4 2.3 %image.1 = bf16[16,2,16,128]{3,2,1,0:T(8,128)(2,1)S(1)} custom-call(f32[8,16,128]{2,1,0:T(8,128)S(1)} %get-tuple-element.18.after.own, bf16[16,16,128]{2,1,0:T(8,128)(2,1)S(1)} %all_to_all.20.arrived, bf16[8,2,576,128]{3,2,1,0:T(8,128)(2,1)S(1)} %copy-done.9, bf16[8,2,576,128]{3,2,1,0:T(8,128)(2,1)S(1)} %copy-done.10), custom_call_target="tpu_custom_call" | custom-call | flops 10000000000 | bytes 5000000 | tf_op jit(solution)/shard_map/image/pallas_call | solution.py:333
  21.7 0.0 collective-permute-done.other
  21.7 11.4 %all_to_all.21.back = bf16[32,16,128]{2,1,0:T(8,128)(2,1)S(1)} all-to-all(bf16[32,16,128]{2,1,0:T(8,128)(2,1)S(1)} %bitcast.10), channel_id=1, replica_groups=mesh['group'=16,'depth'=2,'mp'=4] {'group','depth'}, dimensions={0} | all-to-all | bytes 262144 | tf_op jit(solution)/shard_map/all_to_all | solution.py:342
  33.1 0.0 slice-done
  33.1 0.0 slice-done.1
  33.1 0.0 copy-done.6
  33.1 0.0 copy-start.11
  33.2 2.0 %merge.1 = (bf16[8,8,128]{2,1,0:T(8,128)(2,1)}, f32[8,4096]{1,0:T(8,128)S(1)}, bf16[8,4096]{1,0:T(8,128)(2,1)S(1)}) custom-call(s32[56]{0:T(128)S(1)} %get-tuple-element.17.plan, bf16[32,16,128]{2,1,0:T(8,128)(2,1)S(1)} %all_to_all.21.back, f32[8,16,128]{2,1,0:T(8,128)S(1)} %get-tuple-element.18.after.own, f32[8,16,128]{2,1,0:T(8,128)S(1)} %collective-permute-done.other, ...), custom_call_target="tpu_custom_call" | custom-call | flops 100000000 | bytes 8800000 | tf_op jit(solution)/shard_map/merge/pallas_call | solution.py:345
  35.1 2.0 %collective-permute-start.3 = (bf16[8,4096]{1,0:T(8,128)(2,1)S(1)}, bf16[8,4096]{1,0:T(8,128)(2,1)S(1)}, u32[]{:S(2)}, u32[]{:S(2)}) collective-permute-start(bf16[8,4096]{1,0:T(8,128)(2,1)S(1)} %get-tuple-element.25), channel_id=1, source_target_pairs={{0,1},{1,0},{2,3},{3,2},{4,5},{5,4},{6,7},{7,6},{8,9},{9,8},{10,11... | collective-permute-start | bytes 196616 | tf_op jit(solution)/shard_map/ppermute | solution.py:359
  37.1 2.5 %collective-permute-start.2 = (bf16[8,4096]{1,0:T(8,128)(2,1)S(1)}, bf16[8,4096]{1,0:T(8,128)(2,1)S(1)}, u32[]{:S(2)}, u32[]{:S(2)}) collective-permute-start(bf16[8,4096]{1,0:T(8,128)(2,1)S(1)} %get-tuple-element.25), channel_id=1, source_target_pairs={{0,3},{1,2},{2,1},{3,0},{4,7},{5,6},{6,5},{7,4},{8,11},{9,10},{10,... | collective-permute-start | bytes 196616 | tf_op jit(solution)/shard_map/ppermute | solution.py:359
  39.6 1.1 %collective-permute-start.1 = (bf16[8,4096]{1,0:T(8,128)(2,1)S(1)}, bf16[8,4096]{1,0:T(8,128)(2,1)S(1)}, u32[]{:S(2)}, u32[]{:S(2)}) collective-permute-start(bf16[8,4096]{1,0:T(8,128)(2,1)S(1)} %get-tuple-element.25), channel_id=1, source_target_pairs={{0,2},{1,3},{2,0},{3,1},{4,6},{5,7},{6,4},{7,5},{8,10},{9,11},{10,... | collective-permute-start | bytes 196616 | tf_op jit(solution)/shard_map/ppermute | solution.py:359
  40.7 0.0 collective-permute-done.3.third
  40.7 1.9 %collective-permute-done.2.second = bf16[8,4096]{1,0:T(8,128)(2,1)S(1)} collective-permute-done((bf16[8,4096]{1,0:T(8,128)(2,1)S(1)}, bf16[8,4096]{1,0:T(8,128)(2,1)S(1)}, u32[]{:S(2)}, u32[]{:S(2)}) %collective-permute-start.2) | collective-permute-done | bytes 65568 | tf_op jit(solution)/shard_map/ppermute | solution.py:359
  42.6 2.8 %collective-permute-done.1.first = bf16[8,4096]{1,0:T(8,128)(2,1)S(1)} collective-permute-done((bf16[8,4096]{1,0:T(8,128)(2,1)S(1)}, bf16[8,4096]{1,0:T(8,128)(2,1)S(1)}, u32[]{:S(2)}, u32[]{:S(2)}) %collective-permute-start.1) | collective-permute-done | bytes 65568 | tf_op jit(solution)/shard_map/ppermute | solution.py:359
  45.4 0.0 copy-done.11
  45.4 0.0 copy-start.3
  45.4 0.0 copy-start.4
  45.4 0.8 norm.1
  46.2 0.0 copy-start.2
  46.2 19.2 %all_to_all.22 = bf16[16,8,4096]{2,1,0:T(8,128)(2,1)S(1)} all-to-all(bf16[16,8,4096]{2,1,0:T(8,128)(2,1)S(1)} %get-tuple-element.26), channel_id=1, replica_groups=mesh['group'=16,'depth'=2,'mp'=4] {'group'}, dimensions={0} | all-to-all | bytes 2097152 | tf_op jit(solution)/shard_map/all_to_all | solution.py:372
  65.4 0.0 copy-done.3
  65.4 0.0 copy-done.4
  65.4 0.0 copy-done.2
  65.4 1.8 %feed.1 = bf16[64,8,1024]{2,1,0:T(8,128)(2,1)S(1)} custom-call(bf16[128,4096]{1,0:T(8,128)(2,1)S(1)} %bitcast.7, bf16[224,4096]{1,0:T(8,128)(2,1)S(1)} %bitcast.8, bf16[224,4096]{1,0:T(8,128)(2,1)S(1)} %bitcast.9, bf16[224,4096]{1,0:T(8,128)(2,1)S(1)} %copy-done.4), custom_call_target="tpu_custom_call" | custom-call | flops 1400000000 | bytes 7000000 | tf_op jit(solution)/shard_map/feed/pallas_call | solution.py:374
  67.2 20.9 %all_to_all.23.arrived = bf16[64,8,1024]{2,1,0:T(8,128)(2,1)S(1)} all-to-all(bf16[64,8,1024]{2,1,0:T(8,128)(2,1)S(1)} %feed.1), channel_id=1, replica_groups=mesh['group'=16,'depth'=2,'mp'=4] {'group','mp'}, dimensions={0} | all-to-all | bytes 2097152 | tf_op jit(solution)/shard_map/all_to_all | solution.py:383
  88.1 0.8 last.1
  (1 shorter events, 0.0 us)
Async XLA Ops:
  0.6 16.8 %copy-start.5 = (bf16[16,8,128]{2,1,0:T(8,128)(2,1)S(1)}, bf16[16,8,128]{2,1,0:T(8,128)(2,1)}, u32[]{:S(2)}) copy-start(bf16[16,8,128]{2,1,0:T(8,128)(2,1)} %queries.1) | copy-start | bytes 98308
  0.6 16.8 %copy-start.1 = (bf16[16,2,256,128]{3,2,1,0:T(8,128)(2,1)S(1)}, bf16[16,2,256,128]{3,2,1,0:T(8,128)(2,1)}, u32[]{:S(2)}) copy-start(bf16[16,2,256,128]{3,2,1,0:T(8,128)(2,1)} %values.2) | copy-start | bytes 6291460
  0.7 16.8 %copy-start = (bf16[16,2,256,128]{3,2,1,0:T(8,128)(2,1)S(1)}, bf16[16,2,256,128]{3,2,1,0:T(8,128)(2,1)}, u32[]{:S(2)}) copy-start(bf16[16,2,256,128]{3,2,1,0:T(8,128)(2,1)} %keys.2) | copy-start | bytes 6291460
  0.7 16.8 %copy-start.8 = (bf16[16,2,128]{2,1,0:T(2,128)(2,1)S(1)}, bf16[16,2,128]{2,1,0:T(2,128)(2,1)}, u32[]{:S(2)}) copy-start(bf16[16,2,128]{2,1,0:T(2,128)(2,1)} %new_values.1) | copy-start | bytes 24580
  0.7 16.8 %copy-start.7 = (bf16[16,2,128]{2,1,0:T(2,128)(2,1)S(1)}, bf16[16,2,128]{2,1,0:T(2,128)(2,1)}, u32[]{:S(2)}) copy-start(bf16[16,2,128]{2,1,0:T(2,128)(2,1)} %new_keys.1) | copy-start | bytes 24580
  0.7 18.7 %copy-start.10 = (bf16[8,2,576,128]{3,2,1,0:T(8,128)(2,1)S(1)}, bf16[8,2,576,128]{3,2,1,0:T(8,128)(2,1)}, u32[]{:S(2)}) copy-start(bf16[8,2,576,128]{3,2,1,0:T(8,128)(2,1)} %values.3) | copy-start | bytes 7077892
  17.4 1.9 %copy-start.9 = (bf16[8,2,576,128]{3,2,1,0:T(8,128)(2,1)S(1)}, bf16[8,2,576,128]{3,2,1,0:T(8,128)(2,1)}, u32[]{:S(2)}) copy-start(bf16[8,2,576,128]{3,2,1,0:T(8,128)(2,1)} %keys.3) | copy-start | bytes 7077892
  19.3 2.4 %collective-permute-start = (f32[8,16,128]{2,1,0:T(8,128)S(1)}, f32[8,16,128]{2,1,0:T(8,128)S(1)}, u32[]{:S(2)}, u32[]{:S(2)}) collective-permute-start(f32[8,16,128]{2,1,0:T(8,128)S(1)} %get-tuple-element.20), channel_id=1, source_target_pairs={{0,4},{4,0},{1,5},{5,1},{2,6},{6,2},{3,7},{7,3},{8,12},{12,8},{9,1... | collective-permute-start | bytes 196616 | tf_op jit(solution)/shard_map/ppermute | solution.py:331
  19.3 13.8 %slice-start = ((s8[8388608]{0:T(1024)(128)(4,1)}), s8[4194304]{0:T(1024)(128)(4,1)S(1)}, s32[]{:S(2)}) async-start(s8[8388608]{0:T(1024)(128)(4,1)} %bitcast.5), calls=%async_computation.4 | async-start | bytes 8388608
  19.4 13.8 %slice-start.1 = ((s8[8388608]{0:T(1024)(128)(4,1)}), s8[4194304]{0:T(1024)(128)(4,1)S(1)}, s32[]{:S(2)}) async-start(s8[8388608]{0:T(1024)(128)(4,1)} %bitcast.5), calls=%async_computation.5 | async-start | bytes 8388608
  19.4 13.8 %copy-start.6 = (bf16[2,4096]{1,0:T(2,128)(2,1)S(1)}, bf16[2,4096]{1,0:T(2,128)(2,1)}, u32[]{:S(2)}) copy-start(bf16[2,4096]{1,0:T(2,128)(2,1)} %states.1) | copy-start | bytes 49156
  33.1 12.3 %copy-start.11 = (f32[4096]{0:T(1024)S(1)}, f32[4096]{0:T(1024)}, u32[]{:S(2)}) copy-start(f32[4096]{0:T(1024)} %param.34) | copy-start | bytes 49156
  35.1 5.6 %collective-permute-start.3 = (bf16[8,4096]{1,0:T(8,128)(2,1)S(1)}, bf16[8,4096]{1,0:T(8,128)(2,1)S(1)}, u32[]{:S(2)}, u32[]{:S(2)}) collective-permute-start(bf16[8,4096]{1,0:T(8,128)(2,1)S(1)} %get-tuple-element.25), channel_id=1, source_target_pairs={{0,1},{1,0},{2,3},{3,2},{4,5},{5,4},{6,7},{7,6},{8,9},{9,8},{10,11... | collective-permute-start | bytes 196616 | tf_op jit(solution)/shard_map/ppermute | solution.py:359
  37.1 5.5 %collective-permute-start.2 = (bf16[8,4096]{1,0:T(8,128)(2,1)S(1)}, bf16[8,4096]{1,0:T(8,128)(2,1)S(1)}, u32[]{:S(2)}, u32[]{:S(2)}) collective-permute-start(bf16[8,4096]{1,0:T(8,128)(2,1)S(1)} %get-tuple-element.25), channel_id=1, source_target_pairs={{0,3},{1,2},{2,1},{3,0},{4,7},{5,6},{6,5},{7,4},{8,11},{9,10},{10,... | collective-permute-start | bytes 196616 | tf_op jit(solution)/shard_map/ppermute | solution.py:359
  39.6 5.8 %collective-permute-start.1 = (bf16[8,4096]{1,0:T(8,128)(2,1)S(1)}, bf16[8,4096]{1,0:T(8,128)(2,1)S(1)}, u32[]{:S(2)}, u32[]{:S(2)}) collective-permute-start(bf16[8,4096]{1,0:T(8,128)(2,1)S(1)} %get-tuple-element.25), channel_id=1, source_target_pairs={{0,2},{1,3},{2,0},{3,1},{4,6},{5,7},{6,4},{7,5},{8,10},{9,11},{10,... | collective-permute-start | bytes 196616 | tf_op jit(solution)/shard_map/ppermute | solution.py:359
  45.4 20.0 %copy-start.3 = (bf16[4096,224]{0,1:T(8,128)(2,1)S(1)}, bf16[4096,224]{0,1:T(8,128)(2,1)}, u32[]{:S(2)}) copy-start(bf16[4096,224]{0,1:T(8,128)(2,1)} %param.36) | copy-start | bytes 5505028
  45.4 20.0 %copy-start.4 = (bf16[224,4096]{1,0:T(8,128)(2,1)S(1)}, bf16[224,4096]{1,0:T(8,128)(2,1)}, u32[]{:S(2)}) copy-start(bf16[224,4096]{1,0:T(8,128)(2,1)} %down.1) | copy-start | bytes 5505028
  46.2 19.2 %copy-start.2 = (bf16[4096,224]{0,1:T(8,128)(2,1)S(1)}, bf16[4096,224]{0,1:T(8,128)(2,1)}, u32[]{:S(2)}) copy-start(bf16[4096,224]{0,1:T(8,128)(2,1)} %param.35) | copy-start | bytes 5505028

commit v7 on v6

--- a/solution.py
+++ b/solution.py
@@ -44,13 +44,10 @@
     return lax.dot_general(a, b, (((1,), (1,)), ((), ())), preferred_element_type=F32)
 
 
-OWN_DEPTH, OWN_MP, LENGTH, SOURCE = 0, 1, 8, 24
-
-
 def route_kernel(
-    slots_hbm, blocks_hbm, count_hbm, first_hbm, images_hbm, lengths_hbm, queries_hbm, out, plan, *scratch
+    slots_hbm, blocks_hbm, count_hbm, first_hbm, images_hbm, queries_hbm, out, plan, *scratch
 ):
-    slots, blocks, count, first, images, lengths, queries, sems = scratch
+    slots, blocks, count, first, images, queries, sems = scratch
     copies = [
         pltpu.make_async_copy(src, dst, sems.at[k])
         for k, (src, dst) in enumerate(
@@ -60,7 +57,6 @@
                 (count_hbm, count),
                 (blocks_hbm, blocks),
                 (slots_hbm, slots),
-                (lengths_hbm, lengths),
                 (queries_hbm, queries),
             )
         )
@@ -71,8 +67,6 @@
     requests = queries.shape[0]
     half = requests // 2
     out[...] = jnp.full(out.shape, -1.0, BF16)
-    plan[OWN_DEPTH] = depth
-    plan[OWN_MP] = lax.axis_index("mp")
     for copy in copies:
         copy.wait()
     listed = count[group]
@@ -83,12 +77,11 @@
 
     for r in range(requests):
         start, read = first[r], images[r]
-        plan[LENGTH + r] = lengths[r]
         for k in range(2):
             place = start + k
             owner, within = source(place)
             live = (k < read) & (place < listed)
-            plan[SOURCE + 2 * r + k] = jnp.where(live, owner * 2 + (place & 1), -1)
+            plan[2 * r + k] = jnp.where(live, owner * 2 + (place & 1), -1)
 
             @pl.when(live & ((place & 1) == depth))
             def _():
@@ -101,8 +94,10 @@
     return jnp.concatenate([pair[0], pair[1]], axis=1)
 
 
-def text_kernel(plan, queries, new_keys, new_values, keys, values, own, other):
-    depth = plan[OWN_DEPTH]
+def text_kernel(lengths_hbm, queries, new_keys, new_values, keys, values, own, other, lengths, sem):
+    fetch = pltpu.make_async_copy(lengths_hbm, lengths, sem)
+    fetch.start()
+    depth = lax.axis_index("depth")
     requests, heads, width = queries.shape
     half = requests // 2
     rows = requests * heads
@@ -118,7 +113,8 @@
     across = jnp.zeros((span, rows), F32)
     for p, r in enumerate(order):
         across = jnp.where(lane == p, matmul_t(side_by_side(keys[r]), both), across)
-    length = jnp.concatenate([jnp.full((heads, 1), plan[LENGTH + r]) for r in order], axis=0)
+    fetch.wait()
+    length = jnp.concatenate([jnp.full((heads, 1), lengths[r]) for r in order], axis=0)
     where = depth * span + lax.broadcasted_iota(jnp.int32, (rows, span), 1)
     allowed = where < length
     s = jnp.where(allowed, across.T * scale, MASKED)
@@ -190,7 +186,9 @@
         )
 
 
-def merge_kernel(plan, back, own, other, states, weight, out, mine, sent, joined):
+def merge_kernel(plan, back, own, other, states, weight, out, mine, sent, joined, sources, value16, sems):
+    fetch = pltpu.make_async_copy(plan, sources, sems.at[0])
+    fetch.start()
     half, heads, width = out.shape
     rows = half * heads
     parts = []
@@ -199,10 +197,12 @@
         parts.append((stats[:, 0:1], stats[:, 64:65], ref[:, 0:8, :].reshape(rows, width)))
     lane = lax.broadcasted_iota(jnp.int32, (heads, 128), 1)
     dead = jnp.where(lane < 32, MASKED, 0.0)
+    begin = 2 * half * lax.axis_index("depth")
+    fetch.wait()
     for k in range(2):
         stats, values = [], []
         for j in range(half):
-            source = plan[SOURCE + 2 * (plan[OWN_DEPTH] * half + j) + k]
+            source = sources[begin + 2 * j + k]
             at = jnp.maximum(source, 0)
             stats.append(jnp.where(source >= 0, back[at, 8:16, :].astype(F32), dead))
             values.append(back[at, 0:8, :].astype(F32))
@@ -216,12 +216,14 @@
     total = sum(f * p[1] for f, p in zip(factors, parts))
     weighted = sum(f * p[2] for f, p in zip(factors, parts))
     value = weighted / total
-    out[...] = value.astype(BF16).reshape(out.shape)
     joined[...] = value
+    value16[...] = value.astype(BF16).reshape(out.shape)
+    leave = pltpu.make_async_copy(value16, out, sems.at[1])
+    leave.start()
     flat = jnp.concatenate(
         [joined[pl.ds(h, half, stride=heads), :] for h in range(heads)], axis=1
     ).astype(BF16)
-    row = lax.broadcasted_iota(jnp.int32, (half, 1), 0) - 2 * plan[OWN_MP]
+    row = lax.broadcasted_iota(jnp.int32, (half, 1), 0) - 2 * lax.axis_index("mp")
     step = 512
     for c in range(mine.shape[1] // step):
         at = slice(c * step, (c + 1) * step)
@@ -230,13 +232,15 @@
         value = before + matmul(flat, weight[:, at])
         mine[:, at] = value
         sent[:, at] = value.astype(BF16)
-
-
-def norm_kernel(plan, mine, first, second, third, gain, rest, out):
+    leave.wait()
+
+
+def norm_kernel(mine, first, second, third, gain, rest, out):
     x = mine[...] + first[...].astype(F32) + second[...].astype(F32) + third[...].astype(F32)
+    position = lax.axis_index("mp")
     kept = x[0:2]
     for c in range(1, x.shape[0] // 2):
-        kept = jnp.where(plan[OWN_MP] == c, x[2 * c : 2 * c + 2], kept)
+        kept = jnp.where(position == c, x[2 * c : 2 * c + 2], kept)
     rest[...] = kept
     spread = jnp.mean(x * x, axis=-1, keepdims=True)
     normed = (x * lax.rsqrt(spread + NORM_EPSILON) * gain[...]).astype(BF16)
@@ -300,15 +304,15 @@
     half = requests // depths
     features = states.shape[1]
 
-    integers = (image_slot, block_list, block_count, image_first, image_count, text_length)
+    integers = (image_slot, block_list, block_count, image_first, image_count)
     in_place = [in_hbm(x) for x in (*integers, queries)]
     routed, plan = call(
         route_kernel,
         (
             jax.ShapeDtypeStruct((groups, 16, width), BF16),
-            jax.ShapeDtypeStruct((SOURCE + 2 * requests,), jnp.int32),
+            jax.ShapeDtypeStruct((2 * requests,), jnp.int32),
         ),
-        [HBM] * 7,
+        [HBM] * 6,
         20_000_000_000,
         100_000,
         "route",
@@ -317,17 +321,18 @@
         out_specs=(VMEM, SMEM),
     )(*in_place)
     arrived = lax.all_to_all(routed, "group", 0, 0, tiled=True)
-    arrived, plan = lax.optimization_barrier((arrived, plan))
+    arrived, queries = lax.optimization_barrier((arrived, queries))
 
     part = jax.ShapeDtypeStruct((half, 16, width), F32)
     own, other = call(
         text_kernel,
         (part, part),
-        [SMEM] + [VMEM] * 5,
+        [HBM] + [VMEM] * 5,
         200_000_000,
         4_400_000,
         "text",
-    )(plan, queries, new_keys, new_values, text_keys, text_values)
+        scratch=[pltpu.SMEM(text_length.shape, jnp.int32), pltpu.SemaphoreType.DMA],
+    )(in_hbm(text_length), queries, new_keys, new_values, text_keys, text_values)
     other = lax.ppermute(other, "depth", [(0, 1), (1, 0)])
 
     back = call(
@@ -349,11 +354,17 @@
             jax.ShapeDtypeStruct((half, features), F32),
             jax.ShapeDtypeStruct((half, features), BF16),
         ),
-        [SMEM] + [VMEM] * 5,
+        [VMEM] * 6,
         100_000_000,
         8_800_000,
         "merge",
-        scratch=[pltpu.VMEM((half * heads, width), F32)],
+        scratch=[
+            pltpu.VMEM((half * heads, width), F32),
+            pltpu.SMEM(plan.shape, jnp.int32),
+            pltpu.VMEM((half, heads, width), BF16),
+            pltpu.SemaphoreType.DMA((2,)),
+        ],
+        out_specs=(HBM, VMEM, VMEM),
     )(plan, back, own, other, states, out_weight)
     passed = [
         lax.ppermute(sent, "mp", [(i, i ^ k) for i in range(ring)]) for k in (2, 3, 1)
@@ -364,11 +375,11 @@
             jax.ShapeDtypeStruct((2, features), F32),
             jax.ShapeDtypeStruct((groups, half, features), BF16),
         ),
-        [SMEM] + [VMEM] * 5,
+        [VMEM] * 5,
         10_000_000_000,
         1_600_000,
         "norm",
-    )(plan, mine, *passed, norm_gain.reshape(1, features))
+    )(mine, *passed, norm_gain.reshape(1, features))
     tokens = lax.all_to_all(normed, "group", 0, 0, tiled=True).reshape(groups * half, features)
     peers = groups * ring
     down = call(

time: 89.1 us -> 88.4 us (level)
  no operation moved by 1% of the time
where the time goes in v7:
time: 88.4 us; the launch traced here: 88.2 us
  blocking collectives  66 us (75%)
  Pallas kernels  10.8 us (12%)
  starting transfers between devices  5.67 us (6%)
  waiting for transfers between devices  4.71 us (5%)
    all_to_all x1, blocking collectives, on_device(): gathered = lax.all_to_all(down, ('group', 'mp'), 0, 0, tiled=True)  20.9 us
    all_to_all x1, blocking collectives, on_device(): lax.all_to_all(normed, 'group', 0, 0, tiled=True)  19.2 us
    all_to_all x1, blocking collectives, on_device(): arrived = lax.all_to_all(routed, 'group', 0, 0, tiled=True)  14.6 us
    all_to_all x1, blocking collectives, on_device(): lax.all_to_all(back.reshape(groups * depths, 16, width), ('group', 'depth...  11.4 us
    ppermute x3, starting transfers between devices, on_device(): lax.ppermute(sent, 'mp', [(i, i ^ k) for i in range(ring)])  5.59 us
    ppermute x3, waiting for transfers between devices, on_device(): lax.ppermute(sent, 'mp', [(i, i ^ k) for i in range(ring)])  4.71 us
    pallas_call x1, Pallas kernels, on_device(): call(image_kernel, jax.ShapeDtypeStruct((groups, depths, 16, width), BF16...  2.31 us
    pallas_call x1, Pallas kernels, on_device(): call(route_kernel, (jax.ShapeDtypeStruct((groups, 16, width), BF16), jax....  2.1 us
  transfers between devices with their start and end apart: 4, of which 2 were waited for; matrix products, arithmetic and copies ran while one was open for 0% of the time, Pallas kernels for 3%

profile of v7, /device:TPU:0, one launch (start us, length us, event | category | flops | bytes accessed | tf_op | source)
XLA Modules:
  0.0 88.2 jit_solution(6637401400900996379)
XLA Ops:
  0.6 0.0 copy-start.5
  0.6 0.0 copy-start.1
  0.7 0.0 copy-start
  0.7 0.0 copy-start.8
  0.7 0.0 copy-start.7
  0.7 0.0 copy-start.10
  0.7 2.1 %route.1 = (bf16[16,16,128]{2,1,0:T(8,128)(2,1)S(1)}, s32[32]{0:T(128)S(1)}) custom-call(s32[128]{0:T(128)} %slots_hbm.1, s32[16,32]{1,0:T(8,128)} %blocks_hbm.1, s32[16]{0:T(128)} %count_hbm.1, s32[16]{0:T(128)} %first_hbm.1, s32[16]{0:T(128)} %images_hbm.1, bf16[16,8,128]{2,1,0:T(8,128)(2,1)} %queries), custom_call_target="tpu_custom_call" | custom-call | flops 20000000000 | bytes 100000 | tf_op jit(solution)/shard_map/route/pallas_call | solution.py:309
  2.8 14.6 %all_to_all.20.arrived = bf16[16,16,128]{2,1,0:T(8,128)(2,1)S(1)} all-to-all(bf16[16,16,128]{2,1,0:T(8,128)(2,1)S(1)} %get-tuple-element.16), channel_id=1, replica_groups=mesh['group'=16,'depth'=2,'mp'=4] {'group'}, dimensions={0} | all-to-all | bytes 131072 | tf_op jit(solution)/shard_map/all_to_all | solution.py:323
  17.4 0.0 copy-done.5
  17.4 0.0 copy-done.1
  17.4 0.0 copy-done
  17.4 0.0 copy-done.8
  17.4 0.0 copy-done.7
  17.4 0.0 copy-start.9
  17.4 1.6 %text.1 = (f32[8,16,128]{2,1,0:T(8,128)S(1)}, f32[8,16,128]{2,1,0:T(8,128)S(1)}) custom-call(s32[16]{0:T(128)} %lengths_hbm.1, bf16[16,8,128]{2,1,0:T(8,128)(2,1)S(1)} %copy-done.5, bf16[16,2,128]{2,1,0:T(2,128)(2,1)S(1)} %copy-done.7, bf16[16,2,128]{2,1,0:T(2,128)(2,1)S(1)} %copy-done.8, bf16[16,2,256,128]{3,2,1,0:T(8,128)(2,1)S(1)} %copy-done, ...), custom_call_target="tpu_custom_call" | custom-call | flops 200000000 | bytes 4400000 | tf_op jit(solution)/shard_map/text/pallas_call | solution.py:327
  19.0 0.1 collective-permute-start
  19.1 0.0 slice-start
  19.1 0.0 copy-done.10
  19.1 0.0 copy-done.9
  19.1 0.0 slice-start.1
  19.2 0.0 copy-start.6
  19.2 2.3 %image.1 = bf16[16,2,16,128]{3,2,1,0:T(8,128)(2,1)S(1)} custom-call(f32[8,16,128]{2,1,0:T(8,128)S(1)} %get-tuple-element.18.after.own, bf16[16,16,128]{2,1,0:T(8,128)(2,1)S(1)} %all_to_all.20.arrived, bf16[8,2,576,128]{3,2,1,0:T(8,128)(2,1)S(1)} %copy-done.9, bf16[8,2,576,128]{3,2,1,0:T(8,128)(2,1)S(1)} %copy-done.10), custom_call_target="tpu_custom_call" | custom-call | flops 10000000000 | bytes 5000000 | tf_op jit(solution)/shard_map/image/pallas_call | solution.py:338
  21.5 0.0 collective-permute-done.other
  21.5 11.4 %all_to_all.21.back = bf16[32,16,128]{2,1,0:T(8,128)(2,1)S(1)} all-to-all(bf16[32,16,128]{2,1,0:T(8,128)(2,1)S(1)} %bitcast.10), channel_id=1, replica_groups=mesh['group'=16,'depth'=2,'mp'=4] {'group','depth'}, dimensions={0} | all-to-all | bytes 262144 | tf_op jit(solution)/shard_map/all_to_all | solution.py:347
  32.9 0.0 slice-done
  32.9 0.0 slice-done.1
  32.9 0.0 copy-done.6
  32.9 0.0 copy-start.11
  32.9 2.0 %merge.1 = (bf16[8,8,128]{2,1,0:T(8,128)(2,1)}, f32[8,4096]{1,0:T(8,128)S(1)}, bf16[8,4096]{1,0:T(8,128)(2,1)S(1)}) custom-call(s32[32]{0:T(128)S(1)} %get-tuple-element.15.plan, bf16[32,16,128]{2,1,0:T(8,128)(2,1)S(1)} %all_to_all.21.back, f32[8,16,128]{2,1,0:T(8,128)S(1)} %get-tuple-element.18.after.own, f32[8,16,128]{2,1,0:T(8,128)S(1)} %collective-permute-done.other, ...), custom_call_target="tpu_custom_call" | custom-call | flops 100000000 | bytes 8800000 | tf_op jit(solution)/shard_map/merge/pallas_call | solution.py:350
  35.0 2.0 %collective-permute-start.3 = (bf16[8,4096]{1,0:T(8,128)(2,1)S(1)}, bf16[8,4096]{1,0:T(8,128)(2,1)S(1)}, u32[]{:S(2)}, u32[]{:S(2)}) collective-permute-start(bf16[8,4096]{1,0:T(8,128)(2,1)S(1)} %get-tuple-element.25), channel_id=1, source_target_pairs={{0,1},{1,0},{2,3},{3,2},{4,5},{5,4},{6,7},{7,6},{8,9},{9,8},{10,11... | collective-permute-start | bytes 196616 | tf_op jit(solution)/shard_map/ppermute | solution.py:370
  37.0 2.5 %collective-permute-start.2 = (bf16[8,4096]{1,0:T(8,128)(2,1)S(1)}, bf16[8,4096]{1,0:T(8,128)(2,1)S(1)}, u32[]{:S(2)}, u32[]{:S(2)}) collective-permute-start(bf16[8,4096]{1,0:T(8,128)(2,1)S(1)} %get-tuple-element.25), channel_id=1, source_target_pairs={{0,3},{1,2},{2,1},{3,0},{4,7},{5,6},{6,5},{7,4},{8,11},{9,10},{10,... | collective-permute-start | bytes 196616 | tf_op jit(solution)/shard_map/ppermute | solution.py:370
  39.5 1.1 %collective-permute-start.1 = (bf16[8,4096]{1,0:T(8,128)(2,1)S(1)}, bf16[8,4096]{1,0:T(8,128)(2,1)S(1)}, u32[]{:S(2)}, u32[]{:S(2)}) collective-permute-start(bf16[8,4096]{1,0:T(8,128)(2,1)S(1)} %get-tuple-element.25), channel_id=1, source_target_pairs={{0,2},{1,3},{2,0},{3,1},{4,6},{5,7},{6,4},{7,5},{8,10},{9,11},{10,... | collective-permute-start | bytes 196616 | tf_op jit(solution)/shard_map/ppermute | solution.py:370
  40.5 0.0 collective-permute-done.3.third
  40.5 1.9 %collective-permute-done.2.second = bf16[8,4096]{1,0:T(8,128)(2,1)S(1)} collective-permute-done((bf16[8,4096]{1,0:T(8,128)(2,1)S(1)}, bf16[8,4096]{1,0:T(8,128)(2,1)S(1)}, u32[]{:S(2)}, u32[]{:S(2)}) %collective-permute-start.2) | collective-permute-done | bytes 65568 | tf_op jit(solution)/shard_map/ppermute | solution.py:370
  42.4 2.8 %collective-permute-done.1.first = bf16[8,4096]{1,0:T(8,128)(2,1)S(1)} collective-permute-done((bf16[8,4096]{1,0:T(8,128)(2,1)S(1)}, bf16[8,4096]{1,0:T(8,128)(2,1)S(1)}, u32[]{:S(2)}, u32[]{:S(2)}) %collective-permute-start.1) | collective-permute-done | bytes 65568 | tf_op jit(solution)/shard_map/ppermute | solution.py:370
  45.3 0.0 copy-done.11
  45.3 0.0 copy-start.3
  45.3 0.0 copy-start.4
  45.3 0.3 norm.1
  45.5 0.0 copy-start.2
  45.5 19.2 %all_to_all.22 = bf16[16,8,4096]{2,1,0:T(8,128)(2,1)S(1)} all-to-all(bf16[16,8,4096]{2,1,0:T(8,128)(2,1)S(1)} %get-tuple-element.26), channel_id=1, replica_groups=mesh['group'=16,'depth'=2,'mp'=4] {'group'}, dimensions={0} | all-to-all | bytes 2097152 | tf_op jit(solution)/shard_map/all_to_all | solution.py:383
  64.7 0.0 copy-done.3
  64.7 0.0 copy-done.4
  64.7 0.0 copy-done.2
  64.7 1.8 %feed.1 = bf16[64,8,1024]{2,1,0:T(8,128)(2,1)S(1)} custom-call(bf16[128,4096]{1,0:T(8,128)(2,1)S(1)} %bitcast.7, bf16[224,4096]{1,0:T(8,128)(2,1)S(1)} %bitcast.8, bf16[224,4096]{1,0:T(8,128)(2,1)S(1)} %bitcast.9, bf16[224,4096]{1,0:T(8,128)(2,1)S(1)} %copy-done.4), custom_call_target="tpu_custom_call" | custom-call | flops 1400000000 | bytes 7000000 | tf_op jit(solution)/shard_map/feed/pallas_call | solution.py:385
  66.5 20.9 %all_to_all.23.arrived = bf16[64,8,1024]{2,1,0:T(8,128)(2,1)S(1)} all-to-all(bf16[64,8,1024]{2,1,0:T(8,128)(2,1)S(1)} %feed.1), channel_id=1, replica_groups=mesh['group'=16,'depth'=2,'mp'=4] {'group','mp'}, dimensions={0} | all-to-all | bytes 2097152 | tf_op jit(solution)/shard_map/all_to_all | solution.py:394
  87.4 0.8 last.1
  (1 shorter events, 0.0 us)
Async XLA Ops:
  0.6 16.8 %copy-start.5 = (bf16[16,8,128]{2,1,0:T(8,128)(2,1)S(1)}, bf16[16,8,128]{2,1,0:T(8,128)(2,1)}, u32[]{:S(2)}) copy-start(bf16[16,8,128]{2,1,0:T(8,128)(2,1)} %queries) | copy-start | bytes 98308
  0.6 16.7 %copy-start.1 = (bf16[16,2,256,128]{3,2,1,0:T(8,128)(2,1)S(1)}, bf16[16,2,256,128]{3,2,1,0:T(8,128)(2,1)}, u32[]{:S(2)}) copy-start(bf16[16,2,256,128]{3,2,1,0:T(8,128)(2,1)} %values.2) | copy-start | bytes 6291460
  0.7 16.7 %copy-start = (bf16[16,2,256,128]{3,2,1,0:T(8,128)(2,1)S(1)}, bf16[16,2,256,128]{3,2,1,0:T(8,128)(2,1)}, u32[]{:S(2)}) copy-start(bf16[16,2,256,128]{3,2,1,0:T(8,128)(2,1)} %keys.2) | copy-start | bytes 6291460
  0.7 16.7 %copy-start.8 = (bf16[16,2,128]{2,1,0:T(2,128)(2,1)S(1)}, bf16[16,2,128]{2,1,0:T(2,128)(2,1)}, u32[]{:S(2)}) copy-start(bf16[16,2,128]{2,1,0:T(2,128)(2,1)} %new_values.1) | copy-start | bytes 24580
  0.7 16.7 %copy-start.7 = (bf16[16,2,128]{2,1,0:T(2,128)(2,1)S(1)}, bf16[16,2,128]{2,1,0:T(2,128)(2,1)}, u32[]{:S(2)}) copy-start(bf16[16,2,128]{2,1,0:T(2,128)(2,1)} %new_keys.1) | copy-start | bytes 24580
  0.7 18.4 %copy-start.10 = (bf16[8,2,576,128]{3,2,1,0:T(8,128)(2,1)S(1)}, bf16[8,2,576,128]{3,2,1,0:T(8,128)(2,1)}, u32[]{:S(2)}) copy-start(bf16[8,2,576,128]{3,2,1,0:T(8,128)(2,1)} %values.3) | copy-start | bytes 7077892
  17.4 1.7 %copy-start.9 = (bf16[8,2,576,128]{3,2,1,0:T(8,128)(2,1)S(1)}, bf16[8,2,576,128]{3,2,1,0:T(8,128)(2,1)}, u32[]{:S(2)}) copy-start(bf16[8,2,576,128]{3,2,1,0:T(8,128)(2,1)} %keys.3) | copy-start | bytes 7077892
  19.0 2.5 %collective-permute-start = (f32[8,16,128]{2,1,0:T(8,128)S(1)}, f32[8,16,128]{2,1,0:T(8,128)S(1)}, u32[]{:S(2)}, u32[]{:S(2)}) collective-permute-start(f32[8,16,128]{2,1,0:T(8,128)S(1)} %get-tuple-element.20), channel_id=1, source_target_pairs={{0,4},{4,0},{1,5},{5,1},{2,6},{6,2},{3,7},{7,3},{8,12},{12,8},{9,1... | collective-permute-start | bytes 196616 | tf_op jit(solution)/shard_map/ppermute | solution.py:336
  19.1 13.8 %slice-start = ((s8[8388608]{0:T(1024)(128)(4,1)}), s8[4194304]{0:T(1024)(128)(4,1)S(1)}, s32[]{:S(2)}) async-start(s8[8388608]{0:T(1024)(128)(4,1)} %bitcast.5), calls=%async_computation.4 | async-start | bytes 8388608
  19.1 13.8 %slice-start.1 = ((s8[8388608]{0:T(1024)(128)(4,1)}), s8[4194304]{0:T(1024)(128)(4,1)S(1)}, s32[]{:S(2)}) async-start(s8[8388608]{0:T(1024)(128)(4,1)} %bitcast.5), calls=%async_computation.5 | async-start | bytes 8388608
  19.2 13.8 %copy-start.6 = (bf16[2,4096]{1,0:T(2,128)(2,1)S(1)}, bf16[2,4096]{1,0:T(2,128)(2,1)}, u32[]{:S(2)}) copy-start(bf16[2,4096]{1,0:T(2,128)(2,1)} %states.1) | copy-start | bytes 49156
  32.9 12.3 %copy-start.11 = (f32[4096]{0:T(1024)S(1)}, f32[4096]{0:T(1024)}, u32[]{:S(2)}) copy-start(f32[4096]{0:T(1024)} %param.34) | copy-start | bytes 49156
  35.0 5.6 %collective-permute-start.3 = (bf16[8,4096]{1,0:T(8,128)(2,1)S(1)}, bf16[8,4096]{1,0:T(8,128)(2,1)S(1)}, u32[]{:S(2)}, u32[]{:S(2)}) collective-permute-start(bf16[8,4096]{1,0:T(8,128)(2,1)S(1)} %get-tuple-element.25), channel_id=1, source_target_pairs={{0,1},{1,0},{2,3},{3,2},{4,5},{5,4},{6,7},{7,6},{8,9},{9,8},{10,11... | collective-permute-start | bytes 196616 | tf_op jit(solution)/shard_map/ppermute | solution.py:370
  37.0 5.5 %collective-permute-start.2 = (bf16[8,4096]{1,0:T(8,128)(2,1)S(1)}, bf16[8,4096]{1,0:T(8,128)(2,1)S(1)}, u32[]{:S(2)}, u32[]{:S(2)}) collective-permute-start(bf16[8,4096]{1,0:T(8,128)(2,1)S(1)} %get-tuple-element.25), channel_id=1, source_target_pairs={{0,3},{1,2},{2,1},{3,0},{4,7},{5,6},{6,5},{7,4},{8,11},{9,10},{10,... | collective-permute-start | bytes 196616 | tf_op jit(solution)/shard_map/ppermute | solution.py:370
  39.5 5.8 %collective-permute-start.1 = (bf16[8,4096]{1,0:T(8,128)(2,1)S(1)}, bf16[8,4096]{1,0:T(8,128)(2,1)S(1)}, u32[]{:S(2)}, u32[]{:S(2)}) collective-permute-start(bf16[8,4096]{1,0:T(8,128)(2,1)S(1)} %get-tuple-element.25), channel_id=1, source_target_pairs={{0,2},{1,3},{2,0},{3,1},{4,6},{5,7},{6,4},{7,5},{8,10},{9,11},{10,... | collective-permute-start | bytes 196616 | tf_op jit(solution)/shard_map/ppermute | solution.py:370
  45.3 19.5 %copy-start.3 = (bf16[4096,224]{0,1:T(8,128)(2,1)S(1)}, bf16[4096,224]{0,1:T(8,128)(2,1)}, u32[]{:S(2)}) copy-start(bf16[4096,224]{0,1:T(8,128)(2,1)} %param.36) | copy-start | bytes 5505028
  45.3 19.5 %copy-start.4 = (bf16[224,4096]{1,0:T(8,128)(2,1)S(1)}, bf16[224,4096]{1,0:T(8,128)(2,1)}, u32[]{:S(2)}) copy-start(bf16[224,4096]{1,0:T(8,128)(2,1)} %down.1) | copy-start | bytes 5505028
  45.5 19.2 %copy-start.2 = (bf16[4096,224]{0,1:T(8,128)(2,1)S(1)}, bf16[4096,224]{0,1:T(8,128)(2,1)}, u32[]{:S(2)}) copy-start(bf16[4096,224]{0,1:T(8,128)(2,1)} %param.35) | copy-start | bytes 5505028

commit v8 on v7

--- a/solution.py
+++ b/solution.py
@@ -81,7 +81,8 @@
             place = start + k
             owner, within = source(place)
             live = (k < read) & (place < listed)
-            plan[2 * r + k] = jnp.where(live, owner * 2 + (place & 1), -1)
+            sender = jnp.where(live, owner * 2 + (place & 1), -1)
+            plan[k, 8 * r : 8 * r + 8, :] = jnp.full((8, 128), sender, jnp.int32)
 
             @pl.when(live & ((place & 1) == depth))
             def _():
@@ -186,31 +187,27 @@
         )
 
 
-def merge_kernel(plan, back, own, other, states, weight, out, mine, sent, joined, sources, value16, sems):
-    fetch = pltpu.make_async_copy(plan, sources, sems.at[0])
-    fetch.start()
+def merge_kernel(plan, back, own, other, states, weight, out, mine, sent, joined, value16, sem):
     half, heads, width = out.shape
     rows = half * heads
     parts = []
     for ref in (own, other):
         stats = ref[:, 8:16, :].reshape(rows, 128)
         parts.append((stats[:, 0:1], stats[:, 64:65], ref[:, 0:8, :].reshape(rows, width)))
-    lane = lax.broadcasted_iota(jnp.int32, (heads, 128), 1)
-    dead = jnp.where(lane < 32, MASKED, 0.0)
-    begin = 2 * half * lax.axis_index("depth")
-    fetch.wait()
+    blocks = back[...].reshape(back.shape[0] * 16, width)
+    lane = lax.broadcasted_iota(jnp.int32, (rows, blocks.shape[0]), 1)
+    head = lax.broadcasted_iota(jnp.int32, (rows, blocks.shape[0]), 0) % heads
+    mine_at = pl.ds(pl.multiple_of(rows * lax.axis_index("depth"), rows), rows)
     for k in range(2):
-        stats, values = [], []
-        for j in range(half):
-            source = sources[begin + 2 * j + k]
-            at = jnp.maximum(source, 0)
-            stats.append(jnp.where(source >= 0, back[at, 8:16, :].astype(F32), dead))
-            values.append(back[at, 0:8, :].astype(F32))
-        stats = jnp.concatenate(stats, axis=0)
+        sender = plan[k, mine_at, :]
+        wide = jnp.concatenate([sender] * (blocks.shape[0] // 128), axis=1)
+        at = lane - wide * 16 - head
+        picks = [jnp.where(at == shift, 1.0, 0.0).astype(BF16) for shift in (0, 8)]
+        got = matmul(jnp.concatenate(picks, axis=0), blocks)
+        stats = got[rows : 2 * rows]
         total = stats[:, 64:65] + stats[:, 96:97]
-        parts.append(
-            (stats[:, 0:1] + stats[:, 32:33], total, jnp.concatenate(values, axis=0) * total)
-        )
+        level = jnp.where(sender[:, 0:1] >= 0, stats[:, 0:1] + stats[:, 32:33], MASKED)
+        parts.append((level, total, got[0:rows] * total))
     top = functools.reduce(jnp.maximum, [p[0] for p in parts])
     factors = [jnp.exp2(p[0] - top) for p in parts]
     total = sum(f * p[1] for f, p in zip(factors, parts))
@@ -218,7 +215,7 @@
     value = weighted / total
     joined[...] = value
     value16[...] = value.astype(BF16).reshape(out.shape)
-    leave = pltpu.make_async_copy(value16, out, sems.at[1])
+    leave = pltpu.make_async_copy(value16, out, sem)
     leave.start()
     flat = jnp.concatenate(
         [joined[pl.ds(h, half, stride=heads), :] for h in range(heads)], axis=1
@@ -310,7 +307,7 @@
         route_kernel,
         (
             jax.ShapeDtypeStruct((groups, 16, width), BF16),
-            jax.ShapeDtypeStruct((2 * requests,), jnp.int32),
+            jax.ShapeDtypeStruct((2, requests * heads, 128), jnp.int32),
         ),
         [HBM] * 6,
         20_000_000_000,
@@ -318,7 +315,7 @@
         "route",
         scratch=[pltpu.SMEM(i.shape, jnp.int32) for i in integers]
         + [pltpu.VMEM(queries.shape, BF16), pltpu.SemaphoreType.DMA((len(in_place),))],
-        out_specs=(VMEM, SMEM),
+        out_specs=(VMEM, VMEM),
     )(*in_place)
     arrived = lax.all_to_all(routed, "group", 0, 0, tiled=True)
     arrived, queries = lax.optimization_barrier((arrived, queries))
@@ -360,9 +357,8 @@
         "merge",
         scratch=[
             pltpu.VMEM((half * heads, width), F32),
-            pltpu.SMEM(plan.shape, jnp.int32),
             pltpu.VMEM((half, heads, width), BF16),
-            pltpu.SemaphoreType.DMA((2,)),
+            pltpu.SemaphoreType.DMA,
         ],
         out_specs=(HBM, VMEM, VMEM),
     )(plan, back, own, other, states, out_weight)

time: 88.4 us -> 87.6 us (level)
  Pallas kernels: 10.8 us -> 9.85 us
where the time goes in v8:
time: 87.6 us; the launch traced here: 87.4 us
  blocking collectives  66.2 us (76%)
  Pallas kernels  9.85 us (11%)
  starting transfers between devices  5.68 us (6%)
  waiting for transfers between devices  4.7 us (5%)
    all_to_all x1, blocking collectives, on_device(): gathered = lax.all_to_all(down, ('group', 'mp'), 0, 0, tiled=True)  20.9 us
    all_to_all x1, blocking collectives, on_device(): lax.all_to_all(normed, 'group', 0, 0, tiled=True)  19.2 us
    all_to_all x1, blocking collectives, on_device(): arrived = lax.all_to_all(routed, 'group', 0, 0, tiled=True)  14.7 us
    all_to_all x1, blocking collectives, on_device(): lax.all_to_all(back.reshape(groups * depths, 16, width), ('group', 'depth...  11.4 us
    ppermute x3, starting transfers between devices, on_device(): lax.ppermute(sent, 'mp', [(i, i ^ k) for i in range(ring)])  5.59 us
    ppermute x3, waiting for transfers between devices, on_device(): lax.ppermute(sent, 'mp', [(i, i ^ k) for i in range(ring)])  4.7 us
    pallas_call x1, Pallas kernels, on_device(): call(image_kernel, jax.ShapeDtypeStruct((groups, depths, 16, width), BF16...  2.3 us
    pallas_call x1, Pallas kernels, on_device(): call(feed_kernel, jax.ShapeDtypeStruct((peers, 8, features // 4), BF16),...  1.76 us
  transfers between devices with their start and end apart: 4, of which 2 were waited for; matrix products, arithmetic and copies ran while one was open for 0% of the time, Pallas kernels for 3%

profile of v8, /device:TPU:0, one launch (start us, length us, event | category | flops | bytes accessed | tf_op | source)
XLA Modules:
  0.0 87.4 jit_solution(9518770940649492025)
XLA Ops:
  0.6 0.0 copy-start.5
  0.6 0.0 copy-start.1
  0.7 0.0 copy-start
  0.7 0.0 copy-start.8
  0.7 0.0 copy-start.7
  0.7 0.0 copy-start.10
  0.7 1.5 %route.1 = (bf16[16,16,128]{2,1,0:T(8,128)(2,1)S(1)}, s32[2,128,128]{2,1,0:T(8,128)S(1)}) custom-call(s32[128]{0:T(128)} %slots_hbm.1, s32[16,32]{1,0:T(8,128)} %blocks_hbm.1, s32[16]{0:T(128)} %count_hbm.1, s32[16]{0:T(128)} %first_hbm.1, s32[16]{0:T(128)} %images_hbm.1, bf16[16,8,128]{2,1,0:T(8,128)(2,1)} %queries), custom_call_target="tpu_custom_call" | custom-call | flops 20000000000 | bytes 100000 | tf_op jit(solution)/shard_map/route/pallas_call | solution.py:306
  2.2 14.7 %all_to_all.20.arrived = bf16[16,16,128]{2,1,0:T(8,128)(2,1)S(1)} all-to-all(bf16[16,16,128]{2,1,0:T(8,128)(2,1)S(1)} %get-tuple-element.16), channel_id=1, replica_groups=mesh['group'=16,'depth'=2,'mp'=4] {'group'}, dimensions={0} | all-to-all | bytes 131072 | tf_op jit(solution)/shard_map/all_to_all | solution.py:320
  16.9 0.0 copy-done.5
  16.9 0.0 copy-done.1
  16.9 0.0 copy-done
  17.0 0.0 copy-done.8
  17.0 0.0 copy-done.7
  17.0 0.0 copy-start.9
  17.0 1.6 %text.1 = (f32[8,16,128]{2,1,0:T(8,128)S(1)}, f32[8,16,128]{2,1,0:T(8,128)S(1)}) custom-call(s32[16]{0:T(128)} %lengths_hbm.1, bf16[16,8,128]{2,1,0:T(8,128)(2,1)S(1)} %copy-done.5, bf16[16,2,128]{2,1,0:T(2,128)(2,1)S(1)} %copy-done.7, bf16[16,2,128]{2,1,0:T(2,128)(2,1)S(1)} %copy-done.8, bf16[16,2,256,128]{3,2,1,0:T(8,128)(2,1)S(1)} %copy-done, ...), custom_call_target="tpu_custom_call" | custom-call | flops 200000000 | bytes 4400000 | tf_op jit(solution)/shard_map/text/pallas_call | solution.py:324
  18.6 0.1 collective-permute-start
  18.7 0.0 slice-start
  18.7 0.0 copy-done.10
  18.7 0.0 copy-done.9
  18.7 0.0 slice-start.1
  18.7 0.0 copy-start.6
  18.7 2.3 %image.1 = bf16[16,2,16,128]{3,2,1,0:T(8,128)(2,1)S(1)} custom-call(f32[8,16,128]{2,1,0:T(8,128)S(1)} %get-tuple-element.18.after.own, bf16[16,16,128]{2,1,0:T(8,128)(2,1)S(1)} %all_to_all.20.arrived, bf16[8,2,576,128]{3,2,1,0:T(8,128)(2,1)S(1)} %copy-done.9, bf16[8,2,576,128]{3,2,1,0:T(8,128)(2,1)S(1)} %copy-done.10), custom_call_target="tpu_custom_call" | custom-call | flops 10000000000 | bytes 5000000 | tf_op jit(solution)/shard_map/image/pallas_call | solution.py:335
  21.0 0.0 collective-permute-done.other
  21.0 11.4 %all_to_all.21.back = bf16[32,16,128]{2,1,0:T(8,128)(2,1)S(1)} all-to-all(bf16[32,16,128]{2,1,0:T(8,128)(2,1)S(1)} %bitcast.10), channel_id=1, replica_groups=mesh['group'=16,'depth'=2,'mp'=4] {'group','depth'}, dimensions={0} | all-to-all | bytes 262144 | tf_op jit(solution)/shard_map/all_to_all | solution.py:344
  32.5 0.0 slice-done
  32.5 0.0 slice-done.1
  32.5 0.0 copy-done.6
  32.5 0.0 copy-start.11
  32.5 1.6 %merge.1 = (bf16[8,8,128]{2,1,0:T(8,128)(2,1)}, f32[8,4096]{1,0:T(8,128)S(1)}, bf16[8,4096]{1,0:T(8,128)(2,1)S(1)}) custom-call(s32[2,128,128]{2,1,0:T(8,128)S(1)} %get-tuple-element.15.plan, bf16[32,16,128]{2,1,0:T(8,128)(2,1)S(1)} %all_to_all.21.back, f32[8,16,128]{2,1,0:T(8,128)S(1)} %get-tuple-element.18.after.own, ...), custom_call_target="tpu_custom_call" | custom-call | flops 100000000 | bytes 8800000 | tf_op jit(solution)/shard_map/merge/pallas_call | solution.py:347
  34.1 2.0 %collective-permute-start.3 = (bf16[8,4096]{1,0:T(8,128)(2,1)S(1)}, bf16[8,4096]{1,0:T(8,128)(2,1)S(1)}, u32[]{:S(2)}, u32[]{:S(2)}) collective-permute-start(bf16[8,4096]{1,0:T(8,128)(2,1)S(1)} %get-tuple-element.25), channel_id=1, source_target_pairs={{0,1},{1,0},{2,3},{3,2},{4,5},{5,4},{6,7},{7,6},{8,9},{9,8},{10,11... | collective-permute-start | bytes 196616 | tf_op jit(solution)/shard_map/ppermute | solution.py:366
  36.2 2.5 %collective-permute-start.2 = (bf16[8,4096]{1,0:T(8,128)(2,1)S(1)}, bf16[8,4096]{1,0:T(8,128)(2,1)S(1)}, u32[]{:S(2)}, u32[]{:S(2)}) collective-permute-start(bf16[8,4096]{1,0:T(8,128)(2,1)S(1)} %get-tuple-element.25), channel_id=1, source_target_pairs={{0,3},{1,2},{2,1},{3,0},{4,7},{5,6},{6,5},{7,4},{8,11},{9,10},{10,... | collective-permute-start | bytes 196616 | tf_op jit(solution)/shard_map/ppermute | solution.py:366
  38.7 1.1 %collective-permute-start.1 = (bf16[8,4096]{1,0:T(8,128)(2,1)S(1)}, bf16[8,4096]{1,0:T(8,128)(2,1)S(1)}, u32[]{:S(2)}, u32[]{:S(2)}) collective-permute-start(bf16[8,4096]{1,0:T(8,128)(2,1)S(1)} %get-tuple-element.25), channel_id=1, source_target_pairs={{0,2},{1,3},{2,0},{3,1},{4,6},{5,7},{6,4},{7,5},{8,10},{9,11},{10,... | collective-permute-start | bytes 196616 | tf_op jit(solution)/shard_map/ppermute | solution.py:366
  39.7 0.0 collective-permute-done.3.third
  39.7 1.9 %collective-permute-done.2.second = bf16[8,4096]{1,0:T(8,128)(2,1)S(1)} collective-permute-done((bf16[8,4096]{1,0:T(8,128)(2,1)S(1)}, bf16[8,4096]{1,0:T(8,128)(2,1)S(1)}, u32[]{:S(2)}, u32[]{:S(2)}) %collective-permute-start.2) | collective-permute-done | bytes 65568 | tf_op jit(solution)/shard_map/ppermute | solution.py:366
  41.6 2.8 %collective-permute-done.1.first = bf16[8,4096]{1,0:T(8,128)(2,1)S(1)} collective-permute-done((bf16[8,4096]{1,0:T(8,128)(2,1)S(1)}, bf16[8,4096]{1,0:T(8,128)(2,1)S(1)}, u32[]{:S(2)}, u32[]{:S(2)}) %collective-permute-start.1) | collective-permute-done | bytes 65568 | tf_op jit(solution)/shard_map/ppermute | solution.py:366
  44.4 0.0 copy-done.11
  44.4 0.0 copy-start.3
  44.4 0.0 copy-start.4
  44.4 0.3 norm.1
  44.7 0.0 copy-start.2
  44.7 19.2 %all_to_all.22 = bf16[16,8,4096]{2,1,0:T(8,128)(2,1)S(1)} all-to-all(bf16[16,8,4096]{2,1,0:T(8,128)(2,1)S(1)} %get-tuple-element.26), channel_id=1, replica_groups=mesh['group'=16,'depth'=2,'mp'=4] {'group'}, dimensions={0} | all-to-all | bytes 2097152 | tf_op jit(solution)/shard_map/all_to_all | solution.py:379
  63.9 0.0 copy-done.3
  63.9 0.0 copy-done.4
  63.9 0.0 copy-done.2
  63.9 1.8 %feed.1 = bf16[64,8,1024]{2,1,0:T(8,128)(2,1)S(1)} custom-call(bf16[128,4096]{1,0:T(8,128)(2,1)S(1)} %bitcast.7, bf16[224,4096]{1,0:T(8,128)(2,1)S(1)} %bitcast.8, bf16[224,4096]{1,0:T(8,128)(2,1)S(1)} %bitcast.9, bf16[224,4096]{1,0:T(8,128)(2,1)S(1)} %copy-done.4), custom_call_target="tpu_custom_call" | custom-call | flops 1400000000 | bytes 7000000 | tf_op jit(solution)/shard_map/feed/pallas_call | solution.py:381
  65.7 20.9 %all_to_all.23.arrived = bf16[64,8,1024]{2,1,0:T(8,128)(2,1)S(1)} all-to-all(bf16[64,8,1024]{2,1,0:T(8,128)(2,1)S(1)} %feed.1), channel_id=1, replica_groups=mesh['group'=16,'depth'=2,'mp'=4] {'group','mp'}, dimensions={0} | all-to-all | bytes 2097152 | tf_op jit(solution)/shard_map/all_to_all | solution.py:390
  86.6 0.8 last.1
  (1 shorter events, 0.0 us)
Async XLA Ops:
  0.6 16.3 %copy-start.5 = (bf16[16,8,128]{2,1,0:T(8,128)(2,1)S(1)}, bf16[16,8,128]{2,1,0:T(8,128)(2,1)}, u32[]{:S(2)}) copy-start(bf16[16,8,128]{2,1,0:T(8,128)(2,1)} %queries) | copy-start | bytes 98308
  0.6 16.3 %copy-start.1 = (bf16[16,2,256,128]{3,2,1,0:T(8,128)(2,1)S(1)}, bf16[16,2,256,128]{3,2,1,0:T(8,128)(2,1)}, u32[]{:S(2)}) copy-start(bf16[16,2,256,128]{3,2,1,0:T(8,128)(2,1)} %values.2) | copy-start | bytes 6291460
  0.7 16.3 %copy-start = (bf16[16,2,256,128]{3,2,1,0:T(8,128)(2,1)S(1)}, bf16[16,2,256,128]{3,2,1,0:T(8,128)(2,1)}, u32[]{:S(2)}) copy-start(bf16[16,2,256,128]{3,2,1,0:T(8,128)(2,1)} %keys.2) | copy-start | bytes 6291460
  0.7 16.3 %copy-start.8 = (bf16[16,2,128]{2,1,0:T(2,128)(2,1)S(1)}, bf16[16,2,128]{2,1,0:T(2,128)(2,1)}, u32[]{:S(2)}) copy-start(bf16[16,2,128]{2,1,0:T(2,128)(2,1)} %new_values.1) | copy-start | bytes 24580
  0.7 16.3 %copy-start.7 = (bf16[16,2,128]{2,1,0:T(2,128)(2,1)S(1)}, bf16[16,2,128]{2,1,0:T(2,128)(2,1)}, u32[]{:S(2)}) copy-start(bf16[16,2,128]{2,1,0:T(2,128)(2,1)} %new_keys.1) | copy-start | bytes 24580
  0.7 18.0 %copy-start.10 = (bf16[8,2,576,128]{3,2,1,0:T(8,128)(2,1)S(1)}, bf16[8,2,576,128]{3,2,1,0:T(8,128)(2,1)}, u32[]{:S(2)}) copy-start(bf16[8,2,576,128]{3,2,1,0:T(8,128)(2,1)} %values.3) | copy-start | bytes 7077892
  17.0 1.7 %copy-start.9 = (bf16[8,2,576,128]{3,2,1,0:T(8,128)(2,1)S(1)}, bf16[8,2,576,128]{3,2,1,0:T(8,128)(2,1)}, u32[]{:S(2)}) copy-start(bf16[8,2,576,128]{3,2,1,0:T(8,128)(2,1)} %keys.3) | copy-start | bytes 7077892
  18.6 2.5 %collective-permute-start = (f32[8,16,128]{2,1,0:T(8,128)S(1)}, f32[8,16,128]{2,1,0:T(8,128)S(1)}, u32[]{:S(2)}, u32[]{:S(2)}) collective-permute-start(f32[8,16,128]{2,1,0:T(8,128)S(1)} %get-tuple-element.20), channel_id=1, source_target_pairs={{0,4},{4,0},{1,5},{5,1},{2,6},{6,2},{3,7},{7,3},{8,12},{12,8},{9,1... | collective-permute-start | bytes 196616 | tf_op jit(solution)/shard_map/ppermute | solution.py:333
  18.7 13.8 %slice-start = ((s8[8388608]{0:T(1024)(128)(4,1)}), s8[4194304]{0:T(1024)(128)(4,1)S(1)}, s32[]{:S(2)}) async-start(s8[8388608]{0:T(1024)(128)(4,1)} %bitcast.5), calls=%async_computation.4 | async-start | bytes 8388608
  18.7 13.8 %slice-start.1 = ((s8[8388608]{0:T(1024)(128)(4,1)}), s8[4194304]{0:T(1024)(128)(4,1)S(1)}, s32[]{:S(2)}) async-start(s8[8388608]{0:T(1024)(128)(4,1)} %bitcast.5), calls=%async_computation.5 | async-start | bytes 8388608
  18.7 13.7 %copy-start.6 = (bf16[2,4096]{1,0:T(2,128)(2,1)S(1)}, bf16[2,4096]{1,0:T(2,128)(2,1)}, u32[]{:S(2)}) copy-start(bf16[2,4096]{1,0:T(2,128)(2,1)} %states.1) | copy-start | bytes 49156
  32.5 12.0 %copy-start.11 = (f32[4096]{0:T(1024)S(1)}, f32[4096]{0:T(1024)}, u32[]{:S(2)}) copy-start(f32[4096]{0:T(1024)} %param.34) | copy-start | bytes 49156
  34.1 5.6 %collective-permute-start.3 = (bf16[8,4096]{1,0:T(8,128)(2,1)S(1)}, bf16[8,4096]{1,0:T(8,128)(2,1)S(1)}, u32[]{:S(2)}, u32[]{:S(2)}) collective-permute-start(bf16[8,4096]{1,0:T(8,128)(2,1)S(1)} %get-tuple-element.25), channel_id=1, source_target_pairs={{0,1},{1,0},{2,3},{3,2},{4,5},{5,4},{6,7},{7,6},{8,9},{9,8},{10,11... | collective-permute-start | bytes 196616 | tf_op jit(solution)/shard_map/ppermute | solution.py:366
  36.2 5.5 %collective-permute-start.2 = (bf16[8,4096]{1,0:T(8,128)(2,1)S(1)}, bf16[8,4096]{1,0:T(8,128)(2,1)S(1)}, u32[]{:S(2)}, u32[]{:S(2)}) collective-permute-start(bf16[8,4096]{1,0:T(8,128)(2,1)S(1)} %get-tuple-element.25), channel_id=1, source_target_pairs={{0,3},{1,2},{2,1},{3,0},{4,7},{5,6},{6,5},{7,4},{8,11},{9,10},{10,... | collective-permute-start | bytes 196616 | tf_op jit(solution)/shard_map/ppermute | solution.py:366
  38.7 5.8 %collective-permute-start.1 = (bf16[8,4096]{1,0:T(8,128)(2,1)S(1)}, bf16[8,4096]{1,0:T(8,128)(2,1)S(1)}, u32[]{:S(2)}, u32[]{:S(2)}) collective-permute-start(bf16[8,4096]{1,0:T(8,128)(2,1)S(1)} %get-tuple-element.25), channel_id=1, source_target_pairs={{0,2},{1,3},{2,0},{3,1},{4,6},{5,7},{6,4},{7,5},{8,10},{9,11},{10,... | collective-permute-start | bytes 196616 | tf_op jit(solution)/shard_map/ppermute | solution.py:366
  44.4 19.5 %copy-start.3 = (bf16[4096,224]{0,1:T(8,128)(2,1)S(1)}, bf16[4096,224]{0,1:T(8,128)(2,1)}, u32[]{:S(2)}) copy-start(bf16[4096,224]{0,1:T(8,128)(2,1)} %param.36) | copy-start | bytes 5505028
  44.4 19.5 %copy-start.4 = (bf16[224,4096]{1,0:T(8,128)(2,1)S(1)}, bf16[224,4096]{1,0:T(8,128)(2,1)}, u32[]{:S(2)}) copy-start(bf16[224,4096]{1,0:T(8,128)(2,1)} %down.1) | copy-start | bytes 5505028
  44.7 19.2 %copy-start.2 = (bf16[4096,224]{0,1:T(8,128)(2,1)S(1)}, bf16[4096,224]{0,1:T(8,128)(2,1)}, u32[]{:S(2)}) copy-start(bf16[4096,224]{0,1:T(8,128)(2,1)} %param.35) | copy-start | bytes 5505028

commit v9 on v8

--- a/solution.py
+++ b/solution.py
@@ -246,19 +246,26 @@
 
 
 def feed_kernel(x, gate, up, down, out, lined):
-    a = matmul_t(gate[...], x[...])
-    b = matmul_t(up[...], x[...])
+    units, deep = gate.shape
+    a = jnp.zeros((units, x.shape[0]), F32)
+    b = jnp.zeros((units, x.shape[0]), F32)
+    for k in range(0, deep, 256):
+        piece = x[:, k : k + 256]
+        a = a + matmul_t(gate[:, k : k + 256], piece)
+        b = b + matmul_t(up[:, k : k + 256], piece)
     hidden = (a / (1.0 + jnp.exp(-a)) * b).T.astype(BF16)
     tokens = hidden.shape[0]
-    tiles = lined.shape[0]
-    for q in range(4):
-        at = slice(q * tiles * 128, (q + 1) * tiles * 128)
-        part = matmul(hidden, down[:, at])
-        for c in range(tiles):
-            lined[c, pl.ds(q, tokens, stride=4), :] = part[:, c * 128 : (c + 1) * 128]
-    for c in range(tiles):
-        block = lined[c].astype(BF16).reshape(out.shape[0], 8, 128)
-        out[:, :, c * 128 : (c + 1) * 128] = block
+    quarter = out.shape[2]
+    for begin in range(0, quarter, 256):
+        tiles = range(begin // 128, begin // 128 + 2)
+        for q in range(4):
+            part = matmul(hidden, down[:, q * quarter + begin : q * quarter + begin + 256])
+            for c in tiles:
+                at = c * 128 - begin
+                lined[c, pl.ds(q, tokens, stride=4), :] = part[:, at : at + 128]
+        for c in tiles:
+            block = lined[c].astype(BF16).reshape(out.shape[0], 8, 128)
+            out[:, :, c * 128 : (c + 1) * 128] = block
 
 
 def last_kernel(arrived, residual, out):
@@ -352,7 +359,7 @@
             jax.ShapeDtypeStruct((half, features), BF16),
         ),
         [VMEM] * 6,
-        100_000_000,
+        10_000_000_000,
         8_800_000,
         "merge",
         scratch=[
@@ -372,7 +379,7 @@
             jax.ShapeDtypeStruct((groups, half, features), BF16),
         ),
         [VMEM] * 5,
-        10_000_000_000,
+        0,
         1_600_000,
         "norm",
     )(mine, *passed, norm_gain.reshape(1, features))

time: 87.6 us -> 87.3 us (level)
  no operation moved by 1% of the time
where the time goes in v9:
time: 87.3 us; the launch traced here: 87.1 us
  blocking collectives  65.9 us (75%)
  Pallas kernels  9.8 us (11%)
  starting transfers between devices  5.66 us (6%)
  waiting for transfers between devices  4.72 us (5%)
    all_to_all x1, blocking collectives, on_device(): gathered = lax.all_to_all(down, ('group', 'mp'), 0, 0, tiled=True)  20.9 us
    all_to_all x1, blocking collectives, on_device(): lax.all_to_all(normed, 'group', 0, 0, tiled=True)  18.9 us
    all_to_all x1, blocking collectives, on_device(): arrived = lax.all_to_all(routed, 'group', 0, 0, tiled=True)  14.8 us
    all_to_all x1, blocking collectives, on_device(): lax.all_to_all(back.reshape(groups * depths, 16, width), ('group', 'depth...  11.3 us
    ppermute x3, starting transfers between devices, on_device(): lax.ppermute(sent, 'mp', [(i, i ^ k) for i in range(ring)])  5.58 us
    ppermute x3, waiting for transfers between devices, on_device(): lax.ppermute(sent, 'mp', [(i, i ^ k) for i in range(ring)])  4.71 us
    pallas_call x1, Pallas kernels, on_device(): call(image_kernel, jax.ShapeDtypeStruct((groups, depths, 16, width), BF16...  2.3 us
  transfers between devices with their start and end apart: 4, of which 2 were waited for; matrix products, arithmetic and copies ran while one was open for 0% of the time, Pallas kernels for 3%

profile of v9, /device:TPU:0, one launch (start us, length us, event | category | flops | bytes accessed | tf_op | source)
XLA Modules:
  0.0 87.1 jit_solution(4139370053316807637)
XLA Ops:
  0.6 0.0 copy-start.5
  0.6 0.0 copy-start.1
  0.7 0.0 copy-start
  0.7 0.0 copy-start.8
  0.7 0.0 copy-start.7
  0.7 0.0 copy-start.9
  0.7 0.0 copy-start.10
  0.7 1.5 %route.1 = (bf16[16,16,128]{2,1,0:T(8,128)(2,1)S(1)}, s32[2,128,128]{2,1,0:T(8,128)S(1)}) custom-call(s32[128]{0:T(128)} %slots_hbm.1, s32[16,32]{1,0:T(8,128)} %blocks_hbm.1, s32[16]{0:T(128)} %count_hbm.1, s32[16]{0:T(128)} %first_hbm.1, s32[16]{0:T(128)} %images_hbm.1, bf16[16,8,128]{2,1,0:T(8,128)(2,1)} %queries), custom_call_target="tpu_custom_call" | custom-call | flops 20000000000 | bytes 100000 | tf_op jit(solution)/shard_map/route/pallas_call | solution.py:313
  2.2 14.8 %all_to_all.20.arrived = bf16[16,16,128]{2,1,0:T(8,128)(2,1)S(1)} all-to-all(bf16[16,16,128]{2,1,0:T(8,128)(2,1)S(1)} %get-tuple-element.16), channel_id=1, replica_groups=mesh['group'=16,'depth'=2,'mp'=4] {'group'}, dimensions={0} | all-to-all | bytes 131072 | tf_op jit(solution)/shard_map/all_to_all | solution.py:327
  17.1 0.0 copy-done.5
  17.1 0.0 copy-done.1
  17.1 0.0 copy-done
  17.1 0.0 copy-done.8
  17.1 0.0 copy-done.7
  17.1 0.0 slice-start
  17.1 1.6 %text.1 = (f32[8,16,128]{2,1,0:T(8,128)S(1)}, f32[8,16,128]{2,1,0:T(8,128)S(1)}) custom-call(s32[16]{0:T(128)} %lengths_hbm.1, bf16[16,8,128]{2,1,0:T(8,128)(2,1)S(1)} %copy-done.5, bf16[16,2,128]{2,1,0:T(2,128)(2,1)S(1)} %copy-done.7, bf16[16,2,128]{2,1,0:T(2,128)(2,1)S(1)} %copy-done.8, bf16[16,2,256,128]{3,2,1,0:T(8,128)(2,1)S(1)} %copy-done, ...), custom_call_target="tpu_custom_call" | custom-call | flops 200000000 | bytes 4400000 | tf_op jit(solution)/shard_map/text/pallas_call | solution.py:331
  18.7 0.1 collective-permute-start
  18.8 0.0 copy-done.9
  18.8 0.0 copy-done.10
  18.8 0.0 slice-start.1
  18.8 0.0 copy-start.11
  18.8 2.3 %image.1 = bf16[16,2,16,128]{3,2,1,0:T(8,128)(2,1)S(1)} custom-call(f32[8,16,128]{2,1,0:T(8,128)S(1)} %get-tuple-element.18.after.own, bf16[16,16,128]{2,1,0:T(8,128)(2,1)S(1)} %all_to_all.20.arrived, bf16[8,2,576,128]{3,2,1,0:T(8,128)(2,1)S(1)} %copy-done.9, bf16[8,2,576,128]{3,2,1,0:T(8,128)(2,1)S(1)} %copy-done.10), custom_call_target="tpu_custom_call" | custom-call | flops 10000000000 | bytes 5000000 | tf_op jit(solution)/shard_map/image/pallas_call | solution.py:342
  21.2 0.0 collective-permute-done.other
  21.2 11.3 %all_to_all.21.back = bf16[32,16,128]{2,1,0:T(8,128)(2,1)S(1)} all-to-all(bf16[32,16,128]{2,1,0:T(8,128)(2,1)S(1)} %bitcast.8), channel_id=1, replica_groups=mesh['group'=16,'depth'=2,'mp'=4] {'group','depth'}, dimensions={0} | all-to-all | bytes 262144 | tf_op jit(solution)/shard_map/all_to_all | solution.py:351
  32.5 0.0 slice-done
  32.5 0.0 slice-done.1
  32.5 0.0 copy-done.11
  32.5 0.0 copy-start.6
  32.5 0.0 copy-start.3
  32.5 0.0 copy-start.4
  32.5 1.7 %merge.1 = (bf16[8,8,128]{2,1,0:T(8,128)(2,1)}, f32[8,4096]{1,0:T(8,128)S(1)}, bf16[8,4096]{1,0:T(8,128)(2,1)S(1)}) custom-call(s32[2,128,128]{2,1,0:T(8,128)S(1)} %get-tuple-element.15.plan, bf16[32,16,128]{2,1,0:T(8,128)(2,1)S(1)} %all_to_all.21.back, f32[8,16,128]{2,1,0:T(8,128)S(1)} %get-tuple-element.18.after.own, ...), custom_call_target="tpu_custom_call" | custom-call | flops 10000000000 | bytes 8800000 | tf_op jit(solution)/shard_map/merge/pallas_call | solution.py:354
  34.2 0.0 copy-start.2
  34.2 2.0 %collective-permute-start.3 = (bf16[8,4096]{1,0:T(8,128)(2,1)S(1)}, bf16[8,4096]{1,0:T(8,128)(2,1)S(1)}, u32[]{:S(2)}, u32[]{:S(2)}) collective-permute-start(bf16[8,4096]{1,0:T(8,128)(2,1)S(1)} %get-tuple-element.25), channel_id=1, source_target_pairs={{0,1},{1,0},{2,3},{3,2},{4,5},{5,4},{6,7},{7,6},{8,9},{9,8},{10,11... | collective-permute-start | bytes 196616 | tf_op jit(solution)/shard_map/ppermute | solution.py:373
  36.2 2.5 %collective-permute-start.2 = (bf16[8,4096]{1,0:T(8,128)(2,1)S(1)}, bf16[8,4096]{1,0:T(8,128)(2,1)S(1)}, u32[]{:S(2)}, u32[]{:S(2)}) collective-permute-start(bf16[8,4096]{1,0:T(8,128)(2,1)S(1)} %get-tuple-element.25), channel_id=1, source_target_pairs={{0,3},{1,2},{2,1},{3,0},{4,7},{5,6},{6,5},{7,4},{8,11},{9,10},{10,... | collective-permute-start | bytes 196616 | tf_op jit(solution)/shard_map/ppermute | solution.py:373
  38.7 1.1 %collective-permute-start.1 = (bf16[8,4096]{1,0:T(8,128)(2,1)S(1)}, bf16[8,4096]{1,0:T(8,128)(2,1)S(1)}, u32[]{:S(2)}, u32[]{:S(2)}) collective-permute-start(bf16[8,4096]{1,0:T(8,128)(2,1)S(1)} %get-tuple-element.25), channel_id=1, source_target_pairs={{0,2},{1,3},{2,0},{3,1},{4,6},{5,7},{6,4},{7,5},{8,10},{9,11},{10,... | collective-permute-start | bytes 196616 | tf_op jit(solution)/shard_map/ppermute | solution.py:373
  39.8 0.0 collective-permute-done.3.third
  39.8 1.9 %collective-permute-done.2.second = bf16[8,4096]{1,0:T(8,128)(2,1)S(1)} collective-permute-done((bf16[8,4096]{1,0:T(8,128)(2,1)S(1)}, bf16[8,4096]{1,0:T(8,128)(2,1)S(1)}, u32[]{:S(2)}, u32[]{:S(2)}) %collective-permute-start.2) | collective-permute-done | bytes 65568 | tf_op jit(solution)/shard_map/ppermute | solution.py:373
  41.7 2.8 %collective-permute-done.1.first = bf16[8,4096]{1,0:T(8,128)(2,1)S(1)} collective-permute-done((bf16[8,4096]{1,0:T(8,128)(2,1)S(1)}, bf16[8,4096]{1,0:T(8,128)(2,1)S(1)}, u32[]{:S(2)}, u32[]{:S(2)}) %collective-permute-start.1) | collective-permute-done | bytes 65568 | tf_op jit(solution)/shard_map/ppermute | solution.py:373
  44.5 0.0 copy-done.6
  44.5 0.3 norm.1
  44.7 18.9 %all_to_all.22 = bf16[16,8,4096]{2,1,0:T(8,128)(2,1)S(1)} all-to-all(bf16[16,8,4096]{2,1,0:T(8,128)(2,1)S(1)} %get-tuple-element.26), channel_id=1, replica_groups=mesh['group'=16,'depth'=2,'mp'=4] {'group'}, dimensions={0} | all-to-all | bytes 2097152 | tf_op jit(solution)/shard_map/all_to_all | solution.py:386
  63.7 0.0 copy-done.3
  63.7 0.0 copy-done.4
  63.7 0.0 copy-done.2
  63.7 1.7 %feed.1 = bf16[64,8,1024]{2,1,0:T(8,128)(2,1)S(1)} custom-call(bf16[128,4096]{1,0:T(8,128)(2,1)S(1)} %bitcast.5, bf16[224,4096]{1,0:T(8,128)(2,1)S(1)} %bitcast.6, bf16[224,4096]{1,0:T(8,128)(2,1)S(1)} %bitcast.7, bf16[224,4096]{1,0:T(8,128)(2,1)S(1)} %copy-done.4), custom_call_target="tpu_custom_call" | custom-call | flops 1400000000 | bytes 7000000 | tf_op jit(solution)/shard_map/feed/pallas_call | solution.py:388
  65.4 20.9 %all_to_all.23.arrived = bf16[64,8,1024]{2,1,0:T(8,128)(2,1)S(1)} all-to-all(bf16[64,8,1024]{2,1,0:T(8,128)(2,1)S(1)} %feed.1), channel_id=1, replica_groups=mesh['group'=16,'depth'=2,'mp'=4] {'group','mp'}, dimensions={0} | all-to-all | bytes 2097152 | tf_op jit(solution)/shard_map/all_to_all | solution.py:397
  86.3 0.8 last.1
  (1 shorter events, 0.0 us)
Async XLA Ops:
  0.6 16.4 %copy-start.5 = (bf16[16,8,128]{2,1,0:T(8,128)(2,1)S(1)}, bf16[16,8,128]{2,1,0:T(8,128)(2,1)}, u32[]{:S(2)}) copy-start(bf16[16,8,128]{2,1,0:T(8,128)(2,1)} %queries) | copy-start | bytes 98308
  0.6 16.4 %copy-start.1 = (bf16[16,2,256,128]{3,2,1,0:T(8,128)(2,1)S(1)}, bf16[16,2,256,128]{3,2,1,0:T(8,128)(2,1)}, u32[]{:S(2)}) copy-start(bf16[16,2,256,128]{3,2,1,0:T(8,128)(2,1)} %values.2) | copy-start | bytes 6291460
  0.7 16.4 %copy-start = (bf16[16,2,256,128]{3,2,1,0:T(8,128)(2,1)S(1)}, bf16[16,2,256,128]{3,2,1,0:T(8,128)(2,1)}, u32[]{:S(2)}) copy-start(bf16[16,2,256,128]{3,2,1,0:T(8,128)(2,1)} %keys.2) | copy-start | bytes 6291460
  0.7 16.4 %copy-start.8 = (bf16[16,2,128]{2,1,0:T(2,128)(2,1)S(1)}, bf16[16,2,128]{2,1,0:T(2,128)(2,1)}, u32[]{:S(2)}) copy-start(bf16[16,2,128]{2,1,0:T(2,128)(2,1)} %new_values.1) | copy-start | bytes 24580
  0.7 16.4 %copy-start.7 = (bf16[16,2,128]{2,1,0:T(2,128)(2,1)S(1)}, bf16[16,2,128]{2,1,0:T(2,128)(2,1)}, u32[]{:S(2)}) copy-start(bf16[16,2,128]{2,1,0:T(2,128)(2,1)} %new_keys.1) | copy-start | bytes 24580
  0.7 18.1 %copy-start.9 = (bf16[8,2,576,128]{3,2,1,0:T(8,128)(2,1)S(1)}, bf16[8,2,576,128]{3,2,1,0:T(8,128)(2,1)}, u32[]{:S(2)}) copy-start(bf16[8,2,576,128]{3,2,1,0:T(8,128)(2,1)} %keys.3) | copy-start | bytes 7077892
  0.7 18.1 %copy-start.10 = (bf16[8,2,576,128]{3,2,1,0:T(8,128)(2,1)S(1)}, bf16[8,2,576,128]{3,2,1,0:T(8,128)(2,1)}, u32[]{:S(2)}) copy-start(bf16[8,2,576,128]{3,2,1,0:T(8,128)(2,1)} %values.3) | copy-start | bytes 7077892
  17.1 15.4 %slice-start = ((s8[8388608]{0:T(1024)(128)(4,1)}), s8[4194304]{0:T(1024)(128)(4,1)S(1)}, s32[]{:S(2)}) async-start(s8[8388608]{0:T(1024)(128)(4,1)} %bitcast.10), calls=%async_computation.4 | async-start | bytes 8388608
  18.7 2.5 %collective-permute-start = (f32[8,16,128]{2,1,0:T(8,128)S(1)}, f32[8,16,128]{2,1,0:T(8,128)S(1)}, u32[]{:S(2)}, u32[]{:S(2)}) collective-permute-start(f32[8,16,128]{2,1,0:T(8,128)S(1)} %get-tuple-element.20), channel_id=1, source_target_pairs={{0,4},{4,0},{1,5},{5,1},{2,6},{6,2},{3,7},{7,3},{8,12},{12,8},{9,1... | collective-permute-start | bytes 196616 | tf_op jit(solution)/shard_map/ppermute | solution.py:340
  18.8 13.6 %slice-start.1 = ((s8[8388608]{0:T(1024)(128)(4,1)}), s8[4194304]{0:T(1024)(128)(4,1)S(1)}, s32[]{:S(2)}) async-start(s8[8388608]{0:T(1024)(128)(4,1)} %bitcast.10), calls=%async_computation.5 | async-start | bytes 8388608
  18.8 13.6 %copy-start.11 = (bf16[2,4096]{1,0:T(2,128)(2,1)S(1)}, bf16[2,4096]{1,0:T(2,128)(2,1)}, u32[]{:S(2)}) copy-start(bf16[2,4096]{1,0:T(2,128)(2,1)} %states.1) | copy-start | bytes 49156
  32.5 12.0 %copy-start.6 = (f32[4096]{0:T(1024)S(1)}, f32[4096]{0:T(1024)}, u32[]{:S(2)}) copy-start(f32[4096]{0:T(1024)} %param.34) | copy-start | bytes 49156
  32.5 31.2 %copy-start.3 = (bf16[4096,224]{0,1:T(8,128)(2,1)S(1)}, bf16[4096,224]{0,1:T(8,128)(2,1)}, u32[]{:S(2)}) copy-start(bf16[4096,224]{0,1:T(8,128)(2,1)} %param.36) | copy-start | bytes 5505028
  32.5 31.2 %copy-start.4 = (bf16[224,4096]{1,0:T(8,128)(2,1)S(1)}, bf16[224,4096]{1,0:T(8,128)(2,1)}, u32[]{:S(2)}) copy-start(bf16[224,4096]{1,0:T(8,128)(2,1)} %down.1) | copy-start | bytes 5505028
  34.2 29.5 %copy-start.2 = (bf16[4096,224]{0,1:T(8,128)(2,1)S(1)}, bf16[4096,224]{0,1:T(8,128)(2,1)}, u32[]{:S(2)}) copy-start(bf16[4096,224]{0,1:T(8,128)(2,1)} %param.35) | copy-start | bytes 5505028
  34.2 5.6 %collective-permute-start.3 = (bf16[8,4096]{1,0:T(8,128)(2,1)S(1)}, bf16[8,4096]{1,0:T(8,128)(2,1)S(1)}, u32[]{:S(2)}, u32[]{:S(2)}) collective-permute-start(bf16[8,4096]{1,0:T(8,128)(2,1)S(1)} %get-tuple-element.25), channel_id=1, source_target_pairs={{0,1},{1,0},{2,3},{3,2},{4,5},{5,4},{6,7},{7,6},{8,9},{9,8},{10,11... | collective-permute-start | bytes 196616 | tf_op jit(solution)/shard_map/ppermute | solution.py:373
  36.2 5.5 %collective-permute-start.2 = (bf16[8,4096]{1,0:T(8,128)(2,1)S(1)}, bf16[8,4096]{1,0:T(8,128)(2,1)S(1)}, u32[]{:S(2)}, u32[]{:S(2)}) collective-permute-start(bf16[8,4096]{1,0:T(8,128)(2,1)S(1)} %get-tuple-element.25), channel_id=1, source_target_pairs={{0,3},{1,2},{2,1},{3,0},{4,7},{5,6},{6,5},{7,4},{8,11},{9,10},{10,... | collective-permute-start | bytes 196616 | tf_op jit(solution)/shard_map/ppermute | solution.py:373
  38.7 5.8 %collective-permute-start.1 = (bf16[8,4096]{1,0:T(8,128)(2,1)S(1)}, bf16[8,4096]{1,0:T(8,128)(2,1)S(1)}, u32[]{:S(2)}, u32[]{:S(2)}) collective-permute-start(bf16[8,4096]{1,0:T(8,128)(2,1)S(1)} %get-tuple-element.25), channel_id=1, source_target_pairs={{0,2},{1,3},{2,0},{3,1},{4,6},{5,7},{6,4},{7,5},{8,10},{9,11},{10,... | collective-permute-start | bytes 196616 | tf_op jit(solution)/shard_map/ppermute | solution.py:373

commit v10 on v9

--- a/solution.py
+++ b/solution.py
@@ -164,10 +164,9 @@
     w = jnp.exp2(s - level).astype(BF16)
     present = within[:, 0:1] >= 0.0
     total = jnp.where(present, jnp.sum(w.astype(F32), axis=-1, keepdims=True), 0.0)
-    nothing = jnp.zeros_like(w)
     o = jnp.zeros((rows, 2 * width), F32)
     for i in range(images):
-        o = o + matmul(jnp.where(within[:, 0:1] == float(i), w, nothing), side_by_side(values[i]))
+        o = jnp.where(within[:, 0:1] == float(i), matmul(w, side_by_side(values[i])), o)
     o = jnp.where(low, o[:, 0:width], o[:, width : 2 * width])
     o = o / jnp.where(present, total, 1.0)
     lane = lax.broadcasted_iota(jnp.int32, (rows, width), 1)

time: 87.3 us -> 86.5 us (level)
  transfers between devices with their start and end apart: 4 -> 4, of which waited for: 2 -> 2; matrix products, arithmetic and copies ran while one was open for 0% -> 0% of each run, Pallas kernels for 3% -> 2%
where the time goes in v10:
time: 86.5 us; the launch traced here: 86.3 us
  blocking collectives  65.9 us (76%)
  Pallas kernels  9 us (10%)
  starting transfers between devices  5.68 us (7%)
  waiting for transfers between devices  4.71 us (5%)
  between operations  0.87 us (1%)
    all_to_all x1, blocking collectives, on_device(): gathered = lax.all_to_all(down, ('group', 'mp'), 0, 0, tiled=True)  20.9 us
    all_to_all x1, blocking collectives, on_device(): lax.all_to_all(normed, 'group', 0, 0, tiled=True)  18.9 us
    all_to_all x1, blocking collectives, on_device(): arrived = lax.all_to_all(routed, 'group', 0, 0, tiled=True)  14.8 us
    all_to_all x1, blocking collectives, on_device(): lax.all_to_all(back.reshape(groups * depths, 16, width), ('group', 'depth...  11.3 us
    ppermute x3, starting transfers between devices, on_device(): lax.ppermute(sent, 'mp', [(i, i ^ k) for i in range(ring)])  5.59 us
    ppermute x3, waiting for transfers between devices, on_device(): lax.ppermute(sent, 'mp', [(i, i ^ k) for i in range(ring)])  4.71 us
  transfers between devices with their start and end apart: 4, of which 2 were waited for; matrix products, arithmetic and copies ran while one was open for 0% of the time, Pallas kernels for 2%

profile of v10, /device:TPU:0, one launch (start us, length us, event | category | flops | bytes accessed | tf_op | source)
XLA Modules:
  0.0 86.3 jit_solution(6816024366500351095)
XLA Ops:
  0.6 0.0 copy-start.5
  0.6 0.0 copy-start.1
  0.7 0.0 copy-start
  0.7 0.0 copy-start.8
  0.7 0.0 copy-start.7
  0.7 0.0 copy-start.9
  0.7 0.0 copy-start.10
  0.7 1.5 %route.1 = (bf16[16,16,128]{2,1,0:T(8,128)(2,1)S(1)}, s32[2,128,128]{2,1,0:T(8,128)S(1)}) custom-call(s32[128]{0:T(128)} %slots_hbm.1, s32[16,32]{1,0:T(8,128)} %blocks_hbm.1, s32[16]{0:T(128)} %count_hbm.1, s32[16]{0:T(128)} %first_hbm.1, s32[16]{0:T(128)} %images_hbm.1, bf16[16,8,128]{2,1,0:T(8,128)(2,1)} %queries), custom_call_target="tpu_custom_call" | custom-call | flops 20000000000 | bytes 100000 | tf_op jit(solution)/shard_map/route/pallas_call | solution.py:312
  2.2 14.8 %all_to_all.20.arrived = bf16[16,16,128]{2,1,0:T(8,128)(2,1)S(1)} all-to-all(bf16[16,16,128]{2,1,0:T(8,128)(2,1)S(1)} %get-tuple-element.16), channel_id=1, replica_groups=mesh['group'=16,'depth'=2,'mp'=4] {'group'}, dimensions={0} | all-to-all | bytes 131072 | tf_op jit(solution)/shard_map/all_to_all | solution.py:326
  17.1 0.0 copy-done.5
  17.1 0.0 copy-done.1
  17.1 0.0 copy-done
  17.1 0.0 copy-done.8
  17.1 0.0 copy-done.7
  17.1 0.0 slice-start
  17.1 1.6 %text.1 = (f32[8,16,128]{2,1,0:T(8,128)S(1)}, f32[8,16,128]{2,1,0:T(8,128)S(1)}) custom-call(s32[16]{0:T(128)} %lengths_hbm.1, bf16[16,8,128]{2,1,0:T(8,128)(2,1)S(1)} %copy-done.5, bf16[16,2,128]{2,1,0:T(2,128)(2,1)S(1)} %copy-done.7, bf16[16,2,128]{2,1,0:T(2,128)(2,1)S(1)} %copy-done.8, bf16[16,2,256,128]{3,2,1,0:T(8,128)(2,1)S(1)} %copy-done, ...), custom_call_target="tpu_custom_call" | custom-call | flops 200000000 | bytes 4400000 | tf_op jit(solution)/shard_map/text/pallas_call | solution.py:330
  18.7 0.1 collective-permute-start
  18.8 0.0 copy-done.9
  18.8 0.0 copy-done.10
  18.8 0.0 slice-start.1
  18.8 0.0 copy-start.11
  18.9 1.5 %image.1 = bf16[16,2,16,128]{3,2,1,0:T(8,128)(2,1)S(1)} custom-call(f32[8,16,128]{2,1,0:T(8,128)S(1)} %get-tuple-element.18.after.own, bf16[16,16,128]{2,1,0:T(8,128)(2,1)S(1)} %all_to_all.20.arrived, bf16[8,2,576,128]{3,2,1,0:T(8,128)(2,1)S(1)} %copy-done.9, bf16[8,2,576,128]{3,2,1,0:T(8,128)(2,1)S(1)} %copy-done.10), custom_call_target="tpu_custom_call" | custom-call | flops 10000000000 | bytes 5000000 | tf_op jit(solution)/shard_map/image/pallas_call | solution.py:341
  20.4 0.0 collective-permute-done.other
  20.4 11.3 %all_to_all.21.back = bf16[32,16,128]{2,1,0:T(8,128)(2,1)S(1)} all-to-all(bf16[32,16,128]{2,1,0:T(8,128)(2,1)S(1)} %bitcast.8), channel_id=1, replica_groups=mesh['group'=16,'depth'=2,'mp'=4] {'group','depth'}, dimensions={0} | all-to-all | bytes 262144 | tf_op jit(solution)/shard_map/all_to_all | solution.py:350
  31.7 0.0 slice-done
  31.7 0.0 slice-done.1
  31.7 0.0 copy-done.11
  31.7 0.0 copy-start.6
  31.7 0.0 copy-start.3
  31.7 0.0 copy-start.4
  31.7 1.7 %merge.1 = (bf16[8,8,128]{2,1,0:T(8,128)(2,1)}, f32[8,4096]{1,0:T(8,128)S(1)}, bf16[8,4096]{1,0:T(8,128)(2,1)S(1)}) custom-call(s32[2,128,128]{2,1,0:T(8,128)S(1)} %get-tuple-element.15.plan, bf16[32,16,128]{2,1,0:T(8,128)(2,1)S(1)} %all_to_all.21.back, f32[8,16,128]{2,1,0:T(8,128)S(1)} %get-tuple-element.18.after.own, ...), custom_call_target="tpu_custom_call" | custom-call | flops 10000000000 | bytes 8800000 | tf_op jit(solution)/shard_map/merge/pallas_call | solution.py:353
  33.4 0.0 copy-start.2
  33.4 2.0 %collective-permute-start.3 = (bf16[8,4096]{1,0:T(8,128)(2,1)S(1)}, bf16[8,4096]{1,0:T(8,128)(2,1)S(1)}, u32[]{:S(2)}, u32[]{:S(2)}) collective-permute-start(bf16[8,4096]{1,0:T(8,128)(2,1)S(1)} %get-tuple-element.25), channel_id=1, source_target_pairs={{0,1},{1,0},{2,3},{3,2},{4,5},{5,4},{6,7},{7,6},{8,9},{9,8},{10,11... | collective-permute-start | bytes 196616 | tf_op jit(solution)/shard_map/ppermute | solution.py:372
  35.4 2.5 %collective-permute-start.2 = (bf16[8,4096]{1,0:T(8,128)(2,1)S(1)}, bf16[8,4096]{1,0:T(8,128)(2,1)S(1)}, u32[]{:S(2)}, u32[]{:S(2)}) collective-permute-start(bf16[8,4096]{1,0:T(8,128)(2,1)S(1)} %get-tuple-element.25), channel_id=1, source_target_pairs={{0,3},{1,2},{2,1},{3,0},{4,7},{5,6},{6,5},{7,4},{8,11},{9,10},{10,... | collective-permute-start | bytes 196616 | tf_op jit(solution)/shard_map/ppermute | solution.py:372
  37.9 1.1 %collective-permute-start.1 = (bf16[8,4096]{1,0:T(8,128)(2,1)S(1)}, bf16[8,4096]{1,0:T(8,128)(2,1)S(1)}, u32[]{:S(2)}, u32[]{:S(2)}) collective-permute-start(bf16[8,4096]{1,0:T(8,128)(2,1)S(1)} %get-tuple-element.25), channel_id=1, source_target_pairs={{0,2},{1,3},{2,0},{3,1},{4,6},{5,7},{6,4},{7,5},{8,10},{9,11},{10,... | collective-permute-start | bytes 196616 | tf_op jit(solution)/shard_map/ppermute | solution.py:372
  39.0 0.0 collective-permute-done.3.third
  39.0 1.9 %collective-permute-done.2.second = bf16[8,4096]{1,0:T(8,128)(2,1)S(1)} collective-permute-done((bf16[8,4096]{1,0:T(8,128)(2,1)S(1)}, bf16[8,4096]{1,0:T(8,128)(2,1)S(1)}, u32[]{:S(2)}, u32[]{:S(2)}) %collective-permute-start.2) | collective-permute-done | bytes 65568 | tf_op jit(solution)/shard_map/ppermute | solution.py:372
  40.9 2.8 %collective-permute-done.1.first = bf16[8,4096]{1,0:T(8,128)(2,1)S(1)} collective-permute-done((bf16[8,4096]{1,0:T(8,128)(2,1)S(1)}, bf16[8,4096]{1,0:T(8,128)(2,1)S(1)}, u32[]{:S(2)}, u32[]{:S(2)}) %collective-permute-start.1) | collective-permute-done | bytes 65568 | tf_op jit(solution)/shard_map/ppermute | solution.py:372
  43.7 0.0 copy-done.6
  43.7 0.3 norm.1
  43.9 18.9 %all_to_all.22 = bf16[16,8,4096]{2,1,0:T(8,128)(2,1)S(1)} all-to-all(bf16[16,8,4096]{2,1,0:T(8,128)(2,1)S(1)} %get-tuple-element.26), channel_id=1, replica_groups=mesh['group'=16,'depth'=2,'mp'=4] {'group'}, dimensions={0} | all-to-all | bytes 2097152 | tf_op jit(solution)/shard_map/all_to_all | solution.py:385
  62.9 0.0 copy-done.3
  62.9 0.0 copy-done.4
  62.9 0.0 copy-done.2
  62.9 1.7 %feed.1 = bf16[64,8,1024]{2,1,0:T(8,128)(2,1)S(1)} custom-call(bf16[128,4096]{1,0:T(8,128)(2,1)S(1)} %bitcast.5, bf16[224,4096]{1,0:T(8,128)(2,1)S(1)} %bitcast.6, bf16[224,4096]{1,0:T(8,128)(2,1)S(1)} %bitcast.7, bf16[224,4096]{1,0:T(8,128)(2,1)S(1)} %copy-done.4), custom_call_target="tpu_custom_call" | custom-call | flops 1400000000 | bytes 7000000 | tf_op jit(solution)/shard_map/feed/pallas_call | solution.py:387
  64.6 20.9 %all_to_all.23.arrived = bf16[64,8,1024]{2,1,0:T(8,128)(2,1)S(1)} all-to-all(bf16[64,8,1024]{2,1,0:T(8,128)(2,1)S(1)} %feed.1), channel_id=1, replica_groups=mesh['group'=16,'depth'=2,'mp'=4] {'group','mp'}, dimensions={0} | all-to-all | bytes 2097152 | tf_op jit(solution)/shard_map/all_to_all | solution.py:396
  85.5 0.8 last.1
  (1 shorter events, 0.0 us)
Async XLA Ops:
  0.6 16.4 %copy-start.5 = (bf16[16,8,128]{2,1,0:T(8,128)(2,1)S(1)}, bf16[16,8,128]{2,1,0:T(8,128)(2,1)}, u32[]{:S(2)}) copy-start(bf16[16,8,128]{2,1,0:T(8,128)(2,1)} %queries) | copy-start | bytes 98308
  0.6 16.4 %copy-start.1 = (bf16[16,2,256,128]{3,2,1,0:T(8,128)(2,1)S(1)}, bf16[16,2,256,128]{3,2,1,0:T(8,128)(2,1)}, u32[]{:S(2)}) copy-start(bf16[16,2,256,128]{3,2,1,0:T(8,128)(2,1)} %values.2) | copy-start | bytes 6291460
  0.7 16.4 %copy-start = (bf16[16,2,256,128]{3,2,1,0:T(8,128)(2,1)S(1)}, bf16[16,2,256,128]{3,2,1,0:T(8,128)(2,1)}, u32[]{:S(2)}) copy-start(bf16[16,2,256,128]{3,2,1,0:T(8,128)(2,1)} %keys.2) | copy-start | bytes 6291460
  0.7 16.4 %copy-start.8 = (bf16[16,2,128]{2,1,0:T(2,128)(2,1)S(1)}, bf16[16,2,128]{2,1,0:T(2,128)(2,1)}, u32[]{:S(2)}) copy-start(bf16[16,2,128]{2,1,0:T(2,128)(2,1)} %new_values.1) | copy-start | bytes 24580
  0.7 16.4 %copy-start.7 = (bf16[16,2,128]{2,1,0:T(2,128)(2,1)S(1)}, bf16[16,2,128]{2,1,0:T(2,128)(2,1)}, u32[]{:S(2)}) copy-start(bf16[16,2,128]{2,1,0:T(2,128)(2,1)} %new_keys.1) | copy-start | bytes 24580
  0.7 18.1 %copy-start.9 = (bf16[8,2,576,128]{3,2,1,0:T(8,128)(2,1)S(1)}, bf16[8,2,576,128]{3,2,1,0:T(8,128)(2,1)}, u32[]{:S(2)}) copy-start(bf16[8,2,576,128]{3,2,1,0:T(8,128)(2,1)} %keys.3) | copy-start | bytes 7077892
  0.7 18.1 %copy-start.10 = (bf16[8,2,576,128]{3,2,1,0:T(8,128)(2,1)S(1)}, bf16[8,2,576,128]{3,2,1,0:T(8,128)(2,1)}, u32[]{:S(2)}) copy-start(bf16[8,2,576,128]{3,2,1,0:T(8,128)(2,1)} %values.3) | copy-start | bytes 7077892
  17.1 14.5 %slice-start = ((s8[8388608]{0:T(1024)(128)(4,1)}), s8[4194304]{0:T(1024)(128)(4,1)S(1)}, s32[]{:S(2)}) async-start(s8[8388608]{0:T(1024)(128)(4,1)} %bitcast.10), calls=%async_computation.4 | async-start | bytes 8388608
  18.7 1.7 %collective-permute-start = (f32[8,16,128]{2,1,0:T(8,128)S(1)}, f32[8,16,128]{2,1,0:T(8,128)S(1)}, u32[]{:S(2)}, u32[]{:S(2)}) collective-permute-start(f32[8,16,128]{2,1,0:T(8,128)S(1)} %get-tuple-element.20), channel_id=1, source_target_pairs={{0,4},{4,0},{1,5},{5,1},{2,6},{6,2},{3,7},{7,3},{8,12},{12,8},{9,1... | collective-permute-start | bytes 196616 | tf_op jit(solution)/shard_map/ppermute | solution.py:339
  18.8 12.8 %slice-start.1 = ((s8[8388608]{0:T(1024)(128)(4,1)}), s8[4194304]{0:T(1024)(128)(4,1)S(1)}, s32[]{:S(2)}) async-start(s8[8388608]{0:T(1024)(128)(4,1)} %bitcast.10), calls=%async_computation.5 | async-start | bytes 8388608
  18.8 12.8 %copy-start.11 = (bf16[2,4096]{1,0:T(2,128)(2,1)S(1)}, bf16[2,4096]{1,0:T(2,128)(2,1)}, u32[]{:S(2)}) copy-start(bf16[2,4096]{1,0:T(2,128)(2,1)} %states.1) | copy-start | bytes 49156
  31.7 12.0 %copy-start.6 = (f32[4096]{0:T(1024)S(1)}, f32[4096]{0:T(1024)}, u32[]{:S(2)}) copy-start(f32[4096]{0:T(1024)} %param.34) | copy-start | bytes 49156
  31.7 31.2 %copy-start.3 = (bf16[4096,224]{0,1:T(8,128)(2,1)S(1)}, bf16[4096,224]{0,1:T(8,128)(2,1)}, u32[]{:S(2)}) copy-start(bf16[4096,224]{0,1:T(8,128)(2,1)} %param.36) | copy-start | bytes 5505028
  31.7 31.2 %copy-start.4 = (bf16[224,4096]{1,0:T(8,128)(2,1)S(1)}, bf16[224,4096]{1,0:T(8,128)(2,1)}, u32[]{:S(2)}) copy-start(bf16[224,4096]{1,0:T(8,128)(2,1)} %down.1) | copy-start | bytes 5505028
  33.4 29.5 %copy-start.2 = (bf16[4096,224]{0,1:T(8,128)(2,1)S(1)}, bf16[4096,224]{0,1:T(8,128)(2,1)}, u32[]{:S(2)}) copy-start(bf16[4096,224]{0,1:T(8,128)(2,1)} %param.35) | copy-start | bytes 5505028
  33.4 5.6 %collective-permute-start.3 = (bf16[8,4096]{1,0:T(8,128)(2,1)S(1)}, bf16[8,4096]{1,0:T(8,128)(2,1)S(1)}, u32[]{:S(2)}, u32[]{:S(2)}) collective-permute-start(bf16[8,4096]{1,0:T(8,128)(2,1)S(1)} %get-tuple-element.25), channel_id=1, source_target_pairs={{0,1},{1,0},{2,3},{3,2},{4,5},{5,4},{6,7},{7,6},{8,9},{9,8},{10,11... | collective-permute-start | bytes 196616 | tf_op jit(solution)/shard_map/ppermute | solution.py:372
  35.4 5.5 %collective-permute-start.2 = (bf16[8,4096]{1,0:T(8,128)(2,1)S(1)}, bf16[8,4096]{1,0:T(8,128)(2,1)S(1)}, u32[]{:S(2)}, u32[]{:S(2)}) collective-permute-start(bf16[8,4096]{1,0:T(8,128)(2,1)S(1)} %get-tuple-element.25), channel_id=1, source_target_pairs={{0,3},{1,2},{2,1},{3,0},{4,7},{5,6},{6,5},{7,4},{8,11},{9,10},{10,... | collective-permute-start | bytes 196616 | tf_op jit(solution)/shard_map/ppermute | solution.py:372
  37.9 5.8 %collective-permute-start.1 = (bf16[8,4096]{1,0:T(8,128)(2,1)S(1)}, bf16[8,4096]{1,0:T(8,128)(2,1)S(1)}, u32[]{:S(2)}, u32[]{:S(2)}) collective-permute-start(bf16[8,4096]{1,0:T(8,128)(2,1)S(1)} %get-tuple-element.25), channel_id=1, source_target_pairs={{0,2},{1,3},{2,0},{3,1},{4,6},{5,7},{6,4},{7,5},{8,10},{9,11},{10,... | collective-permute-start | bytes 196616 | tf_op jit(solution)/shard_map/ppermute | solution.py:372

commit v11 on v10

--- a/solution.py
+++ b/solution.py
@@ -154,16 +154,24 @@
     low = lax.broadcasted_iota(jnp.int32, (rows, 1), 0) % 8 < 4
     zero = jnp.zeros_like(q)
     both = jnp.concatenate([jnp.where(low, q, zero), jnp.where(low, zero, q)], axis=1)
-    across = jnp.zeros((patches, rows), F32)
-    for i in range(images):
-        across = jnp.where(
-            within_lane == float(i), matmul_t(side_by_side(keys[i]), both), across
-        )
-    s = across.T * scale
-    level = jnp.floor(jnp.max(s, axis=-1, keepdims=True))
-    w = jnp.exp2(s - level).astype(BF16)
+    pieces = []
+    for begin in range(0, patches, patches // 4):
+        at = slice(begin, begin + patches // 4)
+        piece = jnp.zeros((patches // 4, rows), F32)
+        for i in range(images):
+            pair = jnp.concatenate([keys[i, 0, at, :], keys[i, 1, at, :]], axis=1)
+            piece = jnp.where(within_lane == float(i), matmul_t(pair, both), piece)
+        pieces.append(piece * scale)
+    tops = [jnp.max(piece, axis=0, keepdims=True) for piece in pieces]
+    level = jnp.floor(functools.reduce(jnp.maximum, tops))
+    parts = [jnp.exp2(piece - level).astype(BF16) for piece in pieces]
+    total = sum(jnp.sum(part.astype(F32), axis=0, keepdims=True) for part in parts)
+    w = jnp.concatenate(parts, axis=0).T
+    side = lax.broadcasted_iota(jnp.int32, (width, rows), 0)
+    columns = jnp.where(side < 64, level, total).T
     present = within[:, 0:1] >= 0.0
-    total = jnp.where(present, jnp.sum(w.astype(F32), axis=-1, keepdims=True), 0.0)
+    level = columns[:, 0:1]
+    total = jnp.where(present, columns[:, 64:65], 0.0)
     o = jnp.zeros((rows, 2 * width), F32)
     for i in range(images):
         o = jnp.where(within[:, 0:1] == float(i), matmul(w, side_by_side(values[i])), o)

time: 86.5 us -> 86.5 us (level)
  no operation moved by 1% of the time
where the time goes in v11:
time: 86.5 us; the launch traced here: 86.2 us
  blocking collectives  65.9 us (76%)
  Pallas kernels  8.98 us (10%)
  starting transfers between devices  5.66 us (7%)
  waiting for transfers between devices  4.71 us (5%)
  between operations  0.87 us (1%)
    all_to_all x1, blocking collectives, on_device(): gathered = lax.all_to_all(down, ('group', 'mp'), 0, 0, tiled=True)  20.9 us
    all_to_all x1, blocking collectives, on_device(): lax.all_to_all(normed, 'group', 0, 0, tiled=True)  18.9 us
    all_to_all x1, blocking collectives, on_device(): arrived = lax.all_to_all(routed, 'group', 0, 0, tiled=True)  14.8 us
    all_to_all x1, blocking collectives, on_device(): lax.all_to_all(back.reshape(groups * depths, 16, width), ('group', 'depth...  11.3 us
    ppermute x3, starting transfers between devices, on_device(): lax.ppermute(sent, 'mp', [(i, i ^ k) for i in range(ring)])  5.58 us
    ppermute x3, waiting for transfers between devices, on_device(): lax.ppermute(sent, 'mp', [(i, i ^ k) for i in range(ring)])  4.7 us
  transfers between devices with their start and end apart: 4, of which 2 were waited for; matrix products, arithmetic and copies ran while one was open for 0% of the time, Pallas kernels for 2%

profile of v11, /device:TPU:0, one launch (start us, length us, event | category | flops | bytes accessed | tf_op | source)
XLA Modules:
  0.0 86.2 jit_solution(15687269725758067707)
XLA Ops:
  0.6 0.0 copy-start.5
  0.6 0.0 copy-start.1
  0.7 0.0 copy-start
  0.7 0.0 copy-start.8
  0.7 0.0 copy-start.7
  0.7 0.0 copy-start.9
  0.7 0.0 copy-start.10
  0.7 1.5 %route.1 = (bf16[16,16,128]{2,1,0:T(8,128)(2,1)S(1)}, s32[2,128,128]{2,1,0:T(8,128)S(1)}) custom-call(s32[128]{0:T(128)} %slots_hbm.1, s32[16,32]{1,0:T(8,128)} %blocks_hbm.1, s32[16]{0:T(128)} %count_hbm.1, s32[16]{0:T(128)} %first_hbm.1, s32[16]{0:T(128)} %images_hbm.1, bf16[16,8,128]{2,1,0:T(8,128)(2,1)} %queries), custom_call_target="tpu_custom_call" | custom-call | flops 20000000000 | bytes 100000 | tf_op jit(solution)/shard_map/route/pallas_call | solution.py:320
  2.2 14.8 %all_to_all.20.arrived = bf16[16,16,128]{2,1,0:T(8,128)(2,1)S(1)} all-to-all(bf16[16,16,128]{2,1,0:T(8,128)(2,1)S(1)} %get-tuple-element.16), channel_id=1, replica_groups=mesh['group'=16,'depth'=2,'mp'=4] {'group'}, dimensions={0} | all-to-all | bytes 131072 | tf_op jit(solution)/shard_map/all_to_all | solution.py:334
  17.1 0.0 copy-done.5
  17.1 0.0 copy-done.1
  17.1 0.0 copy-done
  17.1 0.0 copy-done.8
  17.1 0.0 copy-done.7
  17.1 0.0 slice-start
  17.1 1.6 %text.1 = (f32[8,16,128]{2,1,0:T(8,128)S(1)}, f32[8,16,128]{2,1,0:T(8,128)S(1)}) custom-call(s32[16]{0:T(128)} %lengths_hbm.1, bf16[16,8,128]{2,1,0:T(8,128)(2,1)S(1)} %copy-done.5, bf16[16,2,128]{2,1,0:T(2,128)(2,1)S(1)} %copy-done.7, bf16[16,2,128]{2,1,0:T(2,128)(2,1)S(1)} %copy-done.8, bf16[16,2,256,128]{3,2,1,0:T(8,128)(2,1)S(1)} %copy-done, ...), custom_call_target="tpu_custom_call" | custom-call | flops 200000000 | bytes 4400000 | tf_op jit(solution)/shard_map/text/pallas_call | solution.py:338
  18.7 0.1 collective-permute-start
  18.8 0.0 copy-done.9
  18.8 0.0 copy-done.10
  18.8 0.0 slice-start.1
  18.8 0.0 copy-start.11
  18.9 1.5 %image.1 = bf16[16,2,16,128]{3,2,1,0:T(8,128)(2,1)S(1)} custom-call(f32[8,16,128]{2,1,0:T(8,128)S(1)} %get-tuple-element.18.after.own, bf16[16,16,128]{2,1,0:T(8,128)(2,1)S(1)} %all_to_all.20.arrived, bf16[8,2,576,128]{3,2,1,0:T(8,128)(2,1)S(1)} %copy-done.9, bf16[8,2,576,128]{3,2,1,0:T(8,128)(2,1)S(1)} %copy-done.10), custom_call_target="tpu_custom_call" | custom-call | flops 10000000000 | bytes 5000000 | tf_op jit(solution)/shard_map/image/pallas_call | solution.py:349
  20.3 0.0 collective-permute-done.other
  20.3 11.3 %all_to_all.21.back = bf16[32,16,128]{2,1,0:T(8,128)(2,1)S(1)} all-to-all(bf16[32,16,128]{2,1,0:T(8,128)(2,1)S(1)} %bitcast.8), channel_id=1, replica_groups=mesh['group'=16,'depth'=2,'mp'=4] {'group','depth'}, dimensions={0} | all-to-all | bytes 262144 | tf_op jit(solution)/shard_map/all_to_all | solution.py:358
  31.6 0.0 slice-done
  31.6 0.0 slice-done.1
  31.6 0.0 copy-done.11
  31.6 0.0 copy-start.6
  31.7 0.0 copy-start.3
  31.7 0.0 copy-start.4
  31.7 1.7 %merge.1 = (bf16[8,8,128]{2,1,0:T(8,128)(2,1)}, f32[8,4096]{1,0:T(8,128)S(1)}, bf16[8,4096]{1,0:T(8,128)(2,1)S(1)}) custom-call(s32[2,128,128]{2,1,0:T(8,128)S(1)} %get-tuple-element.15.plan, bf16[32,16,128]{2,1,0:T(8,128)(2,1)S(1)} %all_to_all.21.back, f32[8,16,128]{2,1,0:T(8,128)S(1)} %get-tuple-element.18.after.own, ...), custom_call_target="tpu_custom_call" | custom-call | flops 10000000000 | bytes 8800000 | tf_op jit(solution)/shard_map/merge/pallas_call | solution.py:361
  33.3 0.0 copy-start.2
  33.4 2.0 %collective-permute-start.3 = (bf16[8,4096]{1,0:T(8,128)(2,1)S(1)}, bf16[8,4096]{1,0:T(8,128)(2,1)S(1)}, u32[]{:S(2)}, u32[]{:S(2)}) collective-permute-start(bf16[8,4096]{1,0:T(8,128)(2,1)S(1)} %get-tuple-element.25), channel_id=1, source_target_pairs={{0,1},{1,0},{2,3},{3,2},{4,5},{5,4},{6,7},{7,6},{8,9},{9,8},{10,11... | collective-permute-start | bytes 196616 | tf_op jit(solution)/shard_map/ppermute | solution.py:380
  35.4 2.5 %collective-permute-start.2 = (bf16[8,4096]{1,0:T(8,128)(2,1)S(1)}, bf16[8,4096]{1,0:T(8,128)(2,1)S(1)}, u32[]{:S(2)}, u32[]{:S(2)}) collective-permute-start(bf16[8,4096]{1,0:T(8,128)(2,1)S(1)} %get-tuple-element.25), channel_id=1, source_target_pairs={{0,3},{1,2},{2,1},{3,0},{4,7},{5,6},{6,5},{7,4},{8,11},{9,10},{10,... | collective-permute-start | bytes 196616 | tf_op jit(solution)/shard_map/ppermute | solution.py:380
  37.9 1.1 %collective-permute-start.1 = (bf16[8,4096]{1,0:T(8,128)(2,1)S(1)}, bf16[8,4096]{1,0:T(8,128)(2,1)S(1)}, u32[]{:S(2)}, u32[]{:S(2)}) collective-permute-start(bf16[8,4096]{1,0:T(8,128)(2,1)S(1)} %get-tuple-element.25), channel_id=1, source_target_pairs={{0,2},{1,3},{2,0},{3,1},{4,6},{5,7},{6,4},{7,5},{8,10},{9,11},{10,... | collective-permute-start | bytes 196616 | tf_op jit(solution)/shard_map/ppermute | solution.py:380
  38.9 0.0 collective-permute-done.3.third
  38.9 1.9 %collective-permute-done.2.second = bf16[8,4096]{1,0:T(8,128)(2,1)S(1)} collective-permute-done((bf16[8,4096]{1,0:T(8,128)(2,1)S(1)}, bf16[8,4096]{1,0:T(8,128)(2,1)S(1)}, u32[]{:S(2)}, u32[]{:S(2)}) %collective-permute-start.2) | collective-permute-done | bytes 65568 | tf_op jit(solution)/shard_map/ppermute | solution.py:380
  40.8 2.8 %collective-permute-done.1.first = bf16[8,4096]{1,0:T(8,128)(2,1)S(1)} collective-permute-done((bf16[8,4096]{1,0:T(8,128)(2,1)S(1)}, bf16[8,4096]{1,0:T(8,128)(2,1)S(1)}, u32[]{:S(2)}, u32[]{:S(2)}) %collective-permute-start.1) | collective-permute-done | bytes 65568 | tf_op jit(solution)/shard_map/ppermute | solution.py:380
  43.6 0.0 copy-done.6
  43.6 0.3 norm.1
  43.9 18.9 %all_to_all.22 = bf16[16,8,4096]{2,1,0:T(8,128)(2,1)S(1)} all-to-all(bf16[16,8,4096]{2,1,0:T(8,128)(2,1)S(1)} %get-tuple-element.26), channel_id=1, replica_groups=mesh['group'=16,'depth'=2,'mp'=4] {'group'}, dimensions={0} | all-to-all | bytes 2097152 | tf_op jit(solution)/shard_map/all_to_all | solution.py:393
  62.8 0.0 copy-done.3
  62.8 0.0 copy-done.4
  62.8 0.0 copy-done.2
  62.8 1.7 %feed.1 = bf16[64,8,1024]{2,1,0:T(8,128)(2,1)S(1)} custom-call(bf16[128,4096]{1,0:T(8,128)(2,1)S(1)} %bitcast.5, bf16[224,4096]{1,0:T(8,128)(2,1)S(1)} %bitcast.6, bf16[224,4096]{1,0:T(8,128)(2,1)S(1)} %bitcast.7, bf16[224,4096]{1,0:T(8,128)(2,1)S(1)} %copy-done.4), custom_call_target="tpu_custom_call" | custom-call | flops 1400000000 | bytes 7000000 | tf_op jit(solution)/shard_map/feed/pallas_call | solution.py:395
  64.6 20.9 %all_to_all.23.arrived = bf16[64,8,1024]{2,1,0:T(8,128)(2,1)S(1)} all-to-all(bf16[64,8,1024]{2,1,0:T(8,128)(2,1)S(1)} %feed.1), channel_id=1, replica_groups=mesh['group'=16,'depth'=2,'mp'=4] {'group','mp'}, dimensions={0} | all-to-all | bytes 2097152 | tf_op jit(solution)/shard_map/all_to_all | solution.py:404
  85.5 0.8 last.1
  (1 shorter events, 0.0 us)
Async XLA Ops:
  0.6 16.4 %copy-start.5 = (bf16[16,8,128]{2,1,0:T(8,128)(2,1)S(1)}, bf16[16,8,128]{2,1,0:T(8,128)(2,1)}, u32[]{:S(2)}) copy-start(bf16[16,8,128]{2,1,0:T(8,128)(2,1)} %queries) | copy-start | bytes 98308
  0.6 16.4 %copy-start.1 = (bf16[16,2,256,128]{3,2,1,0:T(8,128)(2,1)S(1)}, bf16[16,2,256,128]{3,2,1,0:T(8,128)(2,1)}, u32[]{:S(2)}) copy-start(bf16[16,2,256,128]{3,2,1,0:T(8,128)(2,1)} %values.2) | copy-start | bytes 6291460
  0.7 16.4 %copy-start = (bf16[16,2,256,128]{3,2,1,0:T(8,128)(2,1)S(1)}, bf16[16,2,256,128]{3,2,1,0:T(8,128)(2,1)}, u32[]{:S(2)}) copy-start(bf16[16,2,256,128]{3,2,1,0:T(8,128)(2,1)} %keys.2) | copy-start | bytes 6291460
  0.7 16.4 %copy-start.8 = (bf16[16,2,128]{2,1,0:T(2,128)(2,1)S(1)}, bf16[16,2,128]{2,1,0:T(2,128)(2,1)}, u32[]{:S(2)}) copy-start(bf16[16,2,128]{2,1,0:T(2,128)(2,1)} %new_values.1) | copy-start | bytes 24580
  0.7 16.4 %copy-start.7 = (bf16[16,2,128]{2,1,0:T(2,128)(2,1)S(1)}, bf16[16,2,128]{2,1,0:T(2,128)(2,1)}, u32[]{:S(2)}) copy-start(bf16[16,2,128]{2,1,0:T(2,128)(2,1)} %new_keys.1) | copy-start | bytes 24580
  0.7 18.1 %copy-start.9 = (bf16[8,2,576,128]{3,2,1,0:T(8,128)(2,1)S(1)}, bf16[8,2,576,128]{3,2,1,0:T(8,128)(2,1)}, u32[]{:S(2)}) copy-start(bf16[8,2,576,128]{3,2,1,0:T(8,128)(2,1)} %keys.3) | copy-start | bytes 7077892
  0.7 18.1 %copy-start.10 = (bf16[8,2,576,128]{3,2,1,0:T(8,128)(2,1)S(1)}, bf16[8,2,576,128]{3,2,1,0:T(8,128)(2,1)}, u32[]{:S(2)}) copy-start(bf16[8,2,576,128]{3,2,1,0:T(8,128)(2,1)} %values.3) | copy-start | bytes 7077892
  17.1 14.5 %slice-start = ((s8[8388608]{0:T(1024)(128)(4,1)}), s8[4194304]{0:T(1024)(128)(4,1)S(1)}, s32[]{:S(2)}) async-start(s8[8388608]{0:T(1024)(128)(4,1)} %bitcast.10), calls=%async_computation.4 | async-start | bytes 8388608
  18.7 1.6 %collective-permute-start = (f32[8,16,128]{2,1,0:T(8,128)S(1)}, f32[8,16,128]{2,1,0:T(8,128)S(1)}, u32[]{:S(2)}, u32[]{:S(2)}) collective-permute-start(f32[8,16,128]{2,1,0:T(8,128)S(1)} %get-tuple-element.20), channel_id=1, source_target_pairs={{0,4},{4,0},{1,5},{5,1},{2,6},{6,2},{3,7},{7,3},{8,12},{12,8},{9,1... | collective-permute-start | bytes 196616 | tf_op jit(solution)/shard_map/ppermute | solution.py:347
  18.8 12.8 %slice-start.1 = ((s8[8388608]{0:T(1024)(128)(4,1)}), s8[4194304]{0:T(1024)(128)(4,1)S(1)}, s32[]{:S(2)}) async-start(s8[8388608]{0:T(1024)(128)(4,1)} %bitcast.10), calls=%async_computation.5 | async-start | bytes 8388608
  18.8 12.8 %copy-start.11 = (bf16[2,4096]{1,0:T(2,128)(2,1)S(1)}, bf16[2,4096]{1,0:T(2,128)(2,1)}, u32[]{:S(2)}) copy-start(bf16[2,4096]{1,0:T(2,128)(2,1)} %states.1) | copy-start | bytes 49156
  31.6 12.0 %copy-start.6 = (f32[4096]{0:T(1024)S(1)}, f32[4096]{0:T(1024)}, u32[]{:S(2)}) copy-start(f32[4096]{0:T(1024)} %param.34) | copy-start | bytes 49156
  31.7 31.2 %copy-start.3 = (bf16[4096,224]{0,1:T(8,128)(2,1)S(1)}, bf16[4096,224]{0,1:T(8,128)(2,1)}, u32[]{:S(2)}) copy-start(bf16[4096,224]{0,1:T(8,128)(2,1)} %param.36) | copy-start | bytes 5505028
  31.7 31.2 %copy-start.4 = (bf16[224,4096]{1,0:T(8,128)(2,1)S(1)}, bf16[224,4096]{1,0:T(8,128)(2,1)}, u32[]{:S(2)}) copy-start(bf16[224,4096]{1,0:T(8,128)(2,1)} %down.1) | copy-start | bytes 5505028
  33.3 29.5 %copy-start.2 = (bf16[4096,224]{0,1:T(8,128)(2,1)S(1)}, bf16[4096,224]{0,1:T(8,128)(2,1)}, u32[]{:S(2)}) copy-start(bf16[4096,224]{0,1:T(8,128)(2,1)} %param.35) | copy-start | bytes 5505028
  33.4 5.6 %collective-permute-start.3 = (bf16[8,4096]{1,0:T(8,128)(2,1)S(1)}, bf16[8,4096]{1,0:T(8,128)(2,1)S(1)}, u32[]{:S(2)}, u32[]{:S(2)}) collective-permute-start(bf16[8,4096]{1,0:T(8,128)(2,1)S(1)} %get-tuple-element.25), channel_id=1, source_target_pairs={{0,1},{1,0},{2,3},{3,2},{4,5},{5,4},{6,7},{7,6},{8,9},{9,8},{10,11... | collective-permute-start | bytes 196616 | tf_op jit(solution)/shard_map/ppermute | solution.py:380
  35.4 5.5 %collective-permute-start.2 = (bf16[8,4096]{1,0:T(8,128)(2,1)S(1)}, bf16[8,4096]{1,0:T(8,128)(2,1)S(1)}, u32[]{:S(2)}, u32[]{:S(2)}) collective-permute-start(bf16[8,4096]{1,0:T(8,128)(2,1)S(1)} %get-tuple-element.25), channel_id=1, source_target_pairs={{0,3},{1,2},{2,1},{3,0},{4,7},{5,6},{6,5},{7,4},{8,11},{9,10},{10,... | collective-permute-start | bytes 196616 | tf_op jit(solution)/shard_map/ppermute | solution.py:380
  37.9 5.8 %collective-permute-start.1 = (bf16[8,4096]{1,0:T(8,128)(2,1)S(1)}, bf16[8,4096]{1,0:T(8,128)(2,1)S(1)}, u32[]{:S(2)}, u32[]{:S(2)}) collective-permute-start(bf16[8,4096]{1,0:T(8,128)(2,1)S(1)} %get-tuple-element.25), channel_id=1, source_target_pairs={{0,2},{1,3},{2,0},{3,1},{4,6},{5,7},{6,4},{7,5},{8,10},{9,11},{10,... | collective-permute-start | bytes 196616 | tf_op jit(solution)/shard_map/ppermute | solution.py:380
